TPU v7x, 32 devices: a whole 2x2x4 slice. The times are simulated.
32 devices in a mesh: docs: 8 (over y, x, core), heads: 4 (over z).
Axes of the slice: x: 2, y: 2, z: 4, core: 2. Of those that a mesh axis runs over, the one named last changes fastest.
Arguments:
- layer_input: bfloat16 [16384, 768], P(('docs', 'heads')), may hold values from -6 to 6
- token_boxes: int32 [2, 16384], P(None, 'docs'), may hold values from 0 to 999, as said below
- lengths: int32 [32], P('docs'), may hold values from 32 to 512, as said below
- w_qkv: bfloat16 [768, 3, 768], P(None, None, 'heads'), may hold values from -0.21875 to 0.21875
- qv_bias: bfloat16 [2, 768], P(None, 'heads'), may hold values from -3 to 3
- rel_tables: bfloat16 [2, 12, 32], P(None, 'heads'), may hold values from -4 to 4
- w_out: bfloat16 [768, 768], replicated, may hold values from -0.875 to 0.875
- out_bias: float32 [768], replicated, may hold values from -1 to 1
- gain_one: float32 [768], replicated, may hold values from 0.5 to 1.5
- shift_one: float32 [768], replicated, may hold values from -1 to 1
- w_in: bfloat16 [768, 3072], replicated, may hold values from -0.21875 to 0.21875
- in_bias: float32 [3072], replicated, may hold values from -1 to 1
- w_back: bfloat16 [3072, 768], replicated, may hold values from -0.109375 to 0.109375
- back_bias: float32 [768], replicated, may hold values from -1 to 1
- gain_two: float32 [768], replicated, may hold values from 0.5 to 1.5
- shift_two: float32 [768], replicated, may hold values from -1 to 1
- cotangent: bfloat16 [16384, 768], P(('docs', 'heads')), may hold values from -6 to 6
Outputs:
- layer_output: bfloat16 [16384, 768], P(('docs', 'heads'))
- grad_input: bfloat16 [16384, 768], P(('docs', 'heads'))
- grad_qkv: float32 [768, 3, 768], P(None, None, 'heads')
- grad_qv_bias: float32 [2, 768], P(None, 'heads')
- grad_tables: float32 [2, 12, 32], P(None, 'heads')
- grad_out: float32 [768, 768], P('docs')
- grad_out_bias: float32 [768], P('docs')
- grad_gain_one: float32 [768], P('docs')
- grad_shift_one: float32 [768], P('docs')
- grad_in: float32 [768, 3072], P('docs')
- grad_in_bias: float32 [3072], P('docs')
- grad_back: float32 [3072, 768], P('docs')
- grad_back_bias: float32 [768], P('docs')
- grad_gain_two: float32 [768], P('docs')
- grad_shift_two: float32 [768], P('docs')
Inputs may be any that keep to these rules, and one draw needn't show every extreme that they name: `lengths`: filled tokens of each window; slots after them are padding. Some window is full in every draw. `token_boxes`: box coordinates of each token, row 0 left and row 1 top, on a page of 1000 by 1000.
All inputs are finite; a program needn't handle non-finite values.
Results may differ from a plain program's by a relative error of at most 0.017.
The roundings to bfloat16 on the way count: a program that leaves them out, or rounds other values in their place, can miss the bound.
Values may be sent and summed in bfloat16 or wider, within the bound.
No kernel may reach another device: no remote copies, remote signals or barrier semaphores. Data moves between devices by JAX's collectives and lax.ppermute only.
A program may use at most 192 MiB of HBM per device.

v0:
```python
import functools
import math

import jax
import jax.numpy as jnp
from jax import lax
from jax.experimental import pallas as pl
from jax.experimental.pallas import tpu as pltpu
from jax.sharding import PartitionSpec as P

HEAD_DIM = 64
L = 512
EPS = 1e-05
NEG = -1000000000.0
THRESHOLDS = (1, 2, 3, 4, 6, 8, 12, 16, 24, 32, 48, 64, 96, 128, 192)
ROOT_HALF = 1.0 / math.sqrt(2.0)
DENSITY_SCALE = 1.0 / math.sqrt(2.0 * math.pi)
SCALE = 0.125
KC = 32
QB = 128
RT = 32
FC = 768
MB = 256
BF = jnp.bfloat16
F32 = jnp.float32
I32 = jnp.int32
NT = (((1,), (1,)), ((), ()))


def whole(*shape):
    return pl.BlockSpec(shape, lambda *_: (0,) * len(shape))


def limit(mebibytes):
    return pltpu.CompilerParams(vmem_limit_bytes=mebibytes << 20)


HINT = pl.CostEstimate(flops=1, bytes_accessed=1, transcendentals=0)


def shaped(dtype, *shape):
    return jax.ShapeDtypeStruct(shape, dtype)


def first_bucket_of(offset):
    distance = jnp.abs(offset)
    count = jnp.where(offset > 0, 16, 0).astype(I32)
    for threshold in THRESHOLDS:
        count = count + jnp.where(distance >= threshold, 1, 0).astype(I32)
    return count


def second_bucket_of(across, upward):
    horizontal = jnp.zeros(across.shape, I32)
    for threshold in (-128, -32, -8, 0):
        horizontal = horizontal + jnp.where(across >= threshold, 1, 0)
    for threshold in (8, 32, 128):
        horizontal = horizontal + jnp.where(across > threshold, 1, 0)
    vertical = (
        jnp.where(upward >= -24, 8, 0)
        + jnp.where(upward >= 0, 8, 0)
        + jnp.where(upward > 24, 8, 0)
    )
    return vertical + horizontal


PLACE = ("heads", "core", "x", "y")


def bucket_kernel(place_ref, len_ref, box_ref, out_ref, near_ref, turned_sc):
    filled = len_ref[place_ref[0]]
    boxes = box_ref[...].astype(F32)
    turned_sc[...] = jnp.transpose(jnp.concatenate([boxes] * 4, axis=0)).astype(I32)
    size = 64

    @pl.loop(0, L // size)
    def _(step):
        start = pl.multiple_of(step * size, size)
        rows = pl.ds(start, size)
        across = turned_sc[rows, 0:1] - box_ref[0:1, :]
        upward = turned_sc[rows, 1:2] - box_ref[1:2, :]
        key = lax.broadcasted_iota(I32, (size, L), 0) + start
        out_ref[rows, :] = jnp.where(key < filled, second_bucket_of(across, upward), 32)

    @pl.loop(0, near_ref.shape[0])
    def _(tile):
        offset = (
            128 * (tile - 2)
            + lax.broadcasted_iota(I32, (128, 128), 0)
            - lax.broadcasted_iota(I32, (128, 128), 1)
        )
        near_ref[tile] = first_bucket_of(offset)


def buckets_of(place, lengths, boxes):
    return pl.pallas_call(
        bucket_kernel,
        grid_spec=pltpu.PrefetchScalarGridSpec(
            num_scalar_prefetch=2,
            grid=(1,),
            in_specs=[pl.BlockSpec((2, L), lambda i, place, lengths: (0, place[0]))],
            out_specs=[whole(L, L), whole(5, 128, 128)],
            scratch_shapes=[pltpu.VMEM((L, 8), I32)],
        ),
        out_shape=[shaped(I32, L, L), shaped(I32, 5, 128, 128)],
        name="buckets",
        compiler_params=limit(6),
        cost_estimate=HINT,
    )(place, lengths, boxes)


def lookup(table_row, index):
    table = jnp.broadcast_to(table_row, (index.shape[0], 128))
    return jnp.concatenate(
        [
            jnp.take_along_axis(
                table, index[:, c : c + 128], axis=1, mode="promise_in_bounds"
            )
            for c in range(0, index.shape[1], 128)
        ],
        axis=1,
    )


def head_window(head, width):
    start = head * HEAD_DIM // 128 * 128
    return start, min(128, width - start), head * HEAD_DIM - start


def eights(rows):
    return rows.reshape(rows.shape[0] // 8, 8, rows.shape[1])


def column(row):
    return jnp.transpose(jnp.broadcast_to(row, (8, row.shape[1])))[:, 0:1]


def forward_kernel(gathered, place_ref, x_ref, *refs):
    sources = refs[: 4 if gathered else 1]
    extra_ref, bucket_ref, index_ref = refs[len(sources) : len(sources) + 3]
    rest = refs[len(sources) + 3 :]
    if gathered:
        w_ref, rest = rest[0], rest[1:]
    else:
        w_ref = sources[0]
    ctx_ref, turned_ref, raised_ref, qkv_ref, inverse_ref = rest[:5]
    near_sc, score_sc, query_sc, key_sc = rest[5:9]
    heads = raised_ref.shape[1]
    width = heads * HEAD_DIM

    @pl.when(pl.program_id(0) == 0)
    def _():
        query_sc[...] = jnp.zeros_like(query_sc)

    if gathered:
        whole_sc = rest[9]
        core, here_x, here_y = place_ref[1], place_ref[2], place_ref[3]
        cut = sources[0].shape[3]
        size = cut + sources[1].shape[3]
        for far_y in range(2):
            for far_x in range(2):
                chip = (here_y ^ far_y) * 2 + (here_x ^ far_x)
                for side, pair in ((core, sources[:2]), (1 - core, sources[2:])):
                    at = (chip * 2 + side) * size
                    first = pl.multiple_of(at, 8)
                    whole_sc[pl.ds(first, cut), :] = pair[0][far_y, far_x, 0].astype(F32)
                    second = pl.multiple_of(at + cut, 8)
                    whole_sc[pl.ds(second, size - cut), :] = pair[1][far_x, far_y, 0].astype(F32)
        w_ref[0] = whole_sc[...].astype(BF)

    extra = extra_ref[0, 0:1, :].astype(F32)
    query_bias, value_bias = extra[:, 0:width], extra[:, width : 2 * width]
    first_tables = extra[:, 2 * width : 2 * width + 128]
    second_tables = extra[:, 2 * width + 128 : 2 * width + 256]
    query = lax.dot_general(w_ref[0, 0:width, :], x_ref[...], NT, preferred_element_type=F32)
    qkv_ref[0, 0:width, :] = (query + column(query_bias)).astype(BF)
    key = lax.dot_general(
        w_ref[0, width : 2 * width, :], x_ref[...], NT, preferred_element_type=F32
    )
    qkv_ref[0, width : 2 * width, :] = key.astype(BF)
    value = lax.dot_general(
        w_ref[0, 2 * width : 3 * width, :], x_ref[...], NT, preferred_element_type=F32
    )
    qkv_ref[0, 2 * width : 3 * width, :] = (value + column(value_bias)).astype(BF)
    key_sc[...] = lax.dot_general(
        x_ref[...], w_ref[0, width : 2 * width, :], NT, preferred_element_type=F32
    ).astype(BF)
    inverse_ref[0] = jnp.zeros_like(inverse_ref[0])
    lane = lax.broadcasted_iota(I32, (1, 128), 1)
    for h in range(heads):
        c0, w, low = head_window(h, width)
        own = slice(h * HEAD_DIM, (h + 1) * HEAD_DIM)
        query_sc[h, low : low + HEAD_DIM, :] = qkv_ref[0, own, :] * jnp.asarray(SCALE, BF)
        row = first_tables if h == 0 else jnp.roll(first_tables, -32 * h, axis=1)
        other = second_tables if h == 0 else jnp.roll(second_tables, -32 * h, axis=1)
        other = jnp.where(lane < 32, other, NEG)
        for d in range(5):
            near_sc[h, d] = lookup(row, index_ref[d])
        far = {
            -3: jnp.broadcast_to(row[:, 15:16], (KC, 128)),
            3: jnp.broadcast_to(row[:, 31:32], (KC, 128)),
        }
        key = key_sc[:, c0 : c0 + w]
        for block in range(L // QB):
            cols = slice(block * QB, (block + 1) * QB)
            score_sc[h] = jnp.dot(key, query_sc[h, 0:w, cols], preferred_element_type=F32)
            peak = None
            for step in range(L // KC):
                rows = slice(step * KC, (step + 1) * KC)
                d, inner = step * KC // 128 - block, step * KC % 128
                near = far[d] if abs(d) == 3 else near_sc[h, d + 2, inner : inner + KC, :]
                scores = score_sc[h, rows, :] + near
                scores = scores + lookup(other, bucket_ref[rows, cols])
                score_sc[h, rows, :] = scores
                part = jnp.max(eights(scores), axis=0)
                peak = part if peak is None else jnp.maximum(peak, part)
            peak = jnp.max(peak, axis=0, keepdims=True)
            sums = None
            for step in range(L // KC):
                rows = slice(step * KC, (step + 1) * KC)
                raised = jnp.exp(score_sc[h, rows, :] - peak)
                raised_ref[0, h, rows, cols] = raised.astype(BF)
                part = jnp.sum(eights(raised), axis=0)
                sums = part if sums is None else sums + part
            inverse_ref[0, h : h + 1, cols] = 1.0 / jnp.sum(sums, axis=0, keepdims=True)
        at = 2 * width + h * HEAD_DIM
        out = jnp.dot(
            qkv_ref[0, at : at + HEAD_DIM, :], raised_ref[0, h], preferred_element_type=F32
        )
        turned_ref[0, own, :] = (out * inverse_ref[0, h : h + 1, :]).astype(BF)
    ctx_ref[0] = jnp.transpose(turned_ref[0])


def each(*shape):
    return pl.BlockSpec((1,) + shape, lambda g, *_: (g,) + (0,) * len(shape))


def attend_forward(place, x, sources, extra, bucket, near):
    gathered = len(sources) == 4
    groups, depth = extra.shape[0], x.shape[1]
    if gathered:
        columns = 8 * (sources[0].shape[3] + sources[1].shape[3])
        inputs = [
            pl.BlockSpec(
                (2, 2, 1) + source.shape[3:], lambda g, place: (0, 0, g, 0, 0)
            )
            for source in sources
        ]
    else:
        columns = sources[0].shape[1]
        inputs = [each(columns, depth)]
    heads = columns // (3 * HEAD_DIM)
    width = columns // 3
    out_specs = [
        each(L, width), each(width, L), each(heads, L, L), each(columns, L), each(8, L)
    ]
    out_shape = [
        shaped(BF, groups, L, width),
        shaped(BF, groups, width, L),
        shaped(BF, groups, heads, L, L),
        shaped(BF, groups, columns, L),
        shaped(F32, groups, 8, L),
    ]
    scratch = [
        pltpu.VMEM((heads, 5, 128, 128), F32),
        pltpu.VMEM((heads, L, QB), F32),
        pltpu.VMEM((heads, 128, L), BF),
        pltpu.VMEM((L, width), BF),
    ]
    if gathered:
        out_specs = [each(columns, depth)] + out_specs
        out_shape = [shaped(BF, groups, columns, depth)] + out_shape
        scratch = scratch + [pltpu.VMEM((columns, depth), F32)]
    return pl.pallas_call(
        functools.partial(forward_kernel, gathered),
        grid_spec=pltpu.PrefetchScalarGridSpec(
            num_scalar_prefetch=1,
            grid=(groups,),
            in_specs=[whole(L, depth)] + inputs + [each(8, depth), whole(L, L), whole(5, 128, 128)],
            out_specs=out_specs,
            scratch_shapes=scratch,
        ),
        out_shape=out_shape,
        name="attend_forward",
        compiler_params=limit(22),
        cost_estimate=HINT,
    )(place, x, *sources, extra, bucket, near)


def backward_kernel(
    halved, place_ref, x_ref, w_ref, qkv_ref, raised_ref, inverse_ref, grad_ref, start_ref, *refs
):
    outs = refs[: 5 if halved else 4]
    dx_ref, ds_ref, sums_ref = outs[:3]
    pad_sc, term_sc, rows_sc, turn_sc, value_sc = refs[len(outs) : len(outs) + 5]
    group = pl.program_id(0)
    heads = raised_ref.shape[1]
    width = heads * HEAD_DIM

    @pl.when(group == 0)
    def _():
        pad_sc[...] = jnp.zeros_like(pad_sc)
        dx_ref[...] = start_ref[...]

    value_sc[...] = jnp.transpose(qkv_ref[0, 2 * width : 3 * width, :])
    for h in range(heads):
        c0, w, low = head_window(h, width)
        own = slice(h * HEAD_DIM, (h + 1) * HEAD_DIM)
        pad_sc[h, low : low + HEAD_DIM, :] = grad_ref[0, own, :]
        value = value_sc[:, c0 : c0 + w]
        for block in range(L // QB):
            cols = slice(block * QB, (block + 1) * QB)
            term_sc[h] = jnp.dot(value, pad_sc[h, 0:w, cols], preferred_element_type=F32)
            sums = None
            for step in range(L // KC):
                rows = slice(step * KC, (step + 1) * KC)
                terms = term_sc[h, rows, :] * raised_ref[0, h, rows, cols].astype(F32)
                term_sc[h, rows, :] = terms
                part = jnp.sum(eights(terms), axis=0)
                sums = part if sums is None else sums + part
            inner = jnp.sum(sums, axis=0, keepdims=True) * inverse_ref[0, h : h + 1, cols]
            for step in range(L // KC):
                rows = slice(step * KC, (step + 1) * KC)
                raised = raised_ref[0, h, rows, cols].astype(F32)
                ds_ref[0, h, rows, cols] = (term_sc[h, rows, :] - raised * inner).astype(BF)
        scale = jnp.asarray(SCALE, BF)
        at = width + h * HEAD_DIM
        turn_sc[own, :] = jnp.dot(
            qkv_ref[0, at : at + HEAD_DIM, :] * scale, ds_ref[0, h], preferred_element_type=F32
        ).astype(BF)
        dk = lax.dot_general(
            ds_ref[0, h], qkv_ref[0, c0 : c0 + w, :] * scale, NT, preferred_element_type=F32
        )
        rows_sc[:, at : at + HEAD_DIM] = dk[:, low : low + HEAD_DIM].astype(BF)
        dv = lax.dot_general(
            raised_ref[0, h], grad_ref[0, c0 : c0 + w, :], NT, preferred_element_type=F32
        )
        at = 2 * width + h * HEAD_DIM
        rows_sc[:, at : at + HEAD_DIM] = dv[:, low : low + HEAD_DIM].astype(BF)
    rows_sc[:, 0:width] = jnp.transpose(turn_sc[0:width, :])
    turn_sc[width:, :] = jnp.transpose(rows_sc[:, width:])
    weights = jnp.dot(turn_sc[...], x_ref[...], preferred_element_type=F32)
    if halved:
        sent_ref, kept_ref = outs[3:]
        all_sc = refs[len(outs) + 5]
        all_sc[...] = weights
        core = place_ref[1]
        chips, size = kept_ref.shape[1], kept_ref.shape[2]
        for chip in range(chips):
            for side, ref in ((1 - core, sent_ref), (core, kept_ref)):
                at = pl.multiple_of((chip * 2 + side) * size, 8)
                ref[0, chip] = all_sc[pl.ds(at, size), :].astype(BF)
    else:
        outs[3][0] = weights.astype(BF)
    dx_ref[...] += jnp.dot(rows_sc[...], w_ref[0], preferred_element_type=F32)
    sums_ref[0] = jnp.sum(rows_sc[...].astype(F32), axis=0, keepdims=True)


def attend_backward(place, halves, x, w, qkv, raised, inverse, grad, start, span=None):
    columns, depth = w.shape[1:]
    skip, stop = span or (0, w.shape[0])
    groups = stop - skip
    some = lambda *shape: pl.BlockSpec(
        (1,) + shape, lambda g, *_: (g + skip,) + (0,) * len(shape)
    )
    heads = columns // (3 * HEAD_DIM)
    width = columns // 3
    out_specs = [whole(L, depth), each(heads, L, L), each(1, columns)]
    out_shape = [
        shaped(F32, L, depth),
        shaped(BF, groups, heads, L, L),
        shaped(F32, groups, 1, columns),
    ]
    scratch = [
        pltpu.VMEM((heads, 128, L), BF),
        pltpu.VMEM((heads, L, QB), F32),
        pltpu.VMEM((L, columns), BF),
        pltpu.VMEM((columns, L), BF),
        pltpu.VMEM((L, width), BF),
    ]
    if halves:
        size = columns // (2 * halves)
        out_specs += [each(halves, size, depth)] * 2
        out_shape += [shaped(BF, groups, halves, size, depth)] * 2
        scratch += [pltpu.VMEM((columns, depth), F32)]
    else:
        out_specs += [each(columns, depth)]
        out_shape += [shaped(BF, groups, columns, depth)]
    return pl.pallas_call(
        functools.partial(backward_kernel, bool(halves)),
        grid_spec=pltpu.PrefetchScalarGridSpec(
            num_scalar_prefetch=1,
            grid=(groups,),
            in_specs=[
                whole(L, depth),
                some(columns, depth),
                some(columns, L),
                some(heads, L, L),
                some(8, L),
                some(width, L),
                whole(L, depth),
            ],
            out_specs=out_specs,
            scratch_shapes=scratch,
        ),
        out_shape=out_shape,
        name="attend_backward",
        compiler_params=limit(26),
        cost_estimate=HINT,
    )(place, x, w, qkv, raised, inverse, grad, start)


def table_kernel(skip, *refs):
    bucket_ref, start_ref, acc_ref, hot_sc = refs[-4:]
    step = pl.program_id(0)
    blocks = [
        (ref, g, h) for ref in refs[:-4] for g in range(ref.shape[0]) for h in range(ref.shape[1])
    ]
    half = 32 * 8

    @pl.when(step == 0)
    def _():
        acc_ref[...] = start_ref[...]

    for u in range(RT // 8):
        part = slice(u * 8, (u + 1) * 8)
        second = bucket_ref[part, :]
        offset = (
            lax.broadcasted_iota(I32, (8, L), 0)
            + ((step + skip) * RT + u * 8)
            - lax.broadcasted_iota(I32, (8, L), 1)
        )
        first = first_bucket_of(offset)
        for t in range(0, 32, 2):
            for base, bucket in ((0, first), (half, second)):
                hot_sc[base + t * 8 : base + (t + 2) * 8, :] = jnp.concatenate(
                    [jnp.where(bucket == t, 1.0, 0.0), jnp.where(bucket == t + 1, 1.0, 0.0)],
                    axis=0,
                ).astype(BF)
        left = jnp.concatenate([ref[g, h, part, :] for ref, g, h in blocks], axis=0)
        acc_ref[...] += lax.dot_general(left, hot_sc[...], NT, preferred_element_type=F32)


def table_products(ds, bucket, start, part):
    heads = sum(item.shape[0] * item.shape[1] for item in ds)
    steps = L // RT // 2
    skip = part * steps
    return pl.pallas_call(
        functools.partial(table_kernel, skip),
        grid=(steps,),
        in_specs=[
            pl.BlockSpec(item.shape[:2] + (RT, L), lambda r: (0, 0, r + skip, 0)) for item in ds
        ]
        + [pl.BlockSpec((RT, L), lambda r: (r + skip, 0)), whole(heads * 8, 512)],
        out_specs=whole(heads * 8, 512),
        out_shape=shaped(F32, heads * 8, 512),
        scratch_shapes=[pltpu.VMEM((512, L), BF)],
        name="table_products",
        compiler_params=limit(14),
        cost_estimate=HINT,
    )(*ds, bucket, start)


def short_kernel(per, count, *refs):
    acc_ref, sums = refs[0], refs[1 : 1 + count]
    down_ref, up_ref, in_ref, out_ref = refs[1 + count :]
    heads = acc_ref.shape[0] // 8
    half = 32 * 8
    shape = (heads * 8, 2 * half)
    same = lax.broadcasted_iota(I32, shape, 0) % 8 == lax.broadcasted_iota(I32, shape, 1) % 8
    kept = jnp.where(same, acc_ref[...], 0.0)
    fold = (2 * half, 64)
    right = (
        lax.broadcasted_iota(I32, fold, 0) // 8 == lax.broadcasted_iota(I32, fold, 1)
    ).astype(F32)
    spread = (16, heads * 8)
    left = (
        lax.broadcasted_iota(I32, spread, 1) // 8 == lax.broadcasted_iota(I32, spread, 0)
    ).astype(F32)
    exact = lax.Precision.HIGHEST
    folded = jnp.dot(kept, right, preferred_element_type=F32, precision=exact)
    tables = jnp.dot(left, folded, preferred_element_type=F32, precision=exact)
    wide = 2 * per * 32
    lanes = None
    for h in range(per):
        shape = (8, 16)
        rows = (
            lax.broadcasted_iota(I32, shape, 1) == lax.broadcasted_iota(I32, shape, 0) * per + h
        ).astype(F32)
        shape = (64, wide)
        source, target = lax.broadcasted_iota(I32, shape, 0), lax.broadcasted_iota(I32, shape, 1)
        moved = jnp.where(source < 32, source + h * 32, source + (per - 1 + h) * 32)
        part = jnp.dot(rows, tables, preferred_element_type=F32, precision=exact)
        part = jnp.dot(
            part, (target == moved).astype(F32), preferred_element_type=F32, precision=exact
        )
        lanes = part if lanes is None else lanes + part
    out_ref[...] = jnp.zeros_like(out_ref)
    out_ref[0:3, :] = down_ref[0:3, :]
    out_ref[3:6, :] = up_ref[0:3, :]
    width = out_ref.shape[1]
    deep = in_ref.shape[1] // width
    for n in range(deep):
        out_ref[6 + n : 7 + n, :] = in_ref[0:1, n * width : (n + 1) * width]
    group = 0
    for ref in sums:
        own = ref.shape[2] // 3
        for g in range(ref.shape[0]):
            row = slice(6 + deep + group, 7 + deep + group)
            out_ref[row, 0:own] = ref[g, :, 0:own]
            out_ref[row, own : 2 * own] = ref[g, :, 2 * own :]
            out_ref[row, 2 * own : 2 * own + wide] = lanes[group : group + 1, :]
            group += 1


def short_rows(acc, sums, down, up, inner, per):
    width = down.shape[1]
    rows = -(-(6 + inner.shape[1] // width + acc.shape[0] // 8 // per) // 8) * 8
    vmem = pl.BlockSpec(memory_space=pltpu.VMEM)
    return pl.pallas_call(
        functools.partial(short_kernel, per, len(sums)),
        in_specs=[vmem] * (4 + len(sums)),
        out_specs=vmem,
        out_shape=shaped(F32, rows, width),
        name="short_rows",
        compiler_params=limit(6),
        cost_estimate=HINT,
    )(acc, *sums, down, up, inner)


def mean_of(rows):
    return jnp.mean(rows, axis=-1, keepdims=True)


def normalize(rows):
    centred = rows - mean_of(rows)
    inverse = lax.rsqrt(mean_of(centred * centred) + EPS)
    return centred * inverse, inverse


def normalize_back(scaled, unit, inverse):
    return inverse * (scaled - mean_of(scaled) - unit * mean_of(scaled * unit))


def gelu_parts(values):
    size = jnp.abs(values)
    t = 1.0 / (1.0 + (0.3275911 * ROOT_HALF) * size)
    bell = jnp.exp(values * values * -0.5)
    series = 1.061405429
    for term in (-1.453152027, 1.421413741, -0.284496736, 0.254829592):
        series = term + t * series
    tail = (0.5 * t) * series * bell
    below = jnp.where(values >= 0, 1.0 - tail, tail)
    return values * below, below + values * (bell * DENSITY_SCALE)


def column_sum(rows):
    return jnp.sum(rows, axis=0, keepdims=True)


def up_kernel(
    place_ref, x_ref, ctx_own_ref, ctx_ref, wo_ref, bo_ref, g1_ref, s1_ref, wi_ref, bi_ref, wb_ref,
    bb_ref, g2_ref, s2_ref, cot_ref,
    out_ref, mid_ref, branch_ref, turned_ref, slope_ref, unit_ref, inverse_ref, low_ref, sums_ref,
    normed_sc, low_sc, acc_sc,
):
    step = pl.program_id(0)
    groups = wo_ref.shape[0]

    @pl.when(step == 0)
    def _():
        @pl.loop(0, L // MB)
        def _(r):
            rows = pl.ds(pl.multiple_of(r * MB, MB), MB)
            total = x_ref[rows, :].astype(F32) + bo_ref[...]
            for s in range(groups):
                ctx = ctx_own_ref[0, rows, :] if s == 0 else ctx_ref[s - 1, rows, :]
                quarter = place_ref[0] ^ s
                total = total + jnp.dot(ctx, wo_ref[quarter], preferred_element_type=F32)
            unit, inverse = normalize(total)
            unit_ref[rows, :] = unit
            inverse_ref[rows, :] = jnp.broadcast_to(inverse, (MB, 128))
            normed = unit * g1_ref[...] + s1_ref[...]
            normed_sc[rows, :] = normed
            low_sc[rows, :] = normed.astype(BF)

        low_ref[...] = jnp.transpose(low_sc[...])
        acc_sc[...] = jnp.zeros_like(acc_sc)

    @pl.loop(0, L // MB)
    def _(r):
        rows = pl.ds(pl.multiple_of(r * MB, MB), MB)
        pre = jnp.dot(low_sc[rows, :], wi_ref[...], preferred_element_type=F32) + bi_ref[...]
        acted, slope = gelu_parts(pre)
        acted = acted.astype(BF)
        slope_ref[rows, :] = slope.astype(BF)
        turned_ref[:, rows] = jnp.transpose(acted)
        acc_sc[rows, :] += jnp.dot(acted, wb_ref[...], preferred_element_type=F32)

    @pl.when(step == pl.num_programs(0) - 1)
    def _():
        sums_ref[...] = jnp.zeros_like(sums_ref)

        @pl.loop(0, L // MB)
        def _(r):
            rows = pl.ds(pl.multiple_of(r * MB, MB), MB)
            unit, inverse = normalize(normed_sc[rows, :] + (acc_sc[rows, :] + bb_ref[...]))
            out_ref[rows, :] = (unit * g2_ref[...] + s2_ref[...]).astype(BF)
            upstream = cot_ref[rows, :].astype(F32)
            middle = normalize_back(upstream * g2_ref[...], unit, inverse)
            mid_ref[rows, :] = middle
            branch = middle.astype(BF)
            branch_ref[rows, :] = branch
            sums_ref[0:1, :] += column_sum(upstream * unit)
            sums_ref[1:2, :] += column_sum(upstream)
            sums_ref[2:3, :] += column_sum(branch.astype(F32))


def feed_up(place, x, ctx_own, ctx, w_out, bo, g1, s1, w_in, bi, w_back, bb, g2, s2, cot):
    width = x.shape[1]
    units = w_in.shape[1]
    groups, own = w_out.shape[0], w_out.shape[1]
    row = whole(1, width)
    return pl.pallas_call(
        up_kernel,
        grid_spec=pltpu.PrefetchScalarGridSpec(
            num_scalar_prefetch=1,
            grid=(units // FC,),
            in_specs=[
                whole(L, width),
                whole(1, L, own),
                whole(groups - 1, L, own),
                whole(groups, own, width),
                row,
                row,
                row,
                pl.BlockSpec((width, FC), lambda n, place: (0, n)),
                pl.BlockSpec((1, FC), lambda n, place: (0, n)),
                pl.BlockSpec((FC, width), lambda n, place: (n, 0)),
                row,
                row,
                row,
                whole(L, width),
            ],
            out_specs=[
                whole(L, width),
                whole(L, width),
                whole(L, width),
                pl.BlockSpec((FC, L), lambda n, place: (n, 0)),
                pl.BlockSpec((L, FC), lambda n, place: (0, n)),
                whole(L, width),
                whole(L, 128),
                whole(width, L),
                whole(8, width),
            ],
            scratch_shapes=[
                pltpu.VMEM((L, width), F32),
                pltpu.VMEM((L, width), BF),
                pltpu.VMEM((L, width), F32),
            ],
        ),
        out_shape=[
            shaped(BF, L, width),
            shaped(F32, L, width),
            shaped(BF, L, width),
            shaped(BF, units, L),
            shaped(BF, L, units),
            shaped(F32, L, width),
            shaped(F32, L, 128),
            shaped(BF, width, L),
            shaped(F32, 8, width),
        ],
        name="feed_up",
        compiler_params=limit(32),
        cost_estimate=HINT,
    )(place, x, ctx_own, ctx, w_out, bo, g1, s1, w_in, bi, w_back, bb, g2, s2, cot)


def down_kernel(
    halved, place_ref, branch_ref, slope_ref, wb_ref, wi_ref, low_ref, mid_ref, unit_ref,
    inverse_ref, g1_ref, wo_ref, turned_own_ref, turned_ref, norm_own_ref, norm_ref, *refs
):
    bias_ref, first_ref, grad_own_ref, grad_ref, sums_ref = refs[:5]
    weight_refs = refs[5 : 7 if halved else 6]
    acc_sc, pre_sc, weight_sc = refs[-3:]
    step = pl.program_id(0)
    last = pl.num_programs(0) - 1
    groups, own = wo_ref.shape[0], wo_ref.shape[1]

    def give():
        if not halved:
            weight_refs[0][...] = weight_sc[...]
            return
        core = place_ref[1]
        chips, size = weight_refs[0].shape[0], weight_refs[0].shape[1]
        for chip in range(chips):
            for side, ref in ((1 - core, weight_refs[0]), (core, weight_refs[1])):
                at = pl.multiple_of((chip * 2 + side) * size, size)
                ref[chip] = weight_sc[pl.ds(at, size), :]

    @pl.when(step == 0)
    def _():
        acc_sc[...] = mid_ref[...]

    @pl.when(step < last)
    def _():
        total = None
        for r in range(L // MB):
            rows = slice(r * MB, (r + 1) * MB)
            pre = lax.dot_general(
                branch_ref[rows, :], wb_ref[...], NT, preferred_element_type=F32
            ) * slope_ref[rows, :].astype(F32)
            pre = pre.astype(BF)
            pre_sc[rows, :] = pre
            part = column_sum(pre.astype(F32))
            total = part if r == 0 else total + part
            acc_sc[rows, :] += lax.dot_general(
                pre, wi_ref[...], NT, preferred_element_type=F32
            )
        bias_ref[0:1, :] = total
        weight_sc[...] = jnp.dot(
            low_ref[...], pre_sc[...], preferred_element_type=F32
        ).astype(BF)
        give()

    @pl.when(step == last)
    def _():
        sums_ref[...] = jnp.zeros_like(sums_ref)

        @pl.loop(0, L // MB)
        def _(r):
            rows = pl.ds(pl.multiple_of(r * MB, MB), MB)
            hidden = acc_sc[rows, :]
            unit = unit_ref[rows, :]
            first = normalize_back(hidden * g1_ref[...], unit, inverse_ref[rows, 0:1])
            first_ref[rows, :] = first
            attended = first.astype(BF)
            pre_sc[rows, :] = attended
            sums_ref[0:1, :] += column_sum(hidden * unit)
            sums_ref[1:2, :] += column_sum(hidden)
            sums_ref[2:3, :] += column_sum(attended.astype(F32))

        def quarter_of(s, turned, norm, out):
            quarter = place_ref[0] ^ s
            at = pl.multiple_of(quarter * own, own)
            weight_sc[pl.ds(at, own), :] = jnp.dot(
                turned, pre_sc[...], preferred_element_type=F32
            ).astype(BF)
            grads = lax.dot_general(
                wo_ref[quarter], pre_sc[...], NT, preferred_element_type=F32
            )
            for h in range(own // HEAD_DIM):
                rows = slice(h * HEAD_DIM, (h + 1) * HEAD_DIM)
                out[rows, :] = (grads[rows, :] * norm[h : h + 1, :]).astype(BF)

        quarter_of(0, turned_own_ref[0], norm_own_ref[0], grad_own_ref.at[0])

        @pl.loop(1, groups)
        def _(s):
            quarter_of(s, turned_ref[s - 1], norm_ref[s - 1], grad_ref.at[s - 1])

        give()


def feed_down(place, halves, branch, slope, w_back, w_in, low, mid, unit, inverse, g1, w_out,
              turned_own, turned, norm_own, norm):
    width = branch.shape[1]
    units = w_in.shape[1]
    groups, own = w_out.shape[0], w_out.shape[1]
    steps = units // FC
    inside = lambda n: jnp.minimum(n, steps - 1)
    out_specs = [
        pl.BlockSpec((8, FC), lambda n, place: (0, inside(n))),
        whole(L, width),
        whole(1, own, L),
        whole(groups - 1, own, L),
        whole(8, width),
    ]
    out_shape = [
        shaped(F32, 8, units),
        shaped(F32, L, width),
        shaped(BF, 1, own, L),
        shaped(BF, groups - 1, own, L),
        shaped(F32, 8, width),
    ]
    if halves:
        size = width // (2 * halves)
        out_specs += [pl.BlockSpec((halves, size, FC), lambda n, place: (0, 0, n))] * 2
        out_shape += [shaped(BF, halves, size, units + width)] * 2
    else:
        out_specs += [pl.BlockSpec((width, FC), lambda n, place: (0, n))]
        out_shape += [shaped(BF, width, units + width)]
    return pl.pallas_call(
        functools.partial(down_kernel, bool(halves)),
        grid_spec=pltpu.PrefetchScalarGridSpec(
            num_scalar_prefetch=1,
            grid=(steps + 1,),
            in_specs=[
                whole(L, width),
                pl.BlockSpec((L, FC), lambda n, place: (0, inside(n))),
                pl.BlockSpec((FC, width), lambda n, place: (inside(n), 0)),
                pl.BlockSpec((width, FC), lambda n, place: (0, inside(n))),
                whole(width, L),
                whole(L, width),
                whole(L, width),
                whole(L, 128),
                whole(1, width),
                whole(groups, own, width),
                whole(1, own, L),
                whole(groups - 1, own, L),
                whole(1, 8, L),
                whole(groups - 1, 8, L),
            ],
            out_specs=out_specs,
            scratch_shapes=[
                pltpu.VMEM((L, width), F32),
                pltpu.VMEM((L, FC), BF),
                pltpu.VMEM((width, FC), BF),
            ],
        ),
        out_shape=out_shape,
        name="feed_down",
        compiler_params=limit(34),
        cost_estimate=HINT,
    )(place, branch, slope, w_back, w_in, low, mid, unit, inverse, g1, w_out,
      turned_own, turned, norm_own, norm)


def product_kernel(place_ref, left_ref, right_ref, out_ref):
    out_ref[...] = jnp.dot(
        left_ref[...], right_ref[...], preferred_element_type=F32
    ).astype(BF)


def product(place, left, right, sizes):
    rows, depth = left.shape
    columns = right.shape[1]
    count, size, halved = sizes
    take = (lambda n, place: (2 * n + 1 - place[1], 0)) if halved else (lambda n, place: (n, 0))
    return pl.pallas_call(
        product_kernel,
        grid_spec=pltpu.PrefetchScalarGridSpec(
            num_scalar_prefetch=1,
            grid=(count,),
            in_specs=[pl.BlockSpec((size, depth), take), whole(depth, columns)],
            out_specs=pl.BlockSpec((size, columns), lambda n, place: (n, 0)),
        ),
        out_shape=shaped(BF, count * size, columns),
        name="back_weights",
        compiler_params=limit(10),
        cost_estimate=HINT,
    )(place, left, right)


def kept_kernel(place_ref, left_ref, right_ref, got_ref, a_sent, a_kept, b_sent, b_kept):
    chip = pl.program_id(0)
    chip_y, chip_x = chip // 2, lax.rem(chip, 2)
    here_x, here_y = place_ref[2], place_ref[3]
    value = jnp.dot(left_ref[...], right_ref[...], preferred_element_type=F32)
    value = (value + got_ref[0].astype(F32)).astype(BF)
    cut = a_sent.shape[1]

    @pl.when(chip_x == here_x)
    def _():
        a_kept[chip_y] = value[:cut, :]

    @pl.when(chip_x != here_x)
    def _():
        a_sent[chip_y] = value[:cut, :]

    @pl.when(chip_y == here_y)
    def _():
        b_kept[chip_x] = value[cut:, :]

    @pl.when(chip_y != here_y)
    def _():
        b_sent[chip_x] = value[cut:, :]


def product_kept(place, left, right, got):
    chips, size, columns = got.shape
    depth = left.shape[1]
    part = whole(2, size // 2, columns)
    return pl.pallas_call(
        kept_kernel,
        grid_spec=pltpu.PrefetchScalarGridSpec(
            num_scalar_prefetch=1,
            grid=(chips,),
            in_specs=[
                pl.BlockSpec((size, depth), lambda n, place: (2 * n + place[1], 0)),
                whole(depth, columns),
                pl.BlockSpec((1, size, columns), lambda n, place: (n, 0, 0)),
            ],
            out_specs=[part] * 4,
        ),
        out_shape=[shaped(BF, 2, size // 2, columns)] * 4,
        name="kept_weights",
        compiler_params=limit(14),
        cost_estimate=HINT,
    )(place, left, right, got)


def total_of(*items):
    total = items[0].astype(F32)
    for item in items[1:]:
        total = total + item.astype(F32)
    return total.astype(BF)


def chips_kernel(count, layout, place_ref, *refs):
    inputs, outs = refs[:count], refs[count:]
    here_x, here_y = place_ref[2], place_ref[3]
    for order, (way, sources) in enumerate(layout):
        sent, kept = outs[2 * order], outs[2 * order + 1]
        start = 0
        for number, low, high in sources:
            kept_ref, got_ref = inputs[2 * number], inputs[2 * number + 1]
            for g in range(kept_ref.shape[0]):
                rows = slice(start, start + high - low)
                start += high - low
                for other in range(2):
                    for out, far in ((sent, 1), (kept, 0)):
                        if way == "x":
                            chip = other * 2 + (here_x ^ far)
                        else:
                            chip = (here_y ^ far) * 2 + other
                        out[other, rows, :] = total_of(
                            kept_ref[g, chip, low:high, :], got_ref[g, chip, low:high, :]
                        )


def sum_chips(place, pairs, parts, block):
    specs, out_specs, out_shape = [], [], []
    columns = pairs[0][0].shape[-1]
    for kept, _ in pairs:
        shape = kept.shape[:3] + (block,)
        specs += [pl.BlockSpec(shape, lambda n, place: (0, 0, 0, n))] * 2
    for _, sources in parts:
        height = sum(pairs[n][0].shape[0] * (high - low) for n, low, high in sources)
        out_specs += [pl.BlockSpec((2, height, block), lambda n, place: (0, 0, n))] * 2
        out_shape += [shaped(BF, 2, height, columns)] * 2
    return pl.pallas_call(
        functools.partial(chips_kernel, 2 * len(pairs), parts),
        grid_spec=pltpu.PrefetchScalarGridSpec(
            num_scalar_prefetch=1, grid=(columns // block,), in_specs=specs, out_specs=out_specs
        ),
        out_shape=out_shape,
        name="sum_chips",
        compiler_params=limit(14),
        cost_estimate=HINT,
    )(place, *[item for pair in pairs for item in pair])


def pairs_kernel(place_ref, a_kept, a_got, b_kept, b_got, a_sent, a_own, b_sent, b_own):
    here_x, here_y = place_ref[2], place_ref[3]
    for here, kept, got, sent, own in (
        (here_y, a_kept, a_got, a_sent, a_own),
        (here_x, b_kept, b_got, b_sent, b_own),
    ):
        sent[...] = total_of(kept[1 - here], got[1 - here])
        own[...] = total_of(kept[here], got[here])


def sum_pairs(place, a_kept, a_got, b_kept, b_got, block):
    columns = a_kept.shape[-1]
    spec = lambda item: pl.BlockSpec((2, item.shape[1], block), lambda n, place: (0, 0, n))
    flat = lambda item: pl.BlockSpec((item.shape[1], block), lambda n, place: (0, n))
    return pl.pallas_call(
        pairs_kernel,
        grid_spec=pltpu.PrefetchScalarGridSpec(
            num_scalar_prefetch=1,
            grid=(columns // block,),
            in_specs=[spec(a_kept), spec(a_got), spec(b_kept), spec(b_got)],
            out_specs=[flat(a_kept)] * 2 + [flat(b_kept)] * 2,
        ),
        out_shape=[shaped(BF, a_kept.shape[1], columns)] * 2
        + [shaped(BF, b_kept.shape[1], columns)] * 2,
        name="sum_pairs",
        compiler_params=limit(12),
        cost_estimate=HINT,
    )(place, a_kept, a_got, b_kept, b_got)


def cut_kernel(place_ref, a_kept, a_got, b_kept, b_got, sent, kept, sum_sc):
    cut = a_kept.shape[0]
    sum_sc[0:cut, :] = a_kept[...].astype(F32) + a_got[...].astype(F32)
    sum_sc[cut:, :] = b_kept[...].astype(F32) + b_got[...].astype(F32)
    size = kept.shape[1]
    for s, out in ((0, kept.at[0]), (1, sent.at[0]), (2, kept.at[1]), (3, sent.at[1])):
        at = pl.multiple_of((place_ref[0] ^ s) * size, 8)
        out[...] = sum_sc[pl.ds(at, size), :].astype(BF)


def cut_quarters(place, a_kept, a_got, b_kept, b_got, block):
    columns = a_kept.shape[-1]
    height = a_kept.shape[0] + b_kept.shape[0]
    spec = lambda item: pl.BlockSpec((item.shape[0], block), lambda n, place: (0, n))
    return pl.pallas_call(
        cut_kernel,
        grid_spec=pltpu.PrefetchScalarGridSpec(
            num_scalar_prefetch=1,
            grid=(columns // block,),
            in_specs=[spec(a_kept), spec(a_got), spec(b_kept), spec(b_got)],
            out_specs=[pl.BlockSpec((2, height // 4, block), lambda n, place: (0, 0, n))] * 2,
            scratch_shapes=[pltpu.VMEM((height, block), F32)],
        ),
        out_shape=[shaped(BF, 2, height // 4, columns)] * 2,
        name="cut_quarters",
        compiler_params=limit(12),
        cost_estimate=HINT,
    )(place, a_kept, a_got, b_kept, b_got)


def last_kernel(a_kept, a_got, b_kept, b_got, short_ref, *outs):
    size = outs[0].shape[0] - 16
    many = short_ref.shape[0] // 8 * 8
    first = 10
    for s, out in enumerate(outs):
        rows = slice(s % 2 * size, (s % 2 + 1) * size)
        kept, got = (a_kept, a_got) if s < 2 else (b_kept, b_got)
        out[0:size, :] = total_of(kept[rows, :], got[rows, :])
        row = lax.broadcasted_iota(I32, (many, short_ref.shape[1]), 0)
        short = jnp.where(row < first, short_ref[...], 0.0)
        short = short + jnp.where(row == first, short_ref[first + s : first + s + 1, :], 0.0)
        out[size : size + many, :] = short.astype(BF)


def cut_last(a_kept, a_got, b_kept, b_got, short):
    vmem = pl.BlockSpec(memory_space=pltpu.VMEM)
    size, columns = b_kept.shape[0] // 2, b_kept.shape[1]
    return pl.pallas_call(
        last_kernel,
        in_specs=[vmem] * 5,
        out_specs=[vmem] * 4,
        out_shape=[shaped(BF, size + 16, columns)] * 4,
        name="cut_last",
        compiler_params=limit(8),
        cost_estimate=HINT,
    )(a_kept, a_got, b_kept, b_got, short)


def join_kernel(place_ref, own, one, two, *outs):
    size = own.shape[0]
    start = 0
    for out in outs:
        lanes = slice(start, start + out.shape[1])
        for s, piece in ((0, own[:, lanes]), (2, one[:, lanes]), (1, two[0, :, lanes]), (3, two[1, :, lanes])):
            at = pl.multiple_of((place_ref[0] ^ s) * size, 8)
            out[pl.ds(at, size), :] = piece.astype(F32)
        start += out.shape[1]


def join_quarters(place, own, one, two, widths):
    vmem = pl.BlockSpec(memory_space=pltpu.VMEM)
    return pl.pallas_call(
        join_kernel,
        in_specs=[pl.BlockSpec(memory_space=pltpu.SMEM)] + [vmem] * 3,
        out_specs=[vmem] * len(widths),
        out_shape=[shaped(F32, 4 * own.shape[0], width) for width in widths],
        name="join_quarters",
        compiler_params=limit(8),
        cost_estimate=HINT,
    )(place, own, one, two)


def chips_join_kernel(place_ref, mine_a, mine_b, got_a, got_b, ends_ref, got_ends, out_ref, *outs):
    core, here_x, here_y = place_ref[1], place_ref[2], place_ref[3]
    cut = mine_a.shape[2]
    size = cut + mine_b.shape[2]
    for far_y in range(2):
        for far_x in range(2):
            chip = (here_y ^ far_y) * 2 + (here_x ^ far_x)
            for side, a_ref, b_ref in ((core, mine_a, mine_b), (1 - core, got_a, got_b)):
                at = (chip * 2 + side) * size
                first = pl.multiple_of(at, 8)
                out_ref[pl.ds(first, cut), :] = a_ref[far_y, far_x].astype(F32)
                second = pl.multiple_of(at + cut, 8)
                out_ref[pl.ds(second, size - cut), :] = b_ref[far_x, far_y].astype(F32)
    total = ends_ref[...].astype(F32) + got_ends[...].astype(F32)
    bias_ref, tables_ref, inner_ref = outs[:3]
    vectors = outs[3:]
    here = (here_y * 2 + here_x) * 2 + core
    width = total.shape[1]
    share = vectors[0].shape[1]
    part = inner_ref.shape[1]
    deep = part * 8 // width
    slices = jnp.zeros((len(vectors), share), F32)
    inner = jnp.zeros((1, part), F32)
    for d in range(8):
        mine = here == d
        slices = slices + jnp.where(
            mine, total[0 : len(vectors), d * share : (d + 1) * share], 0.0
        )
        row, lane = 6 + d * part // width, d * part % width
        inner = inner + jnp.where(mine, total[row : row + 1, lane : lane + part], 0.0)
    inner_ref[...] = inner
    for n, ref in enumerate(vectors):
        ref[...] = slices[n : n + 1, :]
    short = total[6 + deep : 7 + deep, :]
    own = bias_ref.shape[1]
    bias_ref[0:1, :] = short[:, 0:own]
    bias_ref[1:2, :] = short[:, own : 2 * own]
    per, _, buckets = tables_ref.shape
    for n in range(2):
        for h in range(per):
            lane = 2 * own + (n * per + h) * buckets
            tables_ref[h, n : n + 1, :] = short[:, lane : lane + buckets]


def join_chips(place, mine_a, mine_b, got_a, got_b, ends, got_ends, units, own, heads, buckets):
    vmem = pl.BlockSpec(memory_space=pltpu.VMEM)
    rows = 8 * (mine_a.shape[2] + mine_b.shape[2])
    width = mine_a.shape[-1]
    out_shape = [
        shaped(F32, rows, width),
        shaped(F32, 2, own),
        shaped(F32, heads, 2, buckets),
        shaped(F32, 1, units // 8),
    ] + [shaped(F32, 1, width // 8)] * 6
    return pl.pallas_call(
        chips_join_kernel,
        in_specs=[pl.BlockSpec(memory_space=pltpu.SMEM)] + [vmem] * 6,
        out_specs=[vmem] * len(out_shape),
        out_shape=out_shape,
        name="join_chips",
        compiler_params=limit(8),
        cost_estimate=HINT,
    )(place, mine_a, mine_b, got_a, got_b, ends, got_ends)


def tie(values, *others):
    return lax.optimization_barrier((values, others))[0]


def swap(array, bit):
    count = lax.axis_size("docs")
    return lax.ppermute(array, "docs", [(i, i ^ (1 << bit)) for i in range(count)])


def away(array, distance):
    count = lax.axis_size("heads")
    return lax.ppermute(array, "heads", [(i, i ^ distance) for i in range(count)])


def in_order(pieces, z):
    stacked = jnp.stack(pieces)
    picks = [lax.dynamic_index_in_dim(stacked, z ^ s, 0) for s in range(len(pieces))]
    return jnp.concatenate(picks, axis=0)


def tree(items):
    while len(items) > 1:
        items = [items[n] + items[n + 1] for n in range(0, len(items), 2)]
    return items[0]


def sum_everywhere(rows):
    for bit in range(lax.axis_size("docs").bit_length() - 1):
        rows = rows + swap(rows, bit)
    return tree([rows] + [away(rows, s) for s in range(1, lax.axis_size("heads"))])


def spread_plane(first, second):
    got = [swap(first, 1), swap(second, 2)]
    first, second = jnp.stack([first, got[0]]), jnp.stack([second, got[1]])
    got = [swap(first, 2), swap(second, 1)]
    return jnp.stack([first, got[0]]), jnp.stack([second, got[1]])


def reduce_docs(blocks):
    bits = blocks.shape[0].bit_length() - 1
    docs = lax.axis_index("docs")
    current = blocks.reshape((2,) * bits + blocks.shape[1:])
    for bit in range(bits):
        mine = (docs >> bit) & 1
        axis = bits - 1 - bit
        sent = lax.dynamic_index_in_dim(current, 1 - mine, axis, keepdims=False)
        kept = lax.dynamic_index_in_dim(current, mine, axis, keepdims=False)
        current = total_of(kept, swap(sent, bit))
    return current


def spread_docs(block):
    count = lax.axis_size("docs")
    docs = lax.axis_index("docs")
    current = block
    for done, bit in enumerate(range(count.bit_length() - 2, -1, -1)):
        got = swap(current, bit)
        mine = ((docs >> bit) & 1) == 1
        current = jnp.stack(
            [jnp.where(mine, got, current), jnp.where(mine, current, got)], axis=done
        )
    return current.reshape((count,) + block.shape)


def body(
    layer_input, token_boxes, lengths, w_qkv, qv_bias, rel_tables, w_out, out_bias,
    gain_one, shift_one, w_in, in_bias, w_back, back_bias, gain_two, shift_two, cotangent,
):
    width = layer_input.shape[1]
    units = w_in.shape[1]
    groups = lax.axis_size("heads")
    count = lax.axis_size("docs")
    docs = lax.axis_index("docs")
    z = lax.axis_index("heads")
    own = w_qkv.shape[2]
    heads = rel_tables.shape[1]
    buckets = rel_tables.shape[2]
    columns = 3 * own
    share = width // count
    small = columns // count
    chips = 4 if count == 8 and share % 16 == 0 and small % 8 == 0 else 0
    place = jnp.stack([z, docs & 1, (docs >> 1) & 1, (docs >> 2) & 1]).astype(I32)

    matrix = w_qkv.transpose(1, 2, 0).reshape(columns, width)
    room = jnp.zeros((128 - heads * buckets,), BF)
    line = jnp.concatenate(
        [qv_bias[0], qv_bias[1], rel_tables[0].reshape(-1), room, rel_tables[1].reshape(-1), room]
    )
    extra = jnp.pad(line[None], ((0, 7), (0, width - line.shape[0])))
    piece = jnp.concatenate(
        [lax.dynamic_slice_in_dim(matrix, docs * small, small, axis=0), extra], axis=0
    )
    got = [away(piece, s) for s in range(1, groups)]
    bucket, near = buckets_of(place, lengths, token_boxes)

    ctx_own, turned_own, raised_own, qkv_own, norm_own = attend_forward(
        place, layer_input, (matrix[None],), extra[None], bucket, near
    )
    arrived = jnp.stack(tie(got, ctx_own))
    if chips:
        cut = (small // 2 + 7) // 8 * 8
        first, second = spread_plane(arrived[:, :cut], arrived[:, cut:small])
        weights, ctx, turned, raised, qkv, norm = attend_forward(
            place, layer_input, (first, second, swap(first, 0), swap(second, 0)),
            arrived[:, small:], bucket, near,
        )
    else:
        weights = spread_docs(arrived[:, :small]).transpose(1, 0, 2, 3)
        weights = weights.reshape(groups - 1, columns, width)
        ctx, turned, raised, qkv, norm = attend_forward(
            place, layer_input, (weights,), arrived[:, small:], bucket, near
        )

    w_out_heads = w_out.reshape(groups, own, width)
    flat = lambda vector: vector.reshape(1, -1)
    layer_output, grad_mid, grad_branch, acted, slope, unit, inverse, low, up_sums = feed_up(
        place, layer_input, ctx_own, ctx, w_out_heads, flat(out_bias), flat(gain_one),
        flat(shift_one), w_in, flat(in_bias), w_back, flat(back_bias), flat(gain_two),
        flat(shift_two), cotangent,
    )
    down = lambda branch: feed_down(
        place, chips, branch, slope, w_back, w_in, low, grad_mid, unit, inverse, flat(gain_one),
        w_out_heads, turned_own, turned, norm_own, norm,
    )
    own_back = lambda grad, start: attend_backward(
        place, chips, layer_input, matrix[None], qkv_own, raised_own, norm_own, grad, start
    )
    rest_back = lambda span, grad, start: attend_backward(
        place, chips, layer_input, weights, qkv, raised, norm, grad, start, span
    )

    if chips:
        half = share // 2
        back_size = units // count
        sent = product(place, acted, grad_branch, (chips, back_size, True))
        got = swap(sent.reshape(chips, back_size, width), 0)
        back = product_kept(place, acted, grad_branch, got)
        back_got = [swap(back[0], 1), swap(back[2], 2)]

        in_sums, grad_first, grad_own, grad_rest, down_sums, dense_sent, dense_kept = down(
            tie(grad_branch, back[0], back[2])
        )
        back_got = tie(back_got, grad_first)
        back = sum_pairs(place, back[1], back_got[0], back[3], back_got[1], width // 2)
        back_got = [swap(back[0], 2), swap(back[2], 1)]
        dense_sent = tie(dense_sent, back[0])
        dense_got = swap(dense_sent, 0)

        dx, ds_own, sums_own, own_sent, own_kept = own_back(
            tie(grad_own, dense_sent, back[0], back[2]), grad_first
        )
        dense_got, back_got = tie((dense_got, back_got), dx)
        dense = sum_chips(
            place,
            [(dense_kept[None], dense_got[None])],
            (("x", ((0, 0, half),)), ("y", ((0, half, share),))),
            (units + width) // 3,
        )
        back_sent, back = cut_quarters(
            place, back[1], back_got[0], back[3], back_got[1], width // 2
        )
        dense = list(dense)
        dense[0], dense[2], own_sent = tie((dense[0], dense[2], own_sent), back_sent)
        dense_got = [swap(dense[0], 1), swap(dense[2], 2)]
        back_got = away(back_sent, 1)
        own_got = swap(own_sent, 0)

        dx, ds_one, sums_one, one_sent, one_kept = rest_back(
            (0, 1), tie(grad_rest, dense[0], dense[2], own_sent, back_sent), dx
        )
        own_got, back_got = tie((own_got, back_got), dx)
        back = total_of(back, back_got)
        one_sent = tie(one_sent, back)
        one_got = swap(one_sent, 0)
        back_got = away(back[1], 2)

        dx, ds_two, sums_two, two_sent, two_kept = rest_back(
            (1, 3), tie(grad_rest, one_sent, back), dx
        )
        dense_got, back_got, one_got = tie((dense_got, back_got, one_got), dx)
        dense = list(
            sum_pairs(
                place, dense[1], dense_got[0], dense[3], dense_got[1], (units + width) // 2
            )
        )
        back = total_of(back[0], back_got)
        two_sent, dense[0], dense[2], back = tie((two_sent, dense[0], dense[2], back), dense[1])
        two_got = swap(two_sent, 0)
        dense_got = [swap(dense[0], 2), swap(dense[2], 1)]
        back_one = away(back, 2)
        scores = (ds_own, ds_one, ds_two)
        acc = table_products(
            scores, tie(bucket, back, two_sent, dense[0], dense[2]),
            jnp.zeros((groups * heads * 8, 512), F32), 0,
        )

        two_got, dense_got, back_one = tie((two_got, dense_got, back_one), acc)
        dense_sent, dense = cut_quarters(
            place, dense[1], dense_got[0], dense[3], dense_got[1], (units + width) // 2
        )
        own_got, one_got, two_got = tie((own_got, one_got, two_got), dense_sent)
        last_a = sum_chips(
            place, [(own_kept, own_got), (one_kept, one_got)],
            (("x", ((0, 0, small), (1, 0, small))),), width // 2,
        )
        last_b = sum_chips(place, [(two_kept, two_got)], (("y", ((0, 0, small),)),), width // 2)
        back_two = jnp.stack([back, back_one])
        last_a, last_b, dense_sent, back_two = tie((last_a, last_b, dense_sent, back_two))
        last_a_got = swap(last_a[0], 1)
        last_b_got = swap(last_b[0], 2)
        dense_got = away(dense_sent, 1)
        back_two = away(back_two, 1)
        acc = table_products(
            scores, tie(bucket, last_b[0], last_a[0], dense_sent), acc, 1
        )
        short = short_rows(acc, (sums_own, sums_one, sums_two), down_sums, up_sums, in_sums, heads)

        last_a_got, last_b_got, dense_got = tie((last_a_got, last_b_got, dense_got), acc)
        last = list(sum_pairs(place, last_a[1], last_a_got, last_b[1], last_b_got, width // 2))
        dense = total_of(dense, dense_got)
        last[0], last[2], dense = tie((last[0], last[2], dense), last[1])
        last_got = [swap(last[0], 2), swap(last[2], 1)]
        dense_got = away(dense[1], 2)
        last_got, short = tie((last_got, short), dense)
        last = cut_last(last[1], last_got[0], last[3], last_got[1], short)
        last_got = [away(last[s], s) for s in range(1, groups)]
        dense_got, back_two = tie((dense_got, back_two), last[0])
        dense = total_of(dense[0], dense_got)
        dense_one = away(dense, 2)
        (out_back,) = join_quarters(place, back, back_one, back_two, (width,))
        last_got = tie(last_got, dense, out_back)
        quarter = total_of(last[0][:small], *[item[:small] for item in last_got])
        ends = tree([item[small:].astype(F32) for item in [last[0]] + last_got]).astype(BF)
        first, second = quarter[:cut], quarter[cut:]
        got = [swap(first, 1), swap(second, 2), swap(ends, 1)]
        dense_one = tie(dense_one, first, second)
        dense_two = away(jnp.stack([dense, dense_one]), 1)
        got = tie(got, dense_one)
        first, second = jnp.stack([first, got[0]]), jnp.stack([second, got[1]])
        ends = total_of(ends, got[2])
        got = [swap(first, 2), swap(second, 1), swap(ends, 2)]
        dense_two = tie(dense_two, first, second)
        first, second = jnp.stack([first, got[0]]), jnp.stack([second, got[1]])
        ends = total_of(ends, got[2])
        got = [swap(first, 0), swap(second, 0), swap(ends, 0)]
        out_in, out_out = join_quarters(place, dense, dense_one, dense_two, (units, width))
        got = tie(got, out_in)
        full, grad_bias, grad_tables, grad_inner, *vectors = join_chips(
            place, first, second, got[0], got[1], ends, got[2], units, own, heads, buckets
        )
        grad_tables = grad_tables.transpose(1, 0, 2)
        vectors = [vector.reshape(share) for vector in vectors]
        grad_inner = grad_inner.reshape(units // count)
    else:
        back_grads = product(place, acted, grad_branch, (units // FC, FC, False))
        in_sums, grad_first, grad_own, grad_rest, down_sums, dense_grads = down(grad_branch)
        dx, ds_own, sums_own, dw_own = own_back(grad_own, grad_first)
        dx, ds_rest, sums_rest, dw_rest = rest_back(None, grad_rest, dx)
        acc = jnp.zeros((groups * heads * 8, 512), F32)
        for part in range(2):
            acc = table_products((ds_own, ds_rest), bucket, acc, part)
        short = short_rows(acc, (sums_own, sums_rest), down_sums, up_sums, in_sums, heads)
        begin = 6 + units // width
        quarters = in_order([short[begin + s] for s in range(groups)], z)
        total = sum_everywhere(jnp.concatenate([short[:begin], quarters], axis=0))
        ends = lax.dynamic_index_in_dim(total, begin + z, 0, keepdims=False)

        def sum_heads(parts):
            return total_of(parts[0], *[away(parts[s], s) for s in range(1, groups)])

        def dense_rows(grads):
            rows = reduce_docs(grads.reshape(count, -1, grads.shape[1]))
            parts = rows.reshape(-1, groups, width)
            parts = [
                lax.dynamic_index_in_dim(parts, z ^ s, 1, keepdims=False) for s in range(groups)
            ]
            mine = sum_heads(parts)
            pieces = [mine] + [away(mine, s) for s in range(1, groups)]
            return in_order(pieces, z).transpose(1, 0, 2).reshape(rows.shape).astype(F32)

        out_back = dense_rows(back_grads)
        rows = dense_rows(dense_grads)
        out_in, out_out = rows[:, :units], rows[:, units:]
        blocks = jnp.concatenate([dw_own, dw_rest]).reshape(groups, count, small, width)
        blocks = blocks.transpose(1, 0, 2, 3).reshape(count, groups * small, width)
        blocks = reduce_docs(blocks).reshape(groups, small, width)
        full = spread_docs(sum_heads([blocks[s] for s in range(groups)]))
        full = full.reshape(columns, width).astype(F32)

        mine = lambda vector: lax.dynamic_slice_in_dim(
            vector, docs * (vector.shape[0] // count), vector.shape[0] // count
        )
        grad_bias = ends[: 2 * own].reshape(2, own)
        grad_tables = ends[2 * own : 2 * own + 2 * heads * buckets].reshape(2, heads, buckets)
        vectors = [mine(total[n]) for n in range(6)]
        grad_inner = mine(total[6:begin].reshape(-1))
    return (
        layer_output,
        dx.astype(BF),
        full.reshape(3, own, width).transpose(2, 0, 1),
        grad_bias,
        grad_tables,
        out_out,
        vectors[2],
        vectors[0],
        vectors[1],
        out_in,
        grad_inner,
        out_back,
        vectors[5],
        vectors[3],
        vectors[4],
    )


def solution(mesh):
    rows = P(("docs", "heads"), None)
    return jax.shard_map(
        body,
        mesh=mesh,
        in_specs=(
            rows,
            P(None, "docs"),
            P("docs"),
            P(None, None, "heads"),
            P(None, "heads"),
            P(None, "heads", None),
            P(),
            P(),
            P(),
            P(),
            P(),
            P(),
            P(),
            P(),
            P(),
            P(),
            rows,
        ),
        out_specs=(
            rows,
            rows,
            P(None, None, "heads"),
            P(None, "heads"),
            P(None, "heads", None),
            P("docs", None),
            P("docs"),
            P("docs"),
            P("docs"),
            P("docs", None),
            P("docs"),
            P("docs", None),
            P("docs"),
            P("docs"),
            P("docs"),
        ),
        check_vma=False,
    )
```

profile of v0, /device:TPU:0, one launch (start us, length us, event | category | flops | bytes accessed | tf_op | source)
XLA Modules:
  0.0 214.5 jit_solution(5277753745065815456)
XLA Ops:
  3.4 3.1 %collective-permute-start = (bf16[80,768]{1,0:T(8,128)(2,1)S(1)}, bf16[80,768]{1,0:T(8,128)(2,1)S(1)}, u32[]{:S(2)}, u32[]{:S(2)}) collective-permute-start(bf16[80,768]{1,0:T(8,128)(2,1)S(1)} %pad_maximum_fusion.9), channel_id=1, source_target_pairs={{0,1},{1,0},{2,3},{3,2},{4,5},{5,4},{6,7},{7,6},{8,9},{9,8},{10,11... | collective-permute-start | bytes 368648 | tf_op jit(solution)/shard_map/ppermute | solution.py:1142
  6.5 2.6 %collective-permute-start.1 = (bf16[80,768]{1,0:T(8,128)(2,1)S(1)}, bf16[80,768]{1,0:T(8,128)(2,1)S(1)}, u32[]{:S(2)}, u32[]{:S(2)}) collective-permute-start(bf16[80,768]{1,0:T(8,128)(2,1)S(1)} %pad_maximum_fusion.9), channel_id=1, source_target_pairs={{0,2},{1,3},{2,0},{3,1},{4,6},{5,7},{6,4},{7,5},{8,10},{9,11},{10,... | collective-permute-start | bytes 368648 | tf_op jit(solution)/shard_map/ppermute | solution.py:1142
  10.5 2.9 %buckets.1 = (s32[512,512]{1,0:T(8,128)S(1)}, s32[5,128,128]{2,1,0:T(8,128)S(1)}) custom-call(s32[4]{0:T(128)S(1)} %pad_add_fusion.place_ref, s32[4]{0:T(128)S(1)} %copy-done.42, s32[2,2048]{1,0:T(2,128)S(1)} %copy-done.40), custom_call_target="tpu_custom_call" | custom-call | flops 1 | bytes 1 | tf_op jit(solution)/shard_map/buckets/pallas_call | solution.py:96
  15.8 4.6 %attend_forward.2 = (bf16[1,512,192]{2,1,0:T(8,128)(2,1)S(1)}, bf16[1,192,512]{2,1,0:T(8,128)(2,1)S(1)}, bf16[1,3,512,512]{3,2,1,0:T(8,128)(2,1)S(1)}, bf16[1,576,512]{2,1,0:T(8,128)(2,1)S(1)}, f32[1,8,512]{2,1,0:T(8,128)S(1)}) custom-call(s32[4]{0:T(128)S(1)} %pad_add_fusion.place_ref, bf16[512,768]{1,0:T(8,128)(2,1)S(1)} %copy-done, ...), custom_call_target="tpu_custom_call" | custom-call | flops 1 | bytes 1 | tf_op jit(solution)/shard_map/attend_forward/pallas_call | solution.py:274
  20.6 1.8 collective-permute-start.3
  22.4 1.6 collective-permute-start.5
  24.0 2.5 %collective-permute-done.3 = bf16[3,40,768]{2,1,0:T(8,128)(2,1)S(1)} collective-permute-done((bf16[3,40,768]{2,1,0:T(8,128)(2,1)S(1)}, bf16[3,40,768]{2,1,0:T(8,128)(2,1)S(1)}, u32[]{:S(2)}, u32[]{:S(2)}) %collective-permute-start.3) | collective-permute-done | bytes 184352 | tf_op jit(solution)/shard_map/ppermute | solution.py:1137
  26.6 1.6 collective-permute-start.4
  28.3 1.6 collective-permute-start.6
  29.8 5.7 %collective-permute-done.4 = bf16[2,3,40,768]{3,2,1,0:T(8,128)(2,1)S(1)} collective-permute-done((bf16[2,3,40,768]{3,2,1,0:T(8,128)(2,1)S(1)}, bf16[2,3,40,768]{3,2,1,0:T(8,128)(2,1)S(1)}, u32[]{:S(2)}, u32[]{:S(2)}) %collective-permute-start.4) | collective-permute-done | bytes 368672 | tf_op jit(solution)/shard_map/ppermute | solution.py:1137
  36.5 2.2 %collective-permute-done.8.refs_3_ = bf16[2,2,3,32,768]{4,3,2,1,0:T(8,128)(2,1)S(1)} collective-permute-done((bf16[2,2,3,32,768]{4,3,2,1,0:T(8,128)(2,1)S(1)}, bf16[2,2,3,32,768]{4,3,2,1,0:T(8,128)(2,1)S(1)}, u32[]{:S(2)}, u32[]{:S(2)}) %collective-permute-start.8) | collective-permute-done | bytes 589856 | tf_op jit(solution)/shard_map/ppermute | solution.py:1137
  38.7 13.5 %attend_forward.3 = (bf16[3,576,768]{2,1,0:T(8,128)(2,1)S(1)}, bf16[3,512,192]{2,1,0:T(8,128)(2,1)S(1)}, bf16[3,192,512]{2,1,0:T(8,128)(2,1)S(1)}, bf16[3,3,512,...) custom-call(s32[4]{0:T(128)S(1)} %pad_add_fusion.place_ref, ...), custom_call_target="tpu_custom_call" | custom-call | flops 1 | bytes 1 | tf_op jit(solution)/shard_map/attend_forward/pallas_call | solution.py:274
  52.3 1.5 copy-done.3
  56.5 17.6 %feed_up.1 = (bf16[512,768]{1,0:T(8,128)(2,1)}, f32[512,768]{1,0:T(8,128)S(1)}, bf16[512,768]{1,0:T(8,128)(2,1)S(1)}, bf16[3072,512]{1,0:T(8,128)(2,1)S(1)}, bf1...) custom-call(s32[4]{0:T(128)S(1)} %pad_add_fusion.place_ref, ...), custom_call_target="tpu_custom_call" | custom-call | flops 1 | bytes 1 | tf_op jit(solution)/shard_map/feed_up/pallas_call | solution.py:624
  74.1 2.6 %back_weights.1 = bf16[1536,768]{1,0:T(8,128)(2,1)S(1)} custom-call(s32[4]{0:T(128)S(1)} %pad_add_fusion.place_ref, bf16[3072,512]{1,0:T(8,128)(2,1)S(1)} %get-tuple-element.180.left_ref, bf16[512,768]{1,0:T(8,128)(2,1)S(1)} %get-tuple-element.183.right_ref.branch_ref), custom_call_target="tpu_custom_call" | custom-call | flops 1 | bytes 1 | tf_op jit(solution)/shard_map/back_weights/pallas_call | solution.py:840
  77.1 4.4 %collective-permute-done.9.got_ref = bf16[4,384,768]{2,1,0:T(8,128)(2,1)S(1)} collective-permute-done((bf16[4,384,768]{2,1,0:T(8,128)(2,1)S(1)}, bf16[4,384,768]{2,1,0:T(8,128)(2,1)S(1)}, u32[]{:S(2)}, u32[]{:S(2)}) %collective-permute-start.9) | collective-permute-done | bytes 2359328 | tf_op jit(solution)/shard_map/ppermute | solution.py:1137
  81.5 2.7 %kept_weights.1 = (bf16[2,192,768]{2,1,0:T(8,128)(2,1)S(1)}, bf16[2,192,768]{2,1,0:T(8,128)(2,1)S(1)}, bf16[2,192,768]{2,1,0:T(8,128)(2,1)S(1)}, bf16[2,192,768]{2,1,0:T(8,128)(2,1)S(1)}) custom-call(s32[4]{0:T(128)S(1)} %pad_add_fusion.place_ref, bf16[3072,512]{1,0:T(8,128)(2,1)S(1)} %get-tuple-element.180.left_ref, ...), custom_call_target="tpu_custom_call" | custom-call | flops 1 | bytes 1 | tf_op jit(solution)/shard_map/kept_weights/pallas_call | solution.py:884
  85.2 1.5 collective-permute-start.11
  87.4 16.1 %feed_down.1 = (f32[8,3072]{1,0:T(8,128)S(1)}, f32[512,768]{1,0:T(8,128)S(1)}, bf16[1,192,512]{2,1,0:T(8,128)(2,1)S(1)}, bf16[3,192,512]{2,1,0:T(8,128)(2,1)S(1)...) custom-call(s32[4]{0:T(128)S(1)} %copy-done.25, ...), custom_call_target="tpu_custom_call" | custom-call | flops 1 | bytes 1 | tf_op jit(solution)/shard_map/feed_down/pallas_call | solution.py:793
  106.6 1.4 copy-done.14
  108.0 4.7 %attend_backward.3 = (f32[512,768]{1,0:T(8,128)S(1)}, bf16[1,3,512,512]{3,2,1,0:T(8,128)(2,1)S(1)}, f32[1,1,576]{2,1,0:T(1,128)S(1)}, bf16[1,4,72,768]{3,2,1,0:T(8,128)(2,1)S(1)}, bf16[1,4,72,768]{3,2,1,0:T(8,128)(2,1)S(1)}) custom-call(s32[4]{0:T(128)S(1)} %copy-done.26, bf16[512,768]{1,0:T(8,128)(2,1)S(1)} %copy-done.1, bf16[1,576,768]{2,1,0:T(8,128)(2,1)S(1)} %bitcast.73, ...), custom_call_target="tpu_custom_call" | custom-call | flops 1 | bytes 1 | tf_op jit(solution)/shard_map/attend_backward/pallas_call | solution.py:389
  112.8 1.6 collective-permute-done.13.a_got
  114.6 1.9 sum_chips.3
  119.6 1.5 collective-permute-start.18
  121.2 4.7 %attend_backward.4 = (f32[512,768]{1,0:T(8,128)S(1)}, bf16[1,3,512,512]{3,2,1,0:T(8,128)(2,1)S(1)}, f32[1,1,576]{2,1,0:T(1,128)S(1)}, bf16[1,4,72,768]{3,2,1,0:T(8,128)(2,1)S(1)}, bf16[1,4,72,768]{3,2,1,0:T(8,128)(2,1)S(1)}) custom-call(s32[4]{0:T(128)S(1)} %copy-done.26, bf16[512,768]{1,0:T(8,128)(2,1)S(1)} %copy-done.1, ...), custom_call_target="tpu_custom_call" | custom-call | flops 1 | bytes 1 | tf_op jit(solution)/shard_map/attend_backward/pallas_call | solution.py:389
  125.9 1.3 collective-permute-done.16
  127.4 2.4 %collective-permute-start.19 = (bf16[96,768]{1,0:T(8,128)(2,1)S(1)}, bf16[96,768]{1,0:T(8,128)(2,1)S(1)}, u32[]{:S(2)}, u32[]{:S(2)}) collective-permute-start(bf16[96,768]{1,0:T(8,128)(2,1)S(1)} %slice_bitcast_fusion.2), channel_id=1, source_target_pairs={{0,2},{1,3},{2,0},{3,1},{4,6},{5,7},{6,4},{7,5},{8,10},{9,11},{10,... | collective-permute-start | bytes 442376 | tf_op jit(solution)/shard_map/ppermute | solution.py:1142
  129.8 9.1 %attend_backward.5 = (f32[512,768]{1,0:T(8,128)S(1)}, bf16[2,3,512,512]{3,2,1,0:T(8,128)(2,1)S(1)}, f32[2,1,576]{2,1,0:T(1,128)S(1)}, bf16[2,4,72,768]{3,2,1,0:T(8,128)(2,1)S(1)}, bf16[2,4,72,768]{3,2,1,0:T(8,128)(2,1)S(1)}) custom-call(s32[4]{0:T(128)S(1)} %copy-done.26, bf16[512,768]{1,0:T(8,128)(2,1)S(1)} %copy-done.1, ...), custom_call_target="tpu_custom_call" | custom-call | flops 1 | bytes 1 | tf_op jit(solution)/shard_map/attend_backward/pallas_call | solution.py:389
  140.6 1.5 collective-permute-start.22
  143.3 2.0 collective-permute-start.24
  145.3 6.2 %table_products.2.refs_4_ = f32[96,512]{1,0:T(8,128)S(1)} custom-call(bf16[1,3,512,512]{3,2,1,0:T(8,128)(2,1)S(1)} %get-tuple-element.244.refs_0_, bf16[1,3,512,512]{3,2,1,0:T(8,128)(2,1)S(1)} %get-tuple-element.245.refs_1_, bf16[2,3,512,512]{3,2,1,0:T(8,128)(2,1)S(1)} %get-tuple-element.246.refs_2_, ...), custom_call_target="tpu_custom_call" | custom-call | flops 1 | bytes 1 | tf_op jit(solution)/shard_map/table_products/pallas_call | solution.py:448
  151.5 1.3 collective-permute-done.24.one
  157.7 1.8 collective-permute-start.27
  159.5 6.2 %table_products.3.refs_0_ = f32[96,512]{1,0:T(8,128)S(1)} custom-call(bf16[1,3,512,512]{3,2,1,0:T(8,128)(2,1)S(1)} %get-tuple-element.244.refs_0_, bf16[1,3,512,512]{3,2,1,0:T(8,128)(2,1)S(1)} %get-tuple-element.245.refs_1_, bf16[2,3,512,512]{3,2,1,0:T(8,128)(2,1)S(1)} %get-tuple-element.246.refs_2_, ...), custom_call_target="tpu_custom_call" | custom-call | flops 1 | bytes 1 | tf_op jit(solution)/shard_map/table_products/pallas_call | solution.py:448
  166.1 1.6 collective-permute-done.27
  168.3 1.4 sum_pairs.5
  171.6 3.4 %collective-permute-start.33 = (bf16[24,3840]{1,0:T(8,128)(2,1)S(1)}, bf16[24,3840]{1,0:T(8,128)(2,1)S(1)}, u32[]{:S(2)}, u32[]{:S(2)}) collective-permute-start(bf16[24,3840]{1,0:T(8,128)(2,1)S(1)} %slice_bitcast_fusion), channel_id=1, source_target_pairs={{0,2},{1,3},{2,0},{3,1},{4,6},{5,7},{6,4},{7,5},{8,10},{9,11},{10,... | collective-permute-start | bytes 552968 | tf_op jit(solution)/shard_map/ppermute | solution.py:1142
  176.7 2.5 %collective-permute-start.30 = (bf16[88,768]{1,0:T(8,128)(2,1)S(1)}, bf16[88,768]{1,0:T(8,128)(2,1)S(1)}, u32[]{:S(2)}, u32[]{:S(2)}) collective-permute-start(bf16[88,768]{1,0:T(8,128)(2,1)S(1)} %get-tuple-element.290), channel_id=1, source_target_pairs={{0,1},{1,0},{2,3},{3,2},{4,5},{5,4},{6,7},{7,6},{8,9},{9,8},{10,11... | collective-permute-start | bytes 405512 | tf_op jit(solution)/shard_map/ppermute | solution.py:1142
  179.7 2.0 collective-permute-start.32
  181.7 1.7 collective-permute-done.33
  183.5 1.6 join_quarters.2
  185.1 9.4 %collective-permute-done.31 = bf16[88,768]{1,0:T(8,128)(2,1)S(1)} collective-permute-done((bf16[88,768]{1,0:T(8,128)(2,1)S(1)}, bf16[88,768]{1,0:T(8,128)(2,1)S(1)}, u32[]{:S(2)}, u32[]{:S(2)}) %collective-permute-start.31) | collective-permute-done | bytes 135200 | tf_op jit(solution)/shard_map/ppermute | solution.py:1142
  195.7 1.4 collective-permute-start.36
  198.1 2.3 %collective-permute-done.38.one = bf16[24,3840]{1,0:T(8,128)(2,1)S(1)} collective-permute-done((bf16[24,3840]{1,0:T(8,128)(2,1)S(1)}, bf16[24,3840]{1,0:T(8,128)(2,1)S(1)}, u32[]{:S(2)}, u32[]{:S(2)}) %collective-permute-start.38) | collective-permute-done | bytes 184352 | tf_op jit(solution)/shard_map/ppermute | solution.py:1142
  203.6 1.5 collective-permute-start.43
  205.0 2.1 %collective-permute-done.40 = bf16[2,32,768]{2,1,0:T(8,128)(2,1)S(1)} collective-permute-done((bf16[2,32,768]{2,1,0:T(8,128)(2,1)S(1)}, bf16[2,32,768]{2,1,0:T(8,128)(2,1)S(1)}, u32[]{:S(2)}, u32[]{:S(2)}) %collective-permute-start.40) | collective-permute-done | bytes 98336 | tf_op jit(solution)/shard_map/ppermute | solution.py:1137
  210.2 1.7 join_quarters.3
  212.0 1.9 join_chips.1
  (213 shorter events, 40.2 us)
Async XLA Ops:
  3.4 17.1 %collective-permute-start = (bf16[80,768]{1,0:T(8,128)(2,1)S(1)}, bf16[80,768]{1,0:T(8,128)(2,1)S(1)}, u32[]{:S(2)}, u32[]{:S(2)}) collective-permute-start(bf16[80,768]{1,0:T(8,128)(2,1)S(1)} %pad_maximum_fusion.9), channel_id=1, source_target_pairs={{0,1},{1,0},{2,3},{3,2},{4,5},{5,4},{6,7},{7,6},{8,9},{9,8},{10,11... | collective-permute-start | bytes 368648 | tf_op jit(solution)/shard_map/ppermute | solution.py:1142
  6.5 14.0 %collective-permute-start.1 = (bf16[80,768]{1,0:T(8,128)(2,1)S(1)}, bf16[80,768]{1,0:T(8,128)(2,1)S(1)}, u32[]{:S(2)}, u32[]{:S(2)}) collective-permute-start(bf16[80,768]{1,0:T(8,128)(2,1)S(1)} %pad_maximum_fusion.9), channel_id=1, source_target_pairs={{0,2},{1,3},{2,0},{3,1},{4,6},{5,7},{6,4},{7,5},{8,10},{9,11},{10,... | collective-permute-start | bytes 368648 | tf_op jit(solution)/shard_map/ppermute | solution.py:1142
  9.1 11.4 %collective-permute-start.2 = (bf16[80,768]{1,0:T(8,128)(2,1)S(1)}, bf16[80,768]{1,0:T(8,128)(2,1)S(1)}, u32[]{:S(2)}, u32[]{:S(2)}) collective-permute-start(bf16[80,768]{1,0:T(8,128)(2,1)S(1)} %pad_maximum_fusion.9), channel_id=1, source_target_pairs={{0,3},{1,2},{2,1},{3,0},{4,7},{5,6},{6,5},{7,4},{8,11},{9,10},{10,... | collective-permute-start | bytes 368648 | tf_op jit(solution)/shard_map/ppermute | solution.py:1142
  10.5 70.9 %copy-start.24 = (s32[4]{0:T(128)}, s32[4]{0:T(128)S(1)}, u32[]{:S(2)}) copy-start(s32[4]{0:T(128)S(1)} %pad_add_fusion.place_ref) | copy-start | bytes 52
  20.6 5.9 %collective-permute-start.3 = (bf16[3,40,768]{2,1,0:T(8,128)(2,1)S(1)}, bf16[3,40,768]{2,1,0:T(8,128)(2,1)S(1)}, u32[]{:S(2)}, u32[]{:S(2)}) collective-permute-start(bf16[3,40,768]{2,1,0:T(8,128)(2,1)S(1)} %get-tuple-element.328), channel_id=1, source_target_pairs={{0,8},{4,12},{8,0},{12,4},{16,24},{20,28},{24,16},{28,20},{1,9},{5... | collective-permute-start | bytes 552968 | tf_op jit(solution)/shard_map/ppermute | solution.py:1137
  22.4 5.7 %collective-permute-start.5 = (bf16[3,32,768]{2,1,0:T(8,128)(2,1)S(1)}, bf16[3,32,768]{2,1,0:T(8,128)(2,1)S(1)}, u32[]{:S(2)}, u32[]{:S(2)}) collective-permute-start(bf16[3,32,768]{2,1,0:T(8,128)(2,1)S(1)} %get-tuple-element.324), channel_id=1, source_target_pairs={{0,16},{4,20},{8,24},{12,28},{16,0},{20,4},{24,8},{28,12},{1,17},{... | collective-permute-start | bytes 442376 | tf_op jit(solution)/shard_map/ppermute | solution.py:1137
  26.6 9.0 %collective-permute-start.4 = (bf16[2,3,40,768]{3,2,1,0:T(8,128)(2,1)S(1)}, bf16[2,3,40,768]{3,2,1,0:T(8,128)(2,1)S(1)}, u32[]{:S(2)}, u32[]{:S(2)}) collective-permute-start(bf16[2,3,40,768]{3,2,1,0:T(8,128)(2,1)S(1)} %get-tuple-element.326), channel_id=1, source_target_pairs={{0,16},{4,20},{8,24},{12,28},{16,0},{20,4},{24,8},{28,12},{1,17},{... | collective-permute-start | bytes 1105928 | tf_op jit(solution)/shard_map/ppermute | solution.py:1137
  28.3 7.4 %collective-permute-start.6 = (bf16[2,3,32,768]{3,2,1,0:T(8,128)(2,1)S(1)}, bf16[2,3,32,768]{3,2,1,0:T(8,128)(2,1)S(1)}, u32[]{:S(2)}, u32[]{:S(2)}) collective-permute-start(bf16[2,3,32,768]{3,2,1,0:T(8,128)(2,1)S(1)} %get-tuple-element.330), channel_id=1, source_target_pairs={{0,8},{4,12},{8,0},{12,4},{16,24},{20,28},{24,16},{28,20},{1,9},{5... | collective-permute-start | bytes 884744 | tf_op jit(solution)/shard_map/ppermute | solution.py:1137
  35.5 20.9 %copy-start.7 = (bf16[768,768]{1,0:T(8,128)(2,1)S(1)}, bf16[768,768]{1,0:T(8,128)(2,1)}, u32[]{:S(2)}) copy-start(bf16[768,768]{1,0:T(8,128)(2,1)} %param.23) | copy-start | bytes 3538948
  35.6 3.1 %collective-permute-start.7 = (bf16[2,2,3,40,768]{4,3,2,1,0:T(8,128)(2,1)S(1)}, bf16[2,2,3,40,768]{4,3,2,1,0:T(8,128)(2,1)S(1)}, u32[]{:S(2)}, u32[]{:S(2)}) collective-permute-start(bf16[2,2,3,40,768]{4,3,2,1,0:T(8,128)(2,1)S(1)} %pad_maximum_fusion.refs_0_), channel_id=1, source_target_pairs={{0,4},{4,0},{8,12},{12,8},{16,20},{20,16},{24,28},{28,24},{1,5},{5... | collective-permute-start | bytes 2211848 | tf_op jit(solution)/shard_map/ppermute | solution.py:1137
  35.8 3.0 %collective-permute-start.8 = (bf16[2,2,3,32,768]{4,3,2,1,0:T(8,128)(2,1)S(1)}, bf16[2,2,3,32,768]{4,3,2,1,0:T(8,128)(2,1)S(1)}, u32[]{:S(2)}, u32[]{:S(2)}) collective-permute-start(bf16[2,2,3,32,768]{4,3,2,1,0:T(8,128)(2,1)S(1)} %pad_maximum_fusion.1.refs_1_), channel_id=1, source_target_pairs={{0,4},{4,0},{8,12},{12,8},{16,20},{20,16},{24,28},{28,24},{1,5},{5... | collective-permute-start | bytes 1769480 | tf_op jit(solution)/shard_map/ppermute | solution.py:1137
  76.9 4.6 %collective-permute-start.9 = (bf16[4,384,768]{2,1,0:T(8,128)(2,1)S(1)}, bf16[4,384,768]{2,1,0:T(8,128)(2,1)S(1)}, u32[]{:S(2)}, u32[]{:S(2)}) collective-permute-start(bf16[4,384,768]{2,1,0:T(8,128)(2,1)S(1)} %bitcast.76), channel_id=1, source_target_pairs={{0,4},{4,0},{8,12},{12,8},{16,20},{20,16},{24,28},{28,24},{1,5},{5... | collective-permute-start | bytes 7077896 | tf_op jit(solution)/shard_map/ppermute | solution.py:1137
  84.2 19.3 %collective-permute-start.10 = (bf16[2,192,768]{2,1,0:T(8,128)(2,1)S(1)}, bf16[2,192,768]{2,1,0:T(8,128)(2,1)S(1)}, u32[]{:S(2)}, u32[]{:S(2)}) collective-permute-start(bf16[2,192,768]{2,1,0:T(8,128)(2,1)S(1)} %get-tuple-element.181), channel_id=1, source_target_pairs={{0,8},{4,12},{8,0},{12,4},{16,24},{20,28},{24,16},{28,20},{1,9},{5... | collective-permute-start | bytes 1769480 | tf_op jit(solution)/shard_map/ppermute | solution.py:1137
  85.2 18.3 %collective-permute-start.11 = (bf16[2,192,768]{2,1,0:T(8,128)(2,1)S(1)}, bf16[2,192,768]{2,1,0:T(8,128)(2,1)S(1)}, u32[]{:S(2)}, u32[]{:S(2)}) collective-permute-start(bf16[2,192,768]{2,1,0:T(8,128)(2,1)S(1)} %get-tuple-element.182), channel_id=1, source_target_pairs={{0,16},{4,20},{8,24},{12,28},{16,0},{20,4},{24,8},{28,12},{1,17},{... | collective-permute-start | bytes 1769480 | tf_op jit(solution)/shard_map/ppermute | solution.py:1137
  104.8 9.7 %collective-permute-start.12 = (bf16[4,96,3840]{2,1,0:T(8,128)(2,1)}, bf16[4,96,3840]{2,1,0:T(8,128)(2,1)S(1)}, u32[]{:S(2)}, u32[]{:S(2)}) collective-permute-start(bf16[4,96,3840]{2,1,0:T(8,128)(2,1)} %get-tuple-element.201), channel_id=1, source_target_pairs={{0,4},{4,0},{8,12},{12,8},{16,20},{20,16},{24,28},{28,24},{1,5},{5... | collective-permute-start | bytes 8847368 | tf_op jit(solution)/shard_map/ppermute | solution.py:1137
  104.9 9.4 %collective-permute-start.13 = (bf16[192,768]{1,0:T(8,128)(2,1)S(1)}, bf16[192,768]{1,0:T(8,128)(2,1)S(1)}, u32[]{:S(2)}, u32[]{:S(2)}) collective-permute-start(bf16[192,768]{1,0:T(8,128)(2,1)S(1)} %get-tuple-element.200), channel_id=1, source_target_pairs={{0,16},{4,20},{8,24},{12,28},{16,0},{20,4},{24,8},{28,12},{1,17},{... | collective-permute-start | bytes 884744 | tf_op jit(solution)/shard_map/ppermute | solution.py:1137
  105.5 9.1 %collective-permute-start.14 = (bf16[192,768]{1,0:T(8,128)(2,1)S(1)}, bf16[192,768]{1,0:T(8,128)(2,1)S(1)}, u32[]{:S(2)}, u32[]{:S(2)}) collective-permute-start(bf16[192,768]{1,0:T(8,128)(2,1)S(1)} %get-tuple-element.202), channel_id=1, source_target_pairs={{0,8},{4,12},{8,0},{12,4},{16,24},{20,28},{24,16},{28,20},{1,9},{5... | collective-permute-start | bytes 884744 | tf_op jit(solution)/shard_map/ppermute | solution.py:1137
  117.7 9.5 %collective-permute-start.15 = (bf16[1,4,72,768]{3,2,1,0:T(8,128)(2,1)S(1)}, bf16[1,4,72,768]{3,2,1,0:T(8,128)(2,1)S(1)}, u32[]{:S(2)}, u32[]{:S(2)}) collective-permute-start(bf16[1,4,72,768]{3,2,1,0:T(8,128)(2,1)S(1)} %get-tuple-element.219), channel_id=1, source_target_pairs={{0,4},{4,0},{8,12},{12,8},{16,20},{20,16},{24,28},{28,24},{1,5},{5... | collective-permute-start | bytes 1327112 | tf_op jit(solution)/shard_map/ppermute | solution.py:1137
  117.8 9.4 %collective-permute-start.16 = (bf16[2,96,768]{2,1,0:T(8,128)(2,1)S(1)}, bf16[2,96,768]{2,1,0:T(8,128)(2,1)S(1)}, u32[]{:S(2)}, u32[]{:S(2)}) collective-permute-start(bf16[2,96,768]{2,1,0:T(8,128)(2,1)S(1)} %get-tuple-element.216), channel_id=1, source_target_pairs={{0,1},{1,0},{2,3},{3,2},{4,5},{5,4},{6,7},{7,6},{8,9},{9,8},{10,11... | collective-permute-start | bytes 884744 | tf_op jit(solution)/shard_map/ppermute | solution.py:1142
  118.5 20.5 %collective-permute-start.17 = (bf16[2,48,3840]{2,1,0:T(8,128)(2,1)S(1)}, bf16[2,48,3840]{2,1,0:T(8,128)(2,1)S(1)}, u32[]{:S(2)}, u32[]{:S(2)}) collective-permute-start(bf16[2,48,3840]{2,1,0:T(8,128)(2,1)S(1)} %get-tuple-element.217), channel_id=1, source_target_pairs={{0,8},{4,12},{8,0},{12,4},{16,24},{20,28},{24,16},{28,20},{1,9},{5... | collective-permute-start | bytes 2211848 | tf_op jit(solution)/shard_map/ppermute | solution.py:1137
  119.6 19.3 %collective-permute-start.18 = (bf16[2,48,3840]{2,1,0:T(8,128)(2,1)S(1)}, bf16[2,48,3840]{2,1,0:T(8,128)(2,1)S(1)}, u32[]{:S(2)}, u32[]{:S(2)}) collective-permute-start(bf16[2,48,3840]{2,1,0:T(8,128)(2,1)S(1)} %get-tuple-element.218), channel_id=1, source_target_pairs={{0,16},{4,20},{8,24},{12,28},{16,0},{20,4},{24,8},{28,12},{1,17},{... | collective-permute-start | bytes 2211848 | tf_op jit(solution)/shard_map/ppermute | solution.py:1137
  127.3 11.7 %collective-permute-start.20 = (bf16[1,4,72,768]{3,2,1,0:T(8,128)(2,1)S(1)}, bf16[1,4,72,768]{3,2,1,0:T(8,128)(2,1)S(1)}, u32[]{:S(2)}, u32[]{:S(2)}) collective-permute-start(bf16[1,4,72,768]{3,2,1,0:T(8,128)(2,1)S(1)} %get-tuple-element.225), channel_id=1, source_target_pairs={{0,4},{4,0},{8,12},{12,8},{16,20},{20,16},{24,28},{28,24},{1,5},{5... | collective-permute-start | bytes 1327112 | tf_op jit(solution)/shard_map/ppermute | solution.py:1137
  127.4 11.6 %collective-permute-start.19 = (bf16[96,768]{1,0:T(8,128)(2,1)S(1)}, bf16[96,768]{1,0:T(8,128)(2,1)S(1)}, u32[]{:S(2)}, u32[]{:S(2)}) collective-permute-start(bf16[96,768]{1,0:T(8,128)(2,1)S(1)} %slice_bitcast_fusion.2), channel_id=1, source_target_pairs={{0,2},{1,3},{2,0},{3,1},{4,6},{5,7},{6,4},{7,5},{8,10},{9,11},{10,... | collective-permute-start | bytes 442376 | tf_op jit(solution)/shard_map/ppermute | solution.py:1142
  140.3 12.5 %collective-permute-start.21 = (bf16[2,4,72,768]{3,2,1,0:T(8,128)(2,1)S(1)}, bf16[2,4,72,768]{3,2,1,0:T(8,128)(2,1)S(1)}, u32[]{:S(2)}, u32[]{:S(2)}) collective-permute-start(bf16[2,4,72,768]{3,2,1,0:T(8,128)(2,1)S(1)} %get-tuple-element.240), channel_id=1, source_target_pairs={{0,4},{4,0},{8,12},{12,8},{16,20},{20,16},{24,28},{28,24},{1,5},{5... | collective-permute-start | bytes 2654216 | tf_op jit(solution)/shard_map/ppermute | solution.py:1137
  140.6 12.2 %collective-permute-start.22 = (bf16[48,3840]{1,0:T(8,128)(2,1)S(1)}, bf16[48,3840]{1,0:T(8,128)(2,1)S(1)}, u32[]{:S(2)}, u32[]{:S(2)}) collective-permute-start(bf16[48,3840]{1,0:T(8,128)(2,1)S(1)} %get-tuple-element.241), channel_id=1, source_target_pairs={{0,16},{4,20},{8,24},{12,28},{16,0},{20,4},{24,8},{28,12},{1,17},{... | collective-permute-start | bytes 1105928 | tf_op jit(solution)/shard_map/ppermute | solution.py:1137
  142.1 10.7 %collective-permute-start.23 = (bf16[48,3840]{1,0:T(8,128)(2,1)S(1)}, bf16[48,3840]{1,0:T(8,128)(2,1)S(1)}, u32[]{:S(2)}, u32[]{:S(2)}) collective-permute-start(bf16[48,3840]{1,0:T(8,128)(2,1)S(1)} %get-tuple-element.242), channel_id=1, source_target_pairs={{0,8},{4,12},{8,0},{12,4},{16,24},{20,28},{24,16},{28,20},{1,9},{5... | collective-permute-start | bytes 1105928 | tf_op jit(solution)/shard_map/ppermute | solution.py:1137
  143.3 9.6 %collective-permute-start.24 = (bf16[96,768]{1,0:T(8,128)(2,1)S(1)}, bf16[96,768]{1,0:T(8,128)(2,1)S(1)}, u32[]{:S(2)}, u32[]{:S(2)}) collective-permute-start(bf16[96,768]{1,0:T(8,128)(2,1)S(1)} %fusion.1.own), channel_id=1, source_target_pairs={{0,2},{1,3},{2,0},{3,1},{4,6},{5,7},{6,4},{7,5},{8,10},{9,11},{10,... | collective-permute-start | bytes 442376 | tf_op jit(solution)/shard_map/ppermute | solution.py:1142
  156.2 11.5 %collective-permute-start.25 = (bf16[2,144,768]{2,1,0:T(8,128)(2,1)S(1)}, bf16[2,144,768]{2,1,0:T(8,128)(2,1)S(1)}, u32[]{:S(2)}, u32[]{:S(2)}) collective-permute-start(bf16[2,144,768]{2,1,0:T(8,128)(2,1)S(1)} %get-tuple-element.264), channel_id=1, source_target_pairs={{0,8},{4,12},{8,0},{12,4},{16,24},{20,28},{24,16},{28,20},{1,9},{5... | collective-permute-start | bytes 1327112 | tf_op jit(solution)/shard_map/ppermute | solution.py:1137
  157.2 11.0 %collective-permute-start.26 = (bf16[2,144,768]{2,1,0:T(8,128)(2,1)S(1)}, bf16[2,144,768]{2,1,0:T(8,128)(2,1)S(1)}, u32[]{:S(2)}, u32[]{:S(2)}) collective-permute-start(bf16[2,144,768]{2,1,0:T(8,128)(2,1)S(1)} %get-tuple-element.265), channel_id=1, source_target_pairs={{0,16},{4,20},{8,24},{12,28},{16,0},{20,4},{24,8},{28,12},{1,17},{... | collective-permute-start | bytes 1327112 | tf_op jit(solution)/shard_map/ppermute | solution.py:1137
  157.7 10.0 %collective-permute-start.27 = (bf16[2,24,3840]{2,1,0:T(8,128)(2,1)S(1)}, bf16[2,24,3840]{2,1,0:T(8,128)(2,1)S(1)}, u32[]{:S(2)}, u32[]{:S(2)}) collective-permute-start(bf16[2,24,3840]{2,1,0:T(8,128)(2,1)S(1)} %get-tuple-element.266), channel_id=1, source_target_pairs={{0,1},{1,0},{2,3},{3,2},{4,5},{5,4},{6,7},{7,6},{8,9},{9,8},{10,11... | collective-permute-start | bytes 1105928 | tf_op jit(solution)/shard_map/ppermute | solution.py:1142
  165.7 16.0 %collective-permute-start.34 = (bf16[2,96,768]{2,1,0:T(8,128)(2,1)S(1)}, bf16[2,96,768]{2,1,0:T(8,128)(2,1)S(1)}, u32[]{:S(2)}, u32[]{:S(2)}) collective-permute-start(bf16[2,96,768]{2,1,0:T(8,128)(2,1)S(1)} %pad_maximum_fusion.6), channel_id=1, source_target_pairs={{0,1},{1,0},{2,3},{3,2},{4,5},{5,4},{6,7},{7,6},{8,9},{9,8},{10,11... | collective-permute-start | bytes 884744 | tf_op jit(solution)/shard_map/ppermute | solution.py:1142
  169.7 6.4 %collective-permute-start.28 = (bf16[144,768]{1,0:T(8,128)(2,1)S(1)}, bf16[144,768]{1,0:T(8,128)(2,1)S(1)}, u32[]{:S(2)}, u32[]{:S(2)}) collective-permute-start(bf16[144,768]{1,0:T(8,128)(2,1)S(1)} %get-tuple-element.276), channel_id=1, source_target_pairs={{0,16},{4,20},{8,24},{12,28},{16,0},{20,4},{24,8},{28,12},{1,17},{... | collective-permute-start | bytes 663560 | tf_op jit(solution)/shard_map/ppermute | solution.py:1137
  170.7 5.9 %collective-permute-start.29 = (bf16[144,768]{1,0:T(8,128)(2,1)S(1)}, bf16[144,768]{1,0:T(8,128)(2,1)S(1)}, u32[]{:S(2)}, u32[]{:S(2)}) collective-permute-start(bf16[144,768]{1,0:T(8,128)(2,1)S(1)} %get-tuple-element.277), channel_id=1, source_target_pairs={{0,8},{4,12},{8,0},{12,4},{16,24},{20,28},{24,16},{28,20},{1,9},{5... | collective-permute-start | bytes 663560 | tf_op jit(solution)/shard_map/ppermute | solution.py:1137
  171.6 11.9 %collective-permute-start.33 = (bf16[24,3840]{1,0:T(8,128)(2,1)S(1)}, bf16[24,3840]{1,0:T(8,128)(2,1)S(1)}, u32[]{:S(2)}, u32[]{:S(2)}) collective-permute-start(bf16[24,3840]{1,0:T(8,128)(2,1)S(1)} %slice_bitcast_fusion), channel_id=1, source_target_pairs={{0,2},{1,3},{2,0},{3,1},{4,6},{5,7},{6,4},{7,5},{8,10},{9,11},{10,... | collective-permute-start | bytes 552968 | tf_op jit(solution)/shard_map/ppermute | solution.py:1142
  176.7 8.4 %collective-permute-start.30 = (bf16[88,768]{1,0:T(8,128)(2,1)S(1)}, bf16[88,768]{1,0:T(8,128)(2,1)S(1)}, u32[]{:S(2)}, u32[]{:S(2)}) collective-permute-start(bf16[88,768]{1,0:T(8,128)(2,1)S(1)} %get-tuple-element.290), channel_id=1, source_target_pairs={{0,1},{1,0},{2,3},{3,2},{4,5},{5,4},{6,7},{7,6},{8,9},{9,8},{10,11... | collective-permute-start | bytes 405512 | tf_op jit(solution)/shard_map/ppermute | solution.py:1142
  179.3 15.2 %collective-permute-start.31 = (bf16[88,768]{1,0:T(8,128)(2,1)S(1)}, bf16[88,768]{1,0:T(8,128)(2,1)S(1)}, u32[]{:S(2)}, u32[]{:S(2)}) collective-permute-start(bf16[88,768]{1,0:T(8,128)(2,1)S(1)} %get-tuple-element.291), channel_id=1, source_target_pairs={{0,2},{1,3},{2,0},{3,1},{4,6},{5,7},{6,4},{7,5},{8,10},{9,11},{10,... | collective-permute-start | bytes 405512 | tf_op jit(solution)/shard_map/ppermute | solution.py:1142
  179.7 14.8 %collective-permute-start.32 = (bf16[88,768]{1,0:T(8,128)(2,1)S(1)}, bf16[88,768]{1,0:T(8,128)(2,1)S(1)}, u32[]{:S(2)}, u32[]{:S(2)}) collective-permute-start(bf16[88,768]{1,0:T(8,128)(2,1)S(1)} %get-tuple-element.292), channel_id=1, source_target_pairs={{0,3},{1,2},{2,1},{3,0},{4,7},{5,6},{6,5},{7,4},{8,11},{9,10},{10,... | collective-permute-start | bytes 405512 | tf_op jit(solution)/shard_map/ppermute | solution.py:1142
  185.1 15.3 %collective-permute-start.38 = (bf16[24,3840]{1,0:T(8,128)(2,1)S(1)}, bf16[24,3840]{1,0:T(8,128)(2,1)S(1)}, u32[]{:S(2)}, u32[]{:S(2)}) collective-permute-start(bf16[24,3840]{1,0:T(8,128)(2,1)S(1)} %fusion.own), channel_id=1, source_target_pairs={{0,2},{1,3},{2,0},{3,1},{4,6},{5,7},{6,4},{7,5},{8,10},{9,11},{10,... | collective-permute-start | bytes 552968 | tf_op jit(solution)/shard_map/ppermute | solution.py:1142
  194.6 7.0 %collective-permute-start.35 = (bf16[40,768]{1,0:T(8,128)(2,1)S(1)}, bf16[40,768]{1,0:T(8,128)(2,1)S(1)}, u32[]{:S(2)}, u32[]{:S(2)}) collective-permute-start(bf16[40,768]{1,0:T(8,128)(2,1)S(1)} %get-tuple-element.336), channel_id=1, source_target_pairs={{0,8},{4,12},{8,0},{12,4},{16,24},{20,28},{24,16},{28,20},{1,9},{5... | collective-permute-start | bytes 184328 | tf_op jit(solution)/shard_map/ppermute | solution.py:1137
  195.7 6.0 %collective-permute-start.36 = (bf16[32,768]{1,0:T(8,128)(2,1)S(1)}, bf16[32,768]{1,0:T(8,128)(2,1)S(1)}, u32[]{:S(2)}, u32[]{:S(2)}) collective-permute-start(bf16[32,768]{1,0:T(8,128)(2,1)S(1)} %get-tuple-element.334), channel_id=1, source_target_pairs={{0,16},{4,20},{8,24},{12,28},{16,0},{20,4},{24,8},{28,12},{1,17},{... | collective-permute-start | bytes 147464 | tf_op jit(solution)/shard_map/ppermute | solution.py:1137
  197.1 4.6 %collective-permute-start.37 = (bf16[16,768]{1,0:T(8,128)(2,1)S(1)}, bf16[16,768]{1,0:T(8,128)(2,1)S(1)}, u32[]{:S(2)}, u32[]{:S(2)}) collective-permute-start(bf16[16,768]{1,0:T(8,128)(2,1)S(1)} %add_convert_fusion.5), channel_id=1, source_target_pairs={{0,8},{4,12},{8,0},{12,4},{16,24},{20,28},{24,16},{28,20},{1,9},{5... | collective-permute-start | bytes 73736 | tf_op jit(solution)/shard_map/ppermute | solution.py:1137
  200.5 9.7 %collective-permute-start.45 = (bf16[2,24,3840]{2,1,0:T(8,128)(2,1)S(1)}, bf16[2,24,3840]{2,1,0:T(8,128)(2,1)S(1)}, u32[]{:S(2)}, u32[]{:S(2)}) collective-permute-start(bf16[2,24,3840]{2,1,0:T(8,128)(2,1)S(1)} %pad_maximum_fusion.4), channel_id=1, source_target_pairs={{0,1},{1,0},{2,3},{3,2},{4,5},{5,4},{6,7},{7,6},{8,9},{9,8},{10,11... | collective-permute-start | bytes 1105928 | tf_op jit(solution)/shard_map/ppermute | solution.py:1142
  201.7 5.6 %collective-permute-start.39 = (bf16[2,40,768]{2,1,0:T(8,128)(2,1)S(1)}, bf16[2,40,768]{2,1,0:T(8,128)(2,1)S(1)}, u32[]{:S(2)}, u32[]{:S(2)}) collective-permute-start(bf16[2,40,768]{2,1,0:T(8,128)(2,1)S(1)} %get-tuple-element.332), channel_id=1, source_target_pairs={{0,16},{4,20},{8,24},{12,28},{16,0},{20,4},{24,8},{28,12},{1,17},{... | collective-permute-start | bytes 368648 | tf_op jit(solution)/shard_map/ppermute | solution.py:1137
  202.5 4.7 %collective-permute-start.40 = (bf16[2,32,768]{2,1,0:T(8,128)(2,1)S(1)}, bf16[2,32,768]{2,1,0:T(8,128)(2,1)S(1)}, u32[]{:S(2)}, u32[]{:S(2)}) collective-permute-start(bf16[2,32,768]{2,1,0:T(8,128)(2,1)S(1)} %get-tuple-element.338), channel_id=1, source_target_pairs={{0,8},{4,12},{8,0},{12,4},{16,24},{20,28},{24,16},{28,20},{1,9},{5... | collective-permute-start | bytes 294920 | tf_op jit(solution)/shard_map/ppermute | solution.py:1137
  203.6 4.3 %collective-permute-start.43 = (bf16[16,768]{1,0:T(8,128)(2,1)S(1)}, bf16[16,768]{1,0:T(8,128)(2,1)S(1)}, u32[]{:S(2)}, u32[]{:S(2)}) collective-permute-start(bf16[16,768]{1,0:T(8,128)(2,1)S(1)} %add_convert_fusion.4), channel_id=1, source_target_pairs={{0,16},{4,20},{8,24},{12,28},{16,0},{20,4},{24,8},{28,12},{1,17},{... | collective-permute-start | bytes 73736 | tf_op jit(solution)/shard_map/ppermute | solution.py:1137
  207.2 4.7 %collective-permute-start.42 = (bf16[2,2,32,768]{3,2,1,0:T(8,128)(2,1)S(1)}, bf16[2,2,32,768]{3,2,1,0:T(8,128)(2,1)S(1)}, u32[]{:S(2)}, u32[]{:S(2)}) collective-permute-start(bf16[2,2,32,768]{3,2,1,0:T(8,128)(2,1)S(1)} %pad_maximum_fusion.8.mine_b), channel_id=1, source_target_pairs={{0,4},{4,0},{8,12},{12,8},{16,20},{20,16},{24,28},{28,24},{1,5},{5... | collective-permute-start | bytes 589832 | tf_op jit(solution)/shard_map/ppermute | solution.py:1137
  207.3 4.6 %collective-permute-start.41 = (bf16[2,2,40,768]{3,2,1,0:T(8,128)(2,1)S(1)}, bf16[2,2,40,768]{3,2,1,0:T(8,128)(2,1)S(1)}, u32[]{:S(2)}, u32[]{:S(2)}) collective-permute-start(bf16[2,2,40,768]{3,2,1,0:T(8,128)(2,1)S(1)} %pad_maximum_fusion.7.mine_a), channel_id=1, source_target_pairs={{0,4},{4,0},{8,12},{12,8},{16,20},{20,16},{24,28},{28,24},{1,5},{5... | collective-permute-start | bytes 737288 | tf_op jit(solution)/shard_map/ppermute | solution.py:1137
  207.9 4.0 %collective-permute-start.44 = (bf16[16,768]{1,0:T(8,128)(2,1)S(1)}, bf16[16,768]{1,0:T(8,128)(2,1)S(1)}, u32[]{:S(2)}, u32[]{:S(2)}) collective-permute-start(bf16[16,768]{1,0:T(8,128)(2,1)S(1)} %add_convert_fusion.3.ends_ref), channel_id=1, source_target_pairs={{0,4},{4,0},{8,12},{12,8},{16,20},{20,16},{24,28},{28,24},{1,5},{5... | collective-permute-start | bytes 73736 | tf_op jit(solution)/shard_map/ppermute | solution.py:1137
  (47 other events, 372.3 us)
where the time goes:
time: 215 us; the launch traced here: 214 us
  Pallas kernels  108 us (50%)
  starting transfers between devices  50.6 us (24%)
  waiting for transfers between devices  38.9 us (18%)
  local copies, waits for them, and re-layouts  13 us (6%)
  other arithmetic  2.4 us (1%)
    ppermute x32, starting transfers between devices, swap(): lax.ppermute(array, 'docs', [(i, i ^ 1 << bit) for i in range(count)])  28.2 us
    ppermute x14, starting transfers between devices, away(): lax.ppermute(array, 'heads', [(i, i ^ distance) for i in range(count)])  22.4 us
    ppermute x32, waiting for transfers between devices, swap(): lax.ppermute(array, 'docs', [(i, i ^ 1 << bit) for i in range(count)])  19.9 us
    ppermute x14, waiting for transfers between devices, away(): lax.ppermute(array, 'heads', [(i, i ^ distance) for i in range(count)])  19 us
    pallas_call x3, Pallas kernels, attend_backward(): pl.pallas_call(functools.partial(backward_kernel, bool(halves)), grid_spe...  18.6 us
    pallas_call x2, Pallas kernels, attend_forward(): pl.pallas_call(functools.partial(forward_kernel, gathered), grid_spec=plt...  18.2 us
    pallas_call x1, Pallas kernels, feed_up(): pl.pallas_call(up_kernel, grid_spec=pltpu.PrefetchScalarGridSpec(num_scal...  17.6 us
    pallas_call x1, Pallas kernels, feed_down(): pl.pallas_call(functools.partial(down_kernel, bool(halves)), grid_spec=pl...  16.1 us
  transfers between devices with their start and end apart: 46, of which 16 were waited for; matrix products, arithmetic and copies ran while one was open for 1% of the time, Pallas kernels for 28%

commit v1 on v0

--- a/solution.py
+++ b/solution.py
@@ -1011,6 +1011,39 @@
     )(place, a_kept, a_got, b_kept, b_got)
 
 
+def halves_kernel(place_ref, a_kept, a_got, b_kept, b_got, *refs):
+    outs, sum_sc = refs[:-1], refs[-1]
+    cut = a_kept.shape[0]
+    sum_sc[0:cut, :] = a_kept[...].astype(F32) + a_got[...].astype(F32)
+    sum_sc[cut:, :] = b_kept[...].astype(F32) + b_got[...].astype(F32)
+    size, wide = outs[0].shape[1:]
+    for out, lanes, first, second in (
+        (outs[0], slice(0, wide), 1, 3),
+        (outs[1], slice(0, wide), 0, 2),
+        (outs[2], slice(wide, 2 * wide), 2, 3),
+        (outs[3], slice(wide, 2 * wide), 0, 1),
+    ):
+        for n, s in ((0, first), (1, second)):
+            at = pl.multiple_of((place_ref[0] ^ s) * size, 8)
+            out[n] = sum_sc[pl.ds(at, size), lanes].astype(BF)
+
+
+def cut_halves(place, a_kept, a_got, b_kept, b_got):
+    vmem = pl.BlockSpec(memory_space=pltpu.VMEM)
+    columns = a_kept.shape[-1]
+    height = a_kept.shape[0] + b_kept.shape[0]
+    return pl.pallas_call(
+        halves_kernel,
+        in_specs=[pl.BlockSpec(memory_space=pltpu.SMEM)] + [vmem] * 4,
+        out_specs=[vmem] * 4,
+        out_shape=[shaped(BF, 2, height // 4, columns // 2)] * 4,
+        scratch_shapes=[pltpu.VMEM((height, columns), F32)],
+        name="cut_halves",
+        compiler_params=limit(8),
+        cost_estimate=HINT,
+    )(place, a_kept, a_got, b_kept, b_got)
+
+
 def last_kernel(a_kept, a_got, b_kept, b_got, short_ref, *outs):
     size = outs[0].shape[0] - 16
     many = short_ref.shape[0] // 8 * 8
@@ -1039,28 +1072,39 @@
     )(a_kept, a_got, b_kept, b_got, short)
 
 
-def join_kernel(place_ref, own, one, two, *outs):
-    size = own.shape[0]
+def join_kernel(orders, place_ref, *refs):
+    inputs, outs = refs[: 3 * len(orders)], refs[3 * len(orders) :]
+    size, wide = inputs[0].shape
     start = 0
     for out in outs:
-        lanes = slice(start, start + out.shape[1])
-        for s, piece in ((0, own[:, lanes]), (2, one[:, lanes]), (1, two[0, :, lanes]), (3, two[1, :, lanes])):
-            at = pl.multiple_of((place_ref[0] ^ s) * size, 8)
-            out[pl.ds(at, size), :] = piece.astype(F32)
+        done = 0
+        while done < out.shape[1]:
+            half, low = divmod(start + done, wide)
+            many = min(wide - low, out.shape[1] - done)
+            own, one, two = inputs[3 * half : 3 * half + 3]
+            lanes = slice(low, low + many)
+            near, far, farther = orders[half]
+            for s, piece in (
+                (0, own[:, lanes]), (near, one[:, lanes]), (far, two[0, :, lanes]),
+                (farther, two[1, :, lanes]),
+            ):
+                at = pl.multiple_of((place_ref[0] ^ s) * size, 8)
+                out[pl.ds(at, size), done : done + many] = piece.astype(F32)
+            done += many
         start += out.shape[1]
 
 
-def join_quarters(place, own, one, two, widths):
+def join_quarters(place, parts, orders, widths):
     vmem = pl.BlockSpec(memory_space=pltpu.VMEM)
     return pl.pallas_call(
-        join_kernel,
-        in_specs=[pl.BlockSpec(memory_space=pltpu.SMEM)] + [vmem] * 3,
+        functools.partial(join_kernel, orders),
+        in_specs=[pl.BlockSpec(memory_space=pltpu.SMEM)] + [vmem] * (3 * len(parts)),
         out_specs=[vmem] * len(widths),
-        out_shape=[shaped(F32, 4 * own.shape[0], width) for width in widths],
+        out_shape=[shaped(F32, 4 * parts[0][0].shape[0], width) for width in widths],
         name="join_quarters",
         compiler_params=limit(8),
         cost_estimate=HINT,
-    )(place, own, one, two)
+    )(place, *[item for part in parts for item in part])
 
 
 def chips_join_kernel(place_ref, mine_a, mine_b, got_a, got_b, ends_ref, got_ends, out_ref, *outs):
@@ -1285,7 +1329,7 @@
             place,
             [(dense_kept[None], dense_got[None])],
             (("x", ((0, 0, half),)), ("y", ((0, half, share),))),
-            (units + width) // 3,
+            FC,
         )
         back_sent, back = cut_quarters(
             place, back[1], back_got[0], back[3], back_got[1], width // 2
@@ -1311,7 +1355,7 @@
         dense_got, back_got, one_got = tie((dense_got, back_got, one_got), dx)
         dense = list(
             sum_pairs(
-                place, dense[1], dense_got[0], dense[3], dense_got[1], (units + width) // 2
+                place, dense[1], dense_got[0], dense[3], dense_got[1], (units + width) // 3
             )
         )
         back = total_of(back[0], back_got)
@@ -1326,9 +1370,8 @@
         )
 
         two_got, dense_got, back_one = tie((two_got, dense_got, back_one), acc)
-        dense_sent, dense = cut_quarters(
-            place, dense[1], dense_got[0], dense[3], dense_got[1], (units + width) // 2
-        )
+        dense = cut_halves(place, dense[1], dense_got[0], dense[3], dense_got[1])
+        dense_sent, dense = [dense[0], dense[2]], [dense[1], dense[3]]
         own_got, one_got, two_got = tie((own_got, one_got, two_got), dense_sent)
         last_a = sum_chips(
             place, [(own_kept, own_got), (one_kept, one_got)],
@@ -1339,7 +1382,7 @@
         last_a, last_b, dense_sent, back_two = tie((last_a, last_b, dense_sent, back_two))
         last_a_got = swap(last_a[0], 1)
         last_b_got = swap(last_b[0], 2)
-        dense_got = away(dense_sent, 1)
+        dense_got = [away(dense_sent[0], 1), away(dense_sent[1], 2)]
         back_two = away(back_two, 1)
         acc = table_products(
             scores, tie(bucket, last_b[0], last_a[0], dense_sent), acc, 1
@@ -1348,24 +1391,25 @@
 
         last_a_got, last_b_got, dense_got = tie((last_a_got, last_b_got, dense_got), acc)
         last = list(sum_pairs(place, last_a[1], last_a_got, last_b[1], last_b_got, width // 2))
-        dense = total_of(dense, dense_got)
+        dense = [total_of(*pair) for pair in zip(dense, dense_got)]
         last[0], last[2], dense = tie((last[0], last[2], dense), last[1])
         last_got = [swap(last[0], 2), swap(last[2], 1)]
-        dense_got = away(dense[1], 2)
-        last_got, short = tie((last_got, short), dense)
+        dense_got = [away(dense[0][1], 2), away(dense[1][1], 1)]
+        last_got, short = tie((last_got, short), dense, back_two)
         last = cut_last(last[1], last_got[0], last[3], last_got[1], short)
         last_got = [away(last[s], s) for s in range(1, groups)]
         dense_got, back_two = tie((dense_got, back_two), last[0])
-        dense = total_of(dense[0], dense_got)
-        dense_one = away(dense, 2)
-        (out_back,) = join_quarters(place, back, back_one, back_two, (width,))
+        dense = [total_of(item[0], got) for item, got in zip(dense, dense_got)]
+        dense_one = [away(dense[0], 2), away(dense[1], 1)]
+        (out_back,) = join_quarters(place, [(back, back_one, back_two)], ((2, 1, 3),), (width,))
         last_got = tie(last_got, dense, out_back)
         quarter = total_of(last[0][:small], *[item[:small] for item in last_got])
         ends = tree([item[small:].astype(F32) for item in [last[0]] + last_got]).astype(BF)
         first, second = quarter[:cut], quarter[cut:]
         got = [swap(first, 1), swap(second, 2), swap(ends, 1)]
         dense_one = tie(dense_one, first, second)
-        dense_two = away(jnp.stack([dense, dense_one]), 1)
+        dense_two = [jnp.stack(pair) for pair in zip(dense, dense_one)]
+        dense_two = [away(dense_two[0], 1), away(dense_two[1], 2)]
         got = tie(got, dense_one)
         first, second = jnp.stack([first, got[0]]), jnp.stack([second, got[1]])
         ends = total_of(ends, got[2])
@@ -1374,7 +1418,9 @@
         first, second = jnp.stack([first, got[0]]), jnp.stack([second, got[1]])
         ends = total_of(ends, got[2])
         got = [swap(first, 0), swap(second, 0), swap(ends, 0)]
-        out_in, out_out = join_quarters(place, dense, dense_one, dense_two, (units, width))
+        out_in, out_out = join_quarters(
+            place, list(zip(dense, dense_one, dense_two)), ((2, 1, 3), (1, 2, 3)), (units, width)
+        )
         got = tie(got, out_in)
         full, grad_bias, grad_tables, grad_inner, *vectors = join_chips(
             place, first, second, got[0], got[1], ends, got[2], units, own, heads, buckets

time: 215 us -> 211 us (0.981)
  waiting for transfers between devices: 38.9 us -> 29 us
  starting transfers between devices: 50.6 us -> 56.6 us
    ppermute x14 -> x18, waiting for transfers between devices: 19 us -> 8.85 us  [away(): lax.ppermute(array, 'heads', [(i, i ^ distance) for i in range(count)])]
    ppermute x14 -> x18, starting transfers between devices: 22.4 us -> 28.2 us  [away(): lax.ppermute(array, 'heads', [(i, i ^ distance) for i in range(count)])]
    unnamed x98 -> x88, local copies, waits for them, and re-layouts: 10.1 us -> 10.1 us
  transfers between devices with their start and end apart: 46 -> 50, of which waited for: 16 -> 13; matrix products, arithmetic and copies ran while one was open for 1% -> 1% of each run, Pallas kernels for 28% -> 29%
where the time goes in v1:
time: 211 us; the launch traced here: 210 us
  Pallas kernels  108 us (51%)
  starting transfers between devices  56.6 us (27%)
  waiting for transfers between devices  29 us (14%)
  local copies, waits for them, and re-layouts  12.9 us (6%)
  other arithmetic  2.42 us (1%)
    ppermute x32, starting transfers between devices, swap(): lax.ppermute(array, 'docs', [(i, i ^ 1 << bit) for i in range(count)])  28.4 us
    ppermute x18, starting transfers between devices, away(): lax.ppermute(array, 'heads', [(i, i ^ distance) for i in range(count)])  28.2 us
    ppermute x32, waiting for transfers between devices, swap(): lax.ppermute(array, 'docs', [(i, i ^ 1 << bit) for i in range(count)])  20.2 us
    pallas_call x3, Pallas kernels, attend_backward(): pl.pallas_call(functools.partial(backward_kernel, bool(halves)), grid_spe...  18.6 us
    pallas_call x2, Pallas kernels, attend_forward(): pl.pallas_call(functools.partial(forward_kernel, gathered), grid_spec=plt...  18.2 us
    pallas_call x1, Pallas kernels, feed_up(): pl.pallas_call(up_kernel, grid_spec=pltpu.PrefetchScalarGridSpec(num_scal...  17.6 us
    pallas_call x1, Pallas kernels, feed_down(): pl.pallas_call(functools.partial(down_kernel, bool(halves)), grid_spec=pl...  16.1 us
    pallas_call x2, Pallas kernels, table_products(): pl.pallas_call(functools.partial(table_kernel, skip), grid=(steps,), in_s...  12.4 us
  transfers between devices with their start and end apart: 50, of which 13 were waited for; matrix products, arithmetic and copies ran while one was open for 1% of the time, Pallas kernels for 29%

profile of v1, /device:TPU:0, one launch (start us, length us, event | category | flops | bytes accessed | tf_op | source)
XLA Modules:
  0.0 210.3 jit_solution(9980000499231028266)
XLA Ops:
  3.4 3.1 %collective-permute-start = (bf16[80,768]{1,0:T(8,128)(2,1)S(1)}, bf16[80,768]{1,0:T(8,128)(2,1)S(1)}, u32[]{:S(2)}, u32[]{:S(2)}) collective-permute-start(bf16[80,768]{1,0:T(8,128)(2,1)S(1)} %pad_maximum_fusion.10), channel_id=1, source_target_pairs={{0,1},{1,0},{2,3},{3,2},{4,5},{5,4},{6,7},{7,6},{8,9},{9,8},{10,11... | collective-permute-start | bytes 368648 | tf_op jit(solution)/shard_map/ppermute | solution.py:1186
  6.5 2.6 %collective-permute-start.1 = (bf16[80,768]{1,0:T(8,128)(2,1)S(1)}, bf16[80,768]{1,0:T(8,128)(2,1)S(1)}, u32[]{:S(2)}, u32[]{:S(2)}) collective-permute-start(bf16[80,768]{1,0:T(8,128)(2,1)S(1)} %pad_maximum_fusion.10), channel_id=1, source_target_pairs={{0,2},{1,3},{2,0},{3,1},{4,6},{5,7},{6,4},{7,5},{8,10},{9,11},{10,... | collective-permute-start | bytes 368648 | tf_op jit(solution)/shard_map/ppermute | solution.py:1186
  10.5 2.9 %buckets.1 = (s32[512,512]{1,0:T(8,128)S(1)}, s32[5,128,128]{2,1,0:T(8,128)S(1)}) custom-call(s32[4]{0:T(128)S(1)} %pad_add_fusion.place_ref, s32[4]{0:T(128)S(1)} %copy-done.37, s32[2,2048]{1,0:T(2,128)S(1)} %copy-done.35), custom_call_target="tpu_custom_call" | custom-call | flops 1 | bytes 1 | tf_op jit(solution)/shard_map/buckets/pallas_call | solution.py:96
  15.8 4.6 %attend_forward.2 = (bf16[1,512,192]{2,1,0:T(8,128)(2,1)S(1)}, bf16[1,192,512]{2,1,0:T(8,128)(2,1)S(1)}, bf16[1,3,512,512]{3,2,1,0:T(8,128)(2,1)S(1)}, bf16[1,576,512]{2,1,0:T(8,128)(2,1)S(1)}, f32[1,8,512]{2,1,0:T(8,128)S(1)}) custom-call(s32[4]{0:T(128)S(1)} %pad_add_fusion.place_ref, bf16[512,768]{1,0:T(8,128)(2,1)S(1)} %copy-done, ...), custom_call_target="tpu_custom_call" | custom-call | flops 1 | bytes 1 | tf_op jit(solution)/shard_map/attend_forward/pallas_call | solution.py:274
  20.6 1.8 collective-permute-start.3
  22.4 1.6 collective-permute-start.5
  24.0 2.5 %collective-permute-done.3 = bf16[3,40,768]{2,1,0:T(8,128)(2,1)S(1)} collective-permute-done((bf16[3,40,768]{2,1,0:T(8,128)(2,1)S(1)}, bf16[3,40,768]{2,1,0:T(8,128)(2,1)S(1)}, u32[]{:S(2)}, u32[]{:S(2)}) %collective-permute-start.3) | collective-permute-done | bytes 184352 | tf_op jit(solution)/shard_map/ppermute | solution.py:1181
  26.6 1.6 collective-permute-start.4
  28.3 1.6 collective-permute-start.6
  29.8 5.7 %collective-permute-done.4 = bf16[2,3,40,768]{3,2,1,0:T(8,128)(2,1)S(1)} collective-permute-done((bf16[2,3,40,768]{3,2,1,0:T(8,128)(2,1)S(1)}, bf16[2,3,40,768]{3,2,1,0:T(8,128)(2,1)S(1)}, u32[]{:S(2)}, u32[]{:S(2)}) %collective-permute-start.4) | collective-permute-done | bytes 368672 | tf_op jit(solution)/shard_map/ppermute | solution.py:1181
  36.5 2.2 %collective-permute-done.8.refs_3_ = bf16[2,2,3,32,768]{4,3,2,1,0:T(8,128)(2,1)S(1)} collective-permute-done((bf16[2,2,3,32,768]{4,3,2,1,0:T(8,128)(2,1)S(1)}, bf16[2,2,3,32,768]{4,3,2,1,0:T(8,128)(2,1)S(1)}, u32[]{:S(2)}, u32[]{:S(2)}) %collective-permute-start.8) | collective-permute-done | bytes 589856 | tf_op jit(solution)/shard_map/ppermute | solution.py:1181
  38.7 13.5 %attend_forward.3 = (bf16[3,576,768]{2,1,0:T(8,128)(2,1)S(1)}, bf16[3,512,192]{2,1,0:T(8,128)(2,1)S(1)}, bf16[3,192,512]{2,1,0:T(8,128)(2,1)S(1)}, bf16[3,3,512,...) custom-call(s32[4]{0:T(128)S(1)} %pad_add_fusion.place_ref, ...), custom_call_target="tpu_custom_call" | custom-call | flops 1 | bytes 1 | tf_op jit(solution)/shard_map/attend_forward/pallas_call | solution.py:274
  52.3 1.5 copy-done.3
  56.5 17.6 %feed_up.1 = (bf16[512,768]{1,0:T(8,128)(2,1)}, f32[512,768]{1,0:T(8,128)S(1)}, bf16[512,768]{1,0:T(8,128)(2,1)S(1)}, bf16[3072,512]{1,0:T(8,128)(2,1)S(1)}, bf1...) custom-call(s32[4]{0:T(128)S(1)} %pad_add_fusion.place_ref, ...), custom_call_target="tpu_custom_call" | custom-call | flops 1 | bytes 1 | tf_op jit(solution)/shard_map/feed_up/pallas_call | solution.py:624
  74.1 2.6 %back_weights.1 = bf16[1536,768]{1,0:T(8,128)(2,1)S(1)} custom-call(s32[4]{0:T(128)S(1)} %pad_add_fusion.place_ref, bf16[3072,512]{1,0:T(8,128)(2,1)S(1)} %get-tuple-element.188.left_ref, bf16[512,768]{1,0:T(8,128)(2,1)S(1)} %get-tuple-element.191.right_ref.branch_ref), custom_call_target="tpu_custom_call" | custom-call | flops 1 | bytes 1 | tf_op jit(solution)/shard_map/back_weights/pallas_call | solution.py:840
  77.1 4.4 %collective-permute-done.9.got_ref = bf16[4,384,768]{2,1,0:T(8,128)(2,1)S(1)} collective-permute-done((bf16[4,384,768]{2,1,0:T(8,128)(2,1)S(1)}, bf16[4,384,768]{2,1,0:T(8,128)(2,1)S(1)}, u32[]{:S(2)}, u32[]{:S(2)}) %collective-permute-start.9) | collective-permute-done | bytes 2359328 | tf_op jit(solution)/shard_map/ppermute | solution.py:1181
  81.5 2.7 %kept_weights.1 = (bf16[2,192,768]{2,1,0:T(8,128)(2,1)S(1)}, bf16[2,192,768]{2,1,0:T(8,128)(2,1)S(1)}, bf16[2,192,768]{2,1,0:T(8,128)(2,1)S(1)}, bf16[2,192,768]{2,1,0:T(8,128)(2,1)S(1)}) custom-call(s32[4]{0:T(128)S(1)} %pad_add_fusion.place_ref, bf16[3072,512]{1,0:T(8,128)(2,1)S(1)} %get-tuple-element.188.left_ref, ...), custom_call_target="tpu_custom_call" | custom-call | flops 1 | bytes 1 | tf_op jit(solution)/shard_map/kept_weights/pallas_call | solution.py:884
  85.2 1.5 collective-permute-start.11
  87.4 16.1 %feed_down.1 = (f32[8,3072]{1,0:T(8,128)S(1)}, f32[512,768]{1,0:T(8,128)S(1)}, bf16[1,192,512]{2,1,0:T(8,128)(2,1)S(1)}, bf16[3,192,512]{2,1,0:T(8,128)(2,1)S(1)...) custom-call(s32[4]{0:T(128)S(1)} %copy-done.25, ...), custom_call_target="tpu_custom_call" | custom-call | flops 1 | bytes 1 | tf_op jit(solution)/shard_map/feed_down/pallas_call | solution.py:793
  106.6 1.4 copy-done.14
  108.0 4.7 %attend_backward.3 = (f32[512,768]{1,0:T(8,128)S(1)}, bf16[1,3,512,512]{3,2,1,0:T(8,128)(2,1)S(1)}, f32[1,1,576]{2,1,0:T(1,128)S(1)}, bf16[1,4,72,768]{3,2,1,0:T(8,128)(2,1)S(1)}, bf16[1,4,72,768]{3,2,1,0:T(8,128)(2,1)S(1)}) custom-call(s32[4]{0:T(128)S(1)} %copy-done.26, bf16[512,768]{1,0:T(8,128)(2,1)S(1)} %copy-done.1, bf16[1,576,768]{2,1,0:T(8,128)(2,1)S(1)} %bitcast.80, ...), custom_call_target="tpu_custom_call" | custom-call | flops 1 | bytes 1 | tf_op jit(solution)/shard_map/attend_backward/pallas_call | solution.py:389
  112.7 1.6 collective-permute-done.13.a_got
  114.5 1.9 sum_chips.3
  119.7 1.5 collective-permute-start.18
  121.2 4.7 %attend_backward.4 = (f32[512,768]{1,0:T(8,128)S(1)}, bf16[1,3,512,512]{3,2,1,0:T(8,128)(2,1)S(1)}, f32[1,1,576]{2,1,0:T(1,128)S(1)}, bf16[1,4,72,768]{3,2,1,0:T(8,128)(2,1)S(1)}, bf16[1,4,72,768]{3,2,1,0:T(8,128)(2,1)S(1)}) custom-call(s32[4]{0:T(128)S(1)} %copy-done.26, bf16[512,768]{1,0:T(8,128)(2,1)S(1)} %copy-done.1, ...), custom_call_target="tpu_custom_call" | custom-call | flops 1 | bytes 1 | tf_op jit(solution)/shard_map/attend_backward/pallas_call | solution.py:389
  125.9 1.3 collective-permute-done.16
  127.4 2.4 %collective-permute-start.19 = (bf16[96,768]{1,0:T(8,128)(2,1)S(1)}, bf16[96,768]{1,0:T(8,128)(2,1)S(1)}, u32[]{:S(2)}, u32[]{:S(2)}) collective-permute-start(bf16[96,768]{1,0:T(8,128)(2,1)S(1)} %slice_bitcast_fusion.1), channel_id=1, source_target_pairs={{0,2},{1,3},{2,0},{3,1},{4,6},{5,7},{6,4},{7,5},{8,10},{9,11},{10,... | collective-permute-start | bytes 442376 | tf_op jit(solution)/shard_map/ppermute | solution.py:1186
  129.9 9.1 %attend_backward.5 = (f32[512,768]{1,0:T(8,128)S(1)}, bf16[2,3,512,512]{3,2,1,0:T(8,128)(2,1)S(1)}, f32[2,1,576]{2,1,0:T(1,128)S(1)}, bf16[2,4,72,768]{3,2,1,0:T(8,128)(2,1)S(1)}, bf16[2,4,72,768]{3,2,1,0:T(8,128)(2,1)S(1)}) custom-call(s32[4]{0:T(128)S(1)} %copy-done.26, bf16[512,768]{1,0:T(8,128)(2,1)S(1)} %copy-done.1, ...), custom_call_target="tpu_custom_call" | custom-call | flops 1 | bytes 1 | tf_op jit(solution)/shard_map/attend_backward/pallas_call | solution.py:389
  139.1 1.3 sum_pairs.4
  140.6 1.5 collective-permute-start.22
  143.3 2.0 collective-permute-start.24
  145.3 6.2 %table_products.2.refs_4_ = f32[96,512]{1,0:T(8,128)S(1)} custom-call(bf16[1,3,512,512]{3,2,1,0:T(8,128)(2,1)S(1)} %get-tuple-element.252.refs_0_, bf16[1,3,512,512]{3,2,1,0:T(8,128)(2,1)S(1)} %get-tuple-element.253.refs_1_, bf16[2,3,512,512]{3,2,1,0:T(8,128)(2,1)S(1)} %get-tuple-element.254.refs_2_, ...), custom_call_target="tpu_custom_call" | custom-call | flops 1 | bytes 1 | tf_op jit(solution)/shard_map/table_products/pallas_call | solution.py:448
  157.5 1.8 collective-permute-start.27
  160.1 6.2 %table_products.3.refs_0_ = f32[96,512]{1,0:T(8,128)S(1)} custom-call(bf16[1,3,512,512]{3,2,1,0:T(8,128)(2,1)S(1)} %get-tuple-element.252.refs_0_, bf16[1,3,512,512]{3,2,1,0:T(8,128)(2,1)S(1)} %get-tuple-element.253.refs_1_, bf16[2,3,512,512]{3,2,1,0:T(8,128)(2,1)S(1)} %get-tuple-element.254.refs_2_, ...), custom_call_target="tpu_custom_call" | custom-call | flops 1 | bytes 1 | tf_op jit(solution)/shard_map/table_products/pallas_call | solution.py:448
  166.3 1.6 collective-permute-start.31
  169.2 1.4 sum_pairs.5
  170.7 1.5 collective-permute-start.29
  173.6 2.4 %collective-permute-start.36 = (bf16[24,1920]{1,0:T(8,128)(2,1)S(1)}, bf16[24,1920]{1,0:T(8,128)(2,1)S(1)}, u32[]{:S(2)}, u32[]{:S(2)}) collective-permute-start(bf16[24,1920]{1,0:T(8,128)(2,1)S(1)} %slice_bitcast_fusion.2), channel_id=1, source_target_pairs={{0,1},{1,0},{2,3},{3,2},{4,5},{5,4},{6,7},{7,6},{8,9},{9,8},{10,11... | collective-permute-start | bytes 276488 | tf_op jit(solution)/shard_map/ppermute | solution.py:1186
  178.3 2.5 %collective-permute-start.33 = (bf16[88,768]{1,0:T(8,128)(2,1)S(1)}, bf16[88,768]{1,0:T(8,128)(2,1)S(1)}, u32[]{:S(2)}, u32[]{:S(2)}) collective-permute-start(bf16[88,768]{1,0:T(8,128)(2,1)S(1)} %get-tuple-element.305), channel_id=1, source_target_pairs={{0,2},{1,3},{2,0},{3,1},{4,6},{5,7},{6,4},{7,5},{8,10},{9,11},{10,... | collective-permute-start | bytes 405512 | tf_op jit(solution)/shard_map/ppermute | solution.py:1186
  180.9 1.9 collective-permute-start.34
  182.8 1.6 join_quarters.2
  184.4 2.5 %collective-permute-start.41 = (bf16[24,1920]{1,0:T(8,128)(2,1)S(1)}, bf16[24,1920]{1,0:T(8,128)(2,1)S(1)}, u32[]{:S(2)}, u32[]{:S(2)}) collective-permute-start(bf16[24,1920]{1,0:T(8,128)(2,1)S(1)} %fusion.1.refs_3_), channel_id=1, source_target_pairs={{0,1},{1,0},{2,3},{3,2},{4,5},{5,4},{6,7},{7,6},{8,9},{9,8},{10,11... | collective-permute-start | bytes 276488 | tf_op jit(solution)/shard_map/ppermute | solution.py:1186
  187.0 4.8 %collective-permute-done.33 = bf16[88,768]{1,0:T(8,128)(2,1)S(1)} collective-permute-done((bf16[88,768]{1,0:T(8,128)(2,1)S(1)}, bf16[88,768]{1,0:T(8,128)(2,1)S(1)}, u32[]{:S(2)}, u32[]{:S(2)}) %collective-permute-start.33) | collective-permute-done | bytes 135200 | tf_op jit(solution)/shard_map/ppermute | solution.py:1186
  192.7 1.3 collective-permute-start.38
  195.3 2.3 %collective-permute-start.48 = (bf16[2,24,1920]{2,1,0:T(8,128)(2,1)S(1)}, bf16[2,24,1920]{2,1,0:T(8,128)(2,1)S(1)}, u32[]{:S(2)}, u32[]{:S(2)}) collective-permute-start(bf16[2,24,1920]{2,1,0:T(8,128)(2,1)S(1)} %pad_maximum_fusion.8), channel_id=1, source_target_pairs={{0,1},{1,0},{2,3},{3,2},{4,5},{5,4},{6,7},{7,6},{8,9},{9,8},{10,11... | collective-permute-start | bytes 552968 | tf_op jit(solution)/shard_map/ppermute | solution.py:1186
  201.8 2.4 %collective-permute-done.43 = bf16[2,32,768]{2,1,0:T(8,128)(2,1)S(1)} collective-permute-done((bf16[2,32,768]{2,1,0:T(8,128)(2,1)S(1)}, bf16[2,32,768]{2,1,0:T(8,128)(2,1)S(1)}, u32[]{:S(2)}, u32[]{:S(2)}) %collective-permute-start.43) | collective-permute-done | bytes 98336 | tf_op jit(solution)/shard_map/ppermute | solution.py:1181
  206.1 1.7 join_quarters.3
  207.8 1.9 join_chips.1
  (214 shorter events, 40.9 us)
Async XLA Ops:
  3.4 17.1 %collective-permute-start = (bf16[80,768]{1,0:T(8,128)(2,1)S(1)}, bf16[80,768]{1,0:T(8,128)(2,1)S(1)}, u32[]{:S(2)}, u32[]{:S(2)}) collective-permute-start(bf16[80,768]{1,0:T(8,128)(2,1)S(1)} %pad_maximum_fusion.10), channel_id=1, source_target_pairs={{0,1},{1,0},{2,3},{3,2},{4,5},{5,4},{6,7},{7,6},{8,9},{9,8},{10,11... | collective-permute-start | bytes 368648 | tf_op jit(solution)/shard_map/ppermute | solution.py:1186
  6.5 14.0 %collective-permute-start.1 = (bf16[80,768]{1,0:T(8,128)(2,1)S(1)}, bf16[80,768]{1,0:T(8,128)(2,1)S(1)}, u32[]{:S(2)}, u32[]{:S(2)}) collective-permute-start(bf16[80,768]{1,0:T(8,128)(2,1)S(1)} %pad_maximum_fusion.10), channel_id=1, source_target_pairs={{0,2},{1,3},{2,0},{3,1},{4,6},{5,7},{6,4},{7,5},{8,10},{9,11},{10,... | collective-permute-start | bytes 368648 | tf_op jit(solution)/shard_map/ppermute | solution.py:1186
  9.1 11.4 %collective-permute-start.2 = (bf16[80,768]{1,0:T(8,128)(2,1)S(1)}, bf16[80,768]{1,0:T(8,128)(2,1)S(1)}, u32[]{:S(2)}, u32[]{:S(2)}) collective-permute-start(bf16[80,768]{1,0:T(8,128)(2,1)S(1)} %pad_maximum_fusion.10), channel_id=1, source_target_pairs={{0,3},{1,2},{2,1},{3,0},{4,7},{5,6},{6,5},{7,4},{8,11},{9,10},{10,... | collective-permute-start | bytes 368648 | tf_op jit(solution)/shard_map/ppermute | solution.py:1186
  20.6 5.9 %collective-permute-start.3 = (bf16[3,40,768]{2,1,0:T(8,128)(2,1)S(1)}, bf16[3,40,768]{2,1,0:T(8,128)(2,1)S(1)}, u32[]{:S(2)}, u32[]{:S(2)}) collective-permute-start(bf16[3,40,768]{2,1,0:T(8,128)(2,1)S(1)} %get-tuple-element.344), channel_id=1, source_target_pairs={{0,8},{4,12},{8,0},{12,4},{16,24},{20,28},{24,16},{28,20},{1,9},{5... | collective-permute-start | bytes 552968 | tf_op jit(solution)/shard_map/ppermute | solution.py:1181
  22.4 5.7 %collective-permute-start.5 = (bf16[3,32,768]{2,1,0:T(8,128)(2,1)S(1)}, bf16[3,32,768]{2,1,0:T(8,128)(2,1)S(1)}, u32[]{:S(2)}, u32[]{:S(2)}) collective-permute-start(bf16[3,32,768]{2,1,0:T(8,128)(2,1)S(1)} %get-tuple-element.340), channel_id=1, source_target_pairs={{0,16},{4,20},{8,24},{12,28},{16,0},{20,4},{24,8},{28,12},{1,17},{... | collective-permute-start | bytes 442376 | tf_op jit(solution)/shard_map/ppermute | solution.py:1181
  26.6 9.0 %collective-permute-start.4 = (bf16[2,3,40,768]{3,2,1,0:T(8,128)(2,1)S(1)}, bf16[2,3,40,768]{3,2,1,0:T(8,128)(2,1)S(1)}, u32[]{:S(2)}, u32[]{:S(2)}) collective-permute-start(bf16[2,3,40,768]{3,2,1,0:T(8,128)(2,1)S(1)} %get-tuple-element.342), channel_id=1, source_target_pairs={{0,16},{4,20},{8,24},{12,28},{16,0},{20,4},{24,8},{28,12},{1,17},{... | collective-permute-start | bytes 1105928 | tf_op jit(solution)/shard_map/ppermute | solution.py:1181
  28.3 7.4 %collective-permute-start.6 = (bf16[2,3,32,768]{3,2,1,0:T(8,128)(2,1)S(1)}, bf16[2,3,32,768]{3,2,1,0:T(8,128)(2,1)S(1)}, u32[]{:S(2)}, u32[]{:S(2)}) collective-permute-start(bf16[2,3,32,768]{3,2,1,0:T(8,128)(2,1)S(1)} %get-tuple-element.346), channel_id=1, source_target_pairs={{0,8},{4,12},{8,0},{12,4},{16,24},{20,28},{24,16},{28,20},{1,9},{5... | collective-permute-start | bytes 884744 | tf_op jit(solution)/shard_map/ppermute | solution.py:1181
  35.6 3.1 %collective-permute-start.7 = (bf16[2,2,3,40,768]{4,3,2,1,0:T(8,128)(2,1)S(1)}, bf16[2,2,3,40,768]{4,3,2,1,0:T(8,128)(2,1)S(1)}, u32[]{:S(2)}, u32[]{:S(2)}) collective-permute-start(bf16[2,2,3,40,768]{4,3,2,1,0:T(8,128)(2,1)S(1)} %pad_maximum_fusion.refs_0_), channel_id=1, source_target_pairs={{0,4},{4,0},{8,12},{12,8},{16,20},{20,16},{24,28},{28,24},{1,5},{5... | collective-permute-start | bytes 2211848 | tf_op jit(solution)/shard_map/ppermute | solution.py:1181
  76.9 4.6 %collective-permute-start.9 = (bf16[4,384,768]{2,1,0:T(8,128)(2,1)S(1)}, bf16[4,384,768]{2,1,0:T(8,128)(2,1)S(1)}, u32[]{:S(2)}, u32[]{:S(2)}) collective-permute-start(bf16[4,384,768]{2,1,0:T(8,128)(2,1)S(1)} %bitcast.83), channel_id=1, source_target_pairs={{0,4},{4,0},{8,12},{12,8},{16,20},{20,16},{24,28},{28,24},{1,5},{5... | collective-permute-start | bytes 7077896 | tf_op jit(solution)/shard_map/ppermute | solution.py:1181
  84.2 19.3 %collective-permute-start.10 = (bf16[2,192,768]{2,1,0:T(8,128)(2,1)S(1)}, bf16[2,192,768]{2,1,0:T(8,128)(2,1)S(1)}, u32[]{:S(2)}, u32[]{:S(2)}) collective-permute-start(bf16[2,192,768]{2,1,0:T(8,128)(2,1)S(1)} %get-tuple-element.189), channel_id=1, source_target_pairs={{0,8},{4,12},{8,0},{12,4},{16,24},{20,28},{24,16},{28,20},{1,9},{5... | collective-permute-start | bytes 1769480 | tf_op jit(solution)/shard_map/ppermute | solution.py:1181
  85.2 18.3 %collective-permute-start.11 = (bf16[2,192,768]{2,1,0:T(8,128)(2,1)S(1)}, bf16[2,192,768]{2,1,0:T(8,128)(2,1)S(1)}, u32[]{:S(2)}, u32[]{:S(2)}) collective-permute-start(bf16[2,192,768]{2,1,0:T(8,128)(2,1)S(1)} %get-tuple-element.190), channel_id=1, source_target_pairs={{0,16},{4,20},{8,24},{12,28},{16,0},{20,4},{24,8},{28,12},{1,17},{... | collective-permute-start | bytes 1769480 | tf_op jit(solution)/shard_map/ppermute | solution.py:1181
  104.8 9.7 %collective-permute-start.12 = (bf16[4,96,3840]{2,1,0:T(8,128)(2,1)}, bf16[4,96,3840]{2,1,0:T(8,128)(2,1)S(1)}, u32[]{:S(2)}, u32[]{:S(2)}) collective-permute-start(bf16[4,96,3840]{2,1,0:T(8,128)(2,1)} %get-tuple-element.209), channel_id=1, source_target_pairs={{0,4},{4,0},{8,12},{12,8},{16,20},{20,16},{24,28},{28,24},{1,5},{5... | collective-permute-start | bytes 8847368 | tf_op jit(solution)/shard_map/ppermute | solution.py:1181
  104.9 9.4 %collective-permute-start.13 = (bf16[192,768]{1,0:T(8,128)(2,1)S(1)}, bf16[192,768]{1,0:T(8,128)(2,1)S(1)}, u32[]{:S(2)}, u32[]{:S(2)}) collective-permute-start(bf16[192,768]{1,0:T(8,128)(2,1)S(1)} %get-tuple-element.208), channel_id=1, source_target_pairs={{0,16},{4,20},{8,24},{12,28},{16,0},{20,4},{24,8},{28,12},{1,17},{... | collective-permute-start | bytes 884744 | tf_op jit(solution)/shard_map/ppermute | solution.py:1181
  105.5 9.1 %collective-permute-start.14 = (bf16[192,768]{1,0:T(8,128)(2,1)S(1)}, bf16[192,768]{1,0:T(8,128)(2,1)S(1)}, u32[]{:S(2)}, u32[]{:S(2)}) collective-permute-start(bf16[192,768]{1,0:T(8,128)(2,1)S(1)} %get-tuple-element.210), channel_id=1, source_target_pairs={{0,8},{4,12},{8,0},{12,4},{16,24},{20,28},{24,16},{28,20},{1,9},{5... | collective-permute-start | bytes 884744 | tf_op jit(solution)/shard_map/ppermute | solution.py:1181
  117.7 9.5 %collective-permute-start.15 = (bf16[1,4,72,768]{3,2,1,0:T(8,128)(2,1)S(1)}, bf16[1,4,72,768]{3,2,1,0:T(8,128)(2,1)S(1)}, u32[]{:S(2)}, u32[]{:S(2)}) collective-permute-start(bf16[1,4,72,768]{3,2,1,0:T(8,128)(2,1)S(1)} %get-tuple-element.227), channel_id=1, source_target_pairs={{0,4},{4,0},{8,12},{12,8},{16,20},{20,16},{24,28},{28,24},{1,5},{5... | collective-permute-start | bytes 1327112 | tf_op jit(solution)/shard_map/ppermute | solution.py:1181
  117.8 9.4 %collective-permute-start.16 = (bf16[2,96,768]{2,1,0:T(8,128)(2,1)S(1)}, bf16[2,96,768]{2,1,0:T(8,128)(2,1)S(1)}, u32[]{:S(2)}, u32[]{:S(2)}) collective-permute-start(bf16[2,96,768]{2,1,0:T(8,128)(2,1)S(1)} %get-tuple-element.224), channel_id=1, source_target_pairs={{0,1},{1,0},{2,3},{3,2},{4,5},{5,4},{6,7},{7,6},{8,9},{9,8},{10,11... | collective-permute-start | bytes 884744 | tf_op jit(solution)/shard_map/ppermute | solution.py:1186
  118.5 20.5 %collective-permute-start.17 = (bf16[2,48,3840]{2,1,0:T(8,128)(2,1)S(1)}, bf16[2,48,3840]{2,1,0:T(8,128)(2,1)S(1)}, u32[]{:S(2)}, u32[]{:S(2)}) collective-permute-start(bf16[2,48,3840]{2,1,0:T(8,128)(2,1)S(1)} %get-tuple-element.225), channel_id=1, source_target_pairs={{0,8},{4,12},{8,0},{12,4},{16,24},{20,28},{24,16},{28,20},{1,9},{5... | collective-permute-start | bytes 2211848 | tf_op jit(solution)/shard_map/ppermute | solution.py:1181
  119.7 19.3 %collective-permute-start.18 = (bf16[2,48,3840]{2,1,0:T(8,128)(2,1)S(1)}, bf16[2,48,3840]{2,1,0:T(8,128)(2,1)S(1)}, u32[]{:S(2)}, u32[]{:S(2)}) collective-permute-start(bf16[2,48,3840]{2,1,0:T(8,128)(2,1)S(1)} %get-tuple-element.226), channel_id=1, source_target_pairs={{0,16},{4,20},{8,24},{12,28},{16,0},{20,4},{24,8},{28,12},{1,17},{... | collective-permute-start | bytes 2211848 | tf_op jit(solution)/shard_map/ppermute | solution.py:1181
  127.3 11.7 %collective-permute-start.20 = (bf16[1,4,72,768]{3,2,1,0:T(8,128)(2,1)S(1)}, bf16[1,4,72,768]{3,2,1,0:T(8,128)(2,1)S(1)}, u32[]{:S(2)}, u32[]{:S(2)}) collective-permute-start(bf16[1,4,72,768]{3,2,1,0:T(8,128)(2,1)S(1)} %get-tuple-element.233), channel_id=1, source_target_pairs={{0,4},{4,0},{8,12},{12,8},{16,20},{20,16},{24,28},{28,24},{1,5},{5... | collective-permute-start | bytes 1327112 | tf_op jit(solution)/shard_map/ppermute | solution.py:1181
  127.4 11.6 %collective-permute-start.19 = (bf16[96,768]{1,0:T(8,128)(2,1)S(1)}, bf16[96,768]{1,0:T(8,128)(2,1)S(1)}, u32[]{:S(2)}, u32[]{:S(2)}) collective-permute-start(bf16[96,768]{1,0:T(8,128)(2,1)S(1)} %slice_bitcast_fusion.1), channel_id=1, source_target_pairs={{0,2},{1,3},{2,0},{3,1},{4,6},{5,7},{6,4},{7,5},{8,10},{9,11},{10,... | collective-permute-start | bytes 442376 | tf_op jit(solution)/shard_map/ppermute | solution.py:1186
  140.4 12.5 %collective-permute-start.21 = (bf16[2,4,72,768]{3,2,1,0:T(8,128)(2,1)S(1)}, bf16[2,4,72,768]{3,2,1,0:T(8,128)(2,1)S(1)}, u32[]{:S(2)}, u32[]{:S(2)}) collective-permute-start(bf16[2,4,72,768]{3,2,1,0:T(8,128)(2,1)S(1)} %get-tuple-element.248), channel_id=1, source_target_pairs={{0,4},{4,0},{8,12},{12,8},{16,20},{20,16},{24,28},{28,24},{1,5},{5... | collective-permute-start | bytes 2654216 | tf_op jit(solution)/shard_map/ppermute | solution.py:1181
  140.6 12.2 %collective-permute-start.22 = (bf16[48,3840]{1,0:T(8,128)(2,1)S(1)}, bf16[48,3840]{1,0:T(8,128)(2,1)S(1)}, u32[]{:S(2)}, u32[]{:S(2)}) collective-permute-start(bf16[48,3840]{1,0:T(8,128)(2,1)S(1)} %get-tuple-element.249), channel_id=1, source_target_pairs={{0,16},{4,20},{8,24},{12,28},{16,0},{20,4},{24,8},{28,12},{1,17},{... | collective-permute-start | bytes 1105928 | tf_op jit(solution)/shard_map/ppermute | solution.py:1181
  142.2 10.7 %collective-permute-start.23 = (bf16[48,3840]{1,0:T(8,128)(2,1)S(1)}, bf16[48,3840]{1,0:T(8,128)(2,1)S(1)}, u32[]{:S(2)}, u32[]{:S(2)}) collective-permute-start(bf16[48,3840]{1,0:T(8,128)(2,1)S(1)} %get-tuple-element.250), channel_id=1, source_target_pairs={{0,8},{4,12},{8,0},{12,4},{16,24},{20,28},{24,16},{28,20},{1,9},{5... | collective-permute-start | bytes 1105928 | tf_op jit(solution)/shard_map/ppermute | solution.py:1181
  143.3 9.5 %collective-permute-start.24 = (bf16[96,768]{1,0:T(8,128)(2,1)S(1)}, bf16[96,768]{1,0:T(8,128)(2,1)S(1)}, u32[]{:S(2)}, u32[]{:S(2)}) collective-permute-start(bf16[96,768]{1,0:T(8,128)(2,1)S(1)} %fusion.refs_0_), channel_id=1, source_target_pairs={{0,2},{1,3},{2,0},{3,1},{4,6},{5,7},{6,4},{7,5},{8,10},{9,11},{10,... | collective-permute-start | bytes 442376 | tf_op jit(solution)/shard_map/ppermute | solution.py:1186
  156.0 13.3 %collective-permute-start.25 = (bf16[2,144,768]{2,1,0:T(8,128)(2,1)S(1)}, bf16[2,144,768]{2,1,0:T(8,128)(2,1)S(1)}, u32[]{:S(2)}, u32[]{:S(2)}) collective-permute-start(bf16[2,144,768]{2,1,0:T(8,128)(2,1)S(1)} %get-tuple-element.273), channel_id=1, source_target_pairs={{0,8},{4,12},{8,0},{12,4},{16,24},{20,28},{24,16},{28,20},{1,9},{5... | collective-permute-start | bytes 1327112 | tf_op jit(solution)/shard_map/ppermute | solution.py:1181
  157.0 12.3 %collective-permute-start.26 = (bf16[2,144,768]{2,1,0:T(8,128)(2,1)S(1)}, bf16[2,144,768]{2,1,0:T(8,128)(2,1)S(1)}, u32[]{:S(2)}, u32[]{:S(2)}) collective-permute-start(bf16[2,144,768]{2,1,0:T(8,128)(2,1)S(1)} %get-tuple-element.274), channel_id=1, source_target_pairs={{0,16},{4,20},{8,24},{12,28},{16,0},{20,4},{24,8},{28,12},{1,17},{... | collective-permute-start | bytes 1327112 | tf_op jit(solution)/shard_map/ppermute | solution.py:1181
  157.5 10.5 %collective-permute-start.27 = (bf16[2,24,1920]{2,1,0:T(8,128)(2,1)S(1)}, bf16[2,24,1920]{2,1,0:T(8,128)(2,1)S(1)}, u32[]{:S(2)}, u32[]{:S(2)}) collective-permute-start(bf16[2,24,1920]{2,1,0:T(8,128)(2,1)S(1)} %get-tuple-element.275), channel_id=1, source_target_pairs={{0,1},{1,0},{2,3},{3,2},{4,5},{5,4},{6,7},{7,6},{8,9},{9,8},{10,11... | collective-permute-start | bytes 552968 | tf_op jit(solution)/shard_map/ppermute | solution.py:1186
  159.3 10.0 %collective-permute-start.28 = (bf16[2,24,1920]{2,1,0:T(8,128)(2,1)S(1)}, bf16[2,24,1920]{2,1,0:T(8,128)(2,1)S(1)}, u32[]{:S(2)}, u32[]{:S(2)}) collective-permute-start(bf16[2,24,1920]{2,1,0:T(8,128)(2,1)S(1)} %get-tuple-element.276), channel_id=1, source_target_pairs={{0,2},{1,3},{2,0},{3,1},{4,6},{5,7},{6,4},{7,5},{8,10},{9,11},{10,... | collective-permute-start | bytes 552968 | tf_op jit(solution)/shard_map/ppermute | solution.py:1186
  166.3 10.7 %collective-permute-start.31 = (bf16[2,96,768]{2,1,0:T(8,128)(2,1)S(1)}, bf16[2,96,768]{2,1,0:T(8,128)(2,1)S(1)}, u32[]{:S(2)}, u32[]{:S(2)}) collective-permute-start(bf16[2,96,768]{2,1,0:T(8,128)(2,1)S(1)} %pad_maximum_fusion.5), channel_id=1, source_target_pairs={{0,1},{1,0},{2,3},{3,2},{4,5},{5,4},{6,7},{7,6},{8,9},{9,8},{10,11... | collective-permute-start | bytes 884744 | tf_op jit(solution)/shard_map/ppermute | solution.py:1186
  170.7 6.4 %collective-permute-start.29 = (bf16[144,768]{1,0:T(8,128)(2,1)S(1)}, bf16[144,768]{1,0:T(8,128)(2,1)S(1)}, u32[]{:S(2)}, u32[]{:S(2)}) collective-permute-start(bf16[144,768]{1,0:T(8,128)(2,1)S(1)} %get-tuple-element.288), channel_id=1, source_target_pairs={{0,16},{4,20},{8,24},{12,28},{16,0},{20,4},{24,8},{28,12},{1,17},{... | collective-permute-start | bytes 663560 | tf_op jit(solution)/shard_map/ppermute | solution.py:1181
  172.2 5.9 %collective-permute-start.30 = (bf16[144,768]{1,0:T(8,128)(2,1)S(1)}, bf16[144,768]{1,0:T(8,128)(2,1)S(1)}, u32[]{:S(2)}, u32[]{:S(2)}) collective-permute-start(bf16[144,768]{1,0:T(8,128)(2,1)S(1)} %get-tuple-element.289), channel_id=1, source_target_pairs={{0,8},{4,12},{8,0},{12,4},{16,24},{20,28},{24,16},{28,20},{1,9},{5... | collective-permute-start | bytes 663560 | tf_op jit(solution)/shard_map/ppermute | solution.py:1181
  173.0 9.7 %collective-permute-start.35 = (bf16[24,1920]{1,0:T(8,128)(2,1)S(1)}, bf16[24,1920]{1,0:T(8,128)(2,1)S(1)}, u32[]{:S(2)}, u32[]{:S(2)}) collective-permute-start(bf16[24,1920]{1,0:T(8,128)(2,1)S(1)} %slice_bitcast_fusion.3), channel_id=1, source_target_pairs={{0,2},{1,3},{2,0},{3,1},{4,6},{5,7},{6,4},{7,5},{8,10},{9,11},{10,... | collective-permute-start | bytes 276488 | tf_op jit(solution)/shard_map/ppermute | solution.py:1186
  173.6 9.1 %collective-permute-start.36 = (bf16[24,1920]{1,0:T(8,128)(2,1)S(1)}, bf16[24,1920]{1,0:T(8,128)(2,1)S(1)}, u32[]{:S(2)}, u32[]{:S(2)}) collective-permute-start(bf16[24,1920]{1,0:T(8,128)(2,1)S(1)} %slice_bitcast_fusion.2), channel_id=1, source_target_pairs={{0,1},{1,0},{2,3},{3,2},{4,5},{5,4},{6,7},{7,6},{8,9},{9,8},{10,11... | collective-permute-start | bytes 276488 | tf_op jit(solution)/shard_map/ppermute | solution.py:1186
  178.3 8.7 %collective-permute-start.32 = (bf16[88,768]{1,0:T(8,128)(2,1)S(1)}, bf16[88,768]{1,0:T(8,128)(2,1)S(1)}, u32[]{:S(2)}, u32[]{:S(2)}) collective-permute-start(bf16[88,768]{1,0:T(8,128)(2,1)S(1)} %get-tuple-element.304), channel_id=1, source_target_pairs={{0,1},{1,0},{2,3},{3,2},{4,5},{5,4},{6,7},{7,6},{8,9},{9,8},{10,11... | collective-permute-start | bytes 405512 | tf_op jit(solution)/shard_map/ppermute | solution.py:1186
  178.3 13.4 %collective-permute-start.33 = (bf16[88,768]{1,0:T(8,128)(2,1)S(1)}, bf16[88,768]{1,0:T(8,128)(2,1)S(1)}, u32[]{:S(2)}, u32[]{:S(2)}) collective-permute-start(bf16[88,768]{1,0:T(8,128)(2,1)S(1)} %get-tuple-element.305), channel_id=1, source_target_pairs={{0,2},{1,3},{2,0},{3,1},{4,6},{5,7},{6,4},{7,5},{8,10},{9,11},{10,... | collective-permute-start | bytes 405512 | tf_op jit(solution)/shard_map/ppermute | solution.py:1186
  180.9 10.9 %collective-permute-start.34 = (bf16[88,768]{1,0:T(8,128)(2,1)S(1)}, bf16[88,768]{1,0:T(8,128)(2,1)S(1)}, u32[]{:S(2)}, u32[]{:S(2)}) collective-permute-start(bf16[88,768]{1,0:T(8,128)(2,1)S(1)} %get-tuple-element.306), channel_id=1, source_target_pairs={{0,3},{1,2},{2,1},{3,0},{4,7},{5,6},{6,5},{7,4},{8,11},{9,10},{10,... | collective-permute-start | bytes 405512 | tf_op jit(solution)/shard_map/ppermute | solution.py:1186
  184.4 10.8 %collective-permute-start.40 = (bf16[24,1920]{1,0:T(8,128)(2,1)S(1)}, bf16[24,1920]{1,0:T(8,128)(2,1)S(1)}, u32[]{:S(2)}, u32[]{:S(2)}) collective-permute-start(bf16[24,1920]{1,0:T(8,128)(2,1)S(1)} %fusion.2.refs_0_), channel_id=1, source_target_pairs={{0,2},{1,3},{2,0},{3,1},{4,6},{5,7},{6,4},{7,5},{8,10},{9,11},{10,... | collective-permute-start | bytes 276488 | tf_op jit(solution)/shard_map/ppermute | solution.py:1186
  184.4 10.8 %collective-permute-start.41 = (bf16[24,1920]{1,0:T(8,128)(2,1)S(1)}, bf16[24,1920]{1,0:T(8,128)(2,1)S(1)}, u32[]{:S(2)}, u32[]{:S(2)}) collective-permute-start(bf16[24,1920]{1,0:T(8,128)(2,1)S(1)} %fusion.1.refs_3_), channel_id=1, source_target_pairs={{0,1},{1,0},{2,3},{3,2},{4,5},{5,4},{6,7},{7,6},{8,9},{9,8},{10,11... | collective-permute-start | bytes 276488 | tf_op jit(solution)/shard_map/ppermute | solution.py:1186
  191.9 6.7 %collective-permute-start.37 = (bf16[40,768]{1,0:T(8,128)(2,1)S(1)}, bf16[40,768]{1,0:T(8,128)(2,1)S(1)}, u32[]{:S(2)}, u32[]{:S(2)}) collective-permute-start(bf16[40,768]{1,0:T(8,128)(2,1)S(1)} %get-tuple-element.352), channel_id=1, source_target_pairs={{0,8},{4,12},{8,0},{12,4},{16,24},{20,28},{24,16},{28,20},{1,9},{5... | collective-permute-start | bytes 184328 | tf_op jit(solution)/shard_map/ppermute | solution.py:1181
  192.7 5.9 %collective-permute-start.38 = (bf16[32,768]{1,0:T(8,128)(2,1)S(1)}, bf16[32,768]{1,0:T(8,128)(2,1)S(1)}, u32[]{:S(2)}, u32[]{:S(2)}) collective-permute-start(bf16[32,768]{1,0:T(8,128)(2,1)S(1)} %get-tuple-element.350), channel_id=1, source_target_pairs={{0,16},{4,20},{8,24},{12,28},{16,0},{20,4},{24,8},{28,12},{1,17},{... | collective-permute-start | bytes 147464 | tf_op jit(solution)/shard_map/ppermute | solution.py:1181
  194.0 4.5 %collective-permute-start.39 = (bf16[16,768]{1,0:T(8,128)(2,1)S(1)}, bf16[16,768]{1,0:T(8,128)(2,1)S(1)}, u32[]{:S(2)}, u32[]{:S(2)}) collective-permute-start(bf16[16,768]{1,0:T(8,128)(2,1)S(1)} %add_convert_fusion.6), channel_id=1, source_target_pairs={{0,8},{4,12},{8,0},{12,4},{16,24},{20,28},{24,16},{28,20},{1,9},{5... | collective-permute-start | bytes 73736 | tf_op jit(solution)/shard_map/ppermute | solution.py:1181
  195.3 10.7 %collective-permute-start.48 = (bf16[2,24,1920]{2,1,0:T(8,128)(2,1)S(1)}, bf16[2,24,1920]{2,1,0:T(8,128)(2,1)S(1)}, u32[]{:S(2)}, u32[]{:S(2)}) collective-permute-start(bf16[2,24,1920]{2,1,0:T(8,128)(2,1)S(1)} %pad_maximum_fusion.8), channel_id=1, source_target_pairs={{0,1},{1,0},{2,3},{3,2},{4,5},{5,4},{6,7},{7,6},{8,9},{9,8},{10,11... | collective-permute-start | bytes 552968 | tf_op jit(solution)/shard_map/ppermute | solution.py:1186
  197.6 8.5 %collective-permute-start.49 = (bf16[2,24,1920]{2,1,0:T(8,128)(2,1)S(1)}, bf16[2,24,1920]{2,1,0:T(8,128)(2,1)S(1)}, u32[]{:S(2)}, u32[]{:S(2)}) collective-permute-start(bf16[2,24,1920]{2,1,0:T(8,128)(2,1)S(1)} %pad_maximum_fusion.9), channel_id=1, source_target_pairs={{0,2},{1,3},{2,0},{3,1},{4,6},{5,7},{6,4},{7,5},{8,10},{9,11},{10,... | collective-permute-start | bytes 552968 | tf_op jit(solution)/shard_map/ppermute | solution.py:1186
  198.6 5.7 %collective-permute-start.42 = (bf16[2,40,768]{2,1,0:T(8,128)(2,1)S(1)}, bf16[2,40,768]{2,1,0:T(8,128)(2,1)S(1)}, u32[]{:S(2)}, u32[]{:S(2)}) collective-permute-start(bf16[2,40,768]{2,1,0:T(8,128)(2,1)S(1)} %get-tuple-element.348), channel_id=1, source_target_pairs={{0,16},{4,20},{8,24},{12,28},{16,0},{20,4},{24,8},{28,12},{1,17},{... | collective-permute-start | bytes 368648 | tf_op jit(solution)/shard_map/ppermute | solution.py:1181
  199.5 4.7 %collective-permute-start.43 = (bf16[2,32,768]{2,1,0:T(8,128)(2,1)S(1)}, bf16[2,32,768]{2,1,0:T(8,128)(2,1)S(1)}, u32[]{:S(2)}, u32[]{:S(2)}) collective-permute-start(bf16[2,32,768]{2,1,0:T(8,128)(2,1)S(1)} %get-tuple-element.354), channel_id=1, source_target_pairs={{0,8},{4,12},{8,0},{12,4},{16,24},{20,28},{24,16},{28,20},{1,9},{5... | collective-permute-start | bytes 294920 | tf_op jit(solution)/shard_map/ppermute | solution.py:1181
  200.6 4.2 %collective-permute-start.46 = (bf16[16,768]{1,0:T(8,128)(2,1)S(1)}, bf16[16,768]{1,0:T(8,128)(2,1)S(1)}, u32[]{:S(2)}, u32[]{:S(2)}) collective-permute-start(bf16[16,768]{1,0:T(8,128)(2,1)S(1)} %add_convert_fusion.5), channel_id=1, source_target_pairs={{0,16},{4,20},{8,24},{12,28},{16,0},{20,4},{24,8},{28,12},{1,17},{... | collective-permute-start | bytes 73736 | tf_op jit(solution)/shard_map/ppermute | solution.py:1181
  204.2 3.7 %collective-permute-start.45 = (bf16[2,2,32,768]{3,2,1,0:T(8,128)(2,1)S(1)}, bf16[2,2,32,768]{3,2,1,0:T(8,128)(2,1)S(1)}, u32[]{:S(2)}, u32[]{:S(2)}) collective-permute-start(bf16[2,2,32,768]{3,2,1,0:T(8,128)(2,1)S(1)} %pad_maximum_fusion.7.mine_b), channel_id=1, source_target_pairs={{0,4},{4,0},{8,12},{12,8},{16,20},{20,16},{24,28},{28,24},{1,5},{5... | collective-permute-start | bytes 589832 | tf_op jit(solution)/shard_map/ppermute | solution.py:1181
  204.3 3.5 %collective-permute-start.44 = (bf16[2,2,40,768]{3,2,1,0:T(8,128)(2,1)S(1)}, bf16[2,2,40,768]{3,2,1,0:T(8,128)(2,1)S(1)}, u32[]{:S(2)}, u32[]{:S(2)}) collective-permute-start(bf16[2,2,40,768]{3,2,1,0:T(8,128)(2,1)S(1)} %pad_maximum_fusion.6.mine_a), channel_id=1, source_target_pairs={{0,4},{4,0},{8,12},{12,8},{16,20},{20,16},{24,28},{28,24},{1,5},{5... | collective-permute-start | bytes 737288 | tf_op jit(solution)/shard_map/ppermute | solution.py:1181
  (46 other events, 421.6 us)

commit v2 on v1

--- a/solution.py
+++ b/solution.py
@@ -31,6 +31,10 @@
     return pl.BlockSpec(shape, lambda *_: (0,) * len(shape))
 
 
+def in_hbm(dtype, *shape):
+    return pltpu.HBM(shape, dtype)
+
+
 def limit(mebibytes):
     return pltpu.CompilerParams(vmem_limit_bytes=mebibytes << 20)
 
@@ -107,6 +111,49 @@
         compiler_params=limit(6),
         cost_estimate=HINT,
     )(place, lengths, boxes)
+
+
+def piece_kernel(place_ref, rows_ref, bias_ref, tables_ref, piece_ref, extra_ref, line_sc):
+    line_sc[...] = jnp.zeros_like(line_sc)
+    own = bias_ref.shape[1]
+    per, _, buckets = tables_ref.shape
+    bias = bias_ref[...].astype(F32)
+    for n in range(2):
+        line_sc[0:1, n * own : (n + 1) * own] = bias[n : n + 1, :]
+        for h in range(per):
+            at = 2 * own + n * 128 + h * buckets
+            line_sc[0:1, at : at + buckets] = tables_ref[h].astype(F32)[n : n + 1, :]
+    extra = line_sc[...].astype(BF)
+    extra_ref[...] = extra
+    size = rows_ref.shape[0]
+    piece_ref[0:size, :] = rows_ref[...]
+    piece_ref[size:, :] = extra
+
+
+def first_piece(place, matrix, bias, tables, docs_count):
+    columns, depth = matrix.shape
+    size = columns // docs_count
+    return pl.pallas_call(
+        piece_kernel,
+        grid_spec=pltpu.PrefetchScalarGridSpec(
+            num_scalar_prefetch=1,
+            grid=(1,),
+            in_specs=[
+                pl.BlockSpec(
+                    (size, depth),
+                    lambda i, place: ((place[3] * 2 + place[2]) * 2 + place[1], 0),
+                ),
+                whole(*bias.shape),
+                whole(*tables.shape),
+            ],
+            out_specs=[whole(size + 8, depth), whole(8, depth)],
+            scratch_shapes=[pltpu.VMEM((8, depth), F32)],
+        ),
+        out_shape=[shaped(BF, size + 8, depth), shaped(BF, 8, depth)],
+        name="first_piece",
+        compiler_params=limit(4),
+        cost_estimate=HINT,
+    )(place, matrix, bias, tables)
 
 
 def lookup(table_row, index):
@@ -254,11 +301,12 @@
     out_specs = [
         each(L, width), each(width, L), each(heads, L, L), each(columns, L), each(8, L)
     ]
+    far = in_hbm if gathered else shaped
     out_shape = [
         shaped(BF, groups, L, width),
-        shaped(BF, groups, width, L),
+        far(BF, groups, width, L),
         shaped(BF, groups, heads, L, L),
-        shaped(BF, groups, columns, L),
+        far(BF, groups, columns, L),
         shaped(F32, groups, 8, L),
     ]
     scratch = [
@@ -269,7 +317,7 @@
     ]
     if gathered:
         out_specs = [each(columns, depth)] + out_specs
-        out_shape = [shaped(BF, groups, columns, depth)] + out_shape
+        out_shape = [in_hbm(BF, groups, columns, depth)] + out_shape
         scratch = scratch + [pltpu.VMEM((columns, depth), F32)]
     return pl.pallas_call(
         functools.partial(forward_kernel, gathered),
@@ -1256,20 +1304,26 @@
     chips = 4 if count == 8 and share % 16 == 0 and small % 8 == 0 else 0
     place = jnp.stack([z, docs & 1, (docs >> 1) & 1, (docs >> 2) & 1]).astype(I32)
 
+    still = lambda array: pltpu.with_memory_space_constraint(array, pltpu.HBM)
     matrix = w_qkv.transpose(1, 2, 0).reshape(columns, width)
-    room = jnp.zeros((128 - heads * buckets,), BF)
-    line = jnp.concatenate(
-        [qv_bias[0], qv_bias[1], rel_tables[0].reshape(-1), room, rel_tables[1].reshape(-1), room]
-    )
-    extra = jnp.pad(line[None], ((0, 7), (0, width - line.shape[0])))
-    piece = jnp.concatenate(
-        [lax.dynamic_slice_in_dim(matrix, docs * small, small, axis=0), extra], axis=0
-    )
+    if chips:
+        piece, extra = first_piece(
+            place, still(matrix), still(qv_bias), still(rel_tables.transpose(1, 0, 2)), count
+        )
+    else:
+        room = jnp.zeros((128 - heads * buckets,), BF)
+        line = jnp.concatenate(
+            [qv_bias[0], qv_bias[1], rel_tables[0].reshape(-1), room, rel_tables[1].reshape(-1), room]
+        )
+        extra = jnp.pad(line[None], ((0, 7), (0, width - line.shape[0])))
+        piece = jnp.concatenate(
+            [lax.dynamic_slice_in_dim(matrix, docs * small, small, axis=0), extra], axis=0
+        )
     got = [away(piece, s) for s in range(1, groups)]
-    bucket, near = buckets_of(place, lengths, token_boxes)
+    bucket, near = buckets_of(place, lengths, still(token_boxes))
 
     ctx_own, turned_own, raised_own, qkv_own, norm_own = attend_forward(
-        place, layer_input, (matrix[None],), extra[None], bucket, near
+        place, still(layer_input), (still(matrix[None]),), extra[None], bucket, near
     )
     arrived = jnp.stack(tie(got, ctx_own))
     if chips:
@@ -1298,7 +1352,7 @@
         w_out_heads, turned_own, turned, norm_own, norm,
     )
     own_back = lambda grad, start: attend_backward(
-        place, chips, layer_input, matrix[None], qkv_own, raised_own, norm_own, grad, start
+        place, chips, layer_input, matrix[None], qkv_own, still(raised_own), norm_own, grad, start
     )
     rest_back = lambda span, grad, start: attend_backward(
         place, chips, layer_input, weights, qkv, raised, norm, grad, start, span
@@ -1406,17 +1460,19 @@
         quarter = total_of(last[0][:small], *[item[:small] for item in last_got])
         ends = tree([item[small:].astype(F32) for item in [last[0]] + last_got]).astype(BF)
         first, second = quarter[:cut], quarter[cut:]
-        got = [swap(first, 1), swap(second, 2), swap(ends, 1)]
+        rest = small - cut
+        got = [swap(first, 1), swap(jnp.concatenate([second, ends]), 2)]
         dense_one = tie(dense_one, first, second)
         dense_two = [jnp.stack(pair) for pair in zip(dense, dense_one)]
         dense_two = [away(dense_two[0], 1), away(dense_two[1], 2)]
         got = tie(got, dense_one)
-        first, second = jnp.stack([first, got[0]]), jnp.stack([second, got[1]])
-        ends = total_of(ends, got[2])
-        got = [swap(first, 2), swap(second, 1), swap(ends, 2)]
-        dense_two = tie(dense_two, first, second)
-        first, second = jnp.stack([first, got[0]]), jnp.stack([second, got[1]])
-        ends = total_of(ends, got[2])
+        ends = total_of(ends, got[1][rest:])
+        first, second = jnp.stack([first, got[0]]), jnp.stack([second, got[1][:rest]])
+        both = jnp.concatenate([second, ends.reshape(2, -1, width)], axis=1)
+        got = [swap(first, 2), swap(both, 1)]
+        dense_two = tie(dense_two, first, both)
+        ends = total_of(ends, got[1][:, rest:].reshape(ends.shape))
+        first, second = jnp.stack([first, got[0]]), jnp.stack([second, got[1][:, :rest]])
         got = [swap(first, 0), swap(second, 0), swap(ends, 0)]
         out_in, out_out = join_quarters(
             place, list(zip(dense, dense_one, dense_two)), ((2, 1, 3), (1, 2, 3)), (units, width)

time: 211 us -> 205 us (0.972)
  local copies, waits for them, and re-layouts: 12.9 us -> 2.23 us
  Pallas kernels: 108 us -> 114 us
    unnamed x88 -> x74, local copies, waits for them, and re-layouts: 10.1 us -> 2.09 us
    pallas_call x2, Pallas kernels: 18.2 us -> 20.3 us  [attend_forward(): pl.pallas_call(functools.partial(forward_kernel, gathered), grid_spec=plt...]
    ppermute x32 -> x30, starting transfers between devices: 28.4 us -> 26.7 us  [swap(): lax.ppermute(array, 'docs', [(i, i ^ 1 << bit) for i in range(count)])]
    ppermute x32 -> x30, waiting for transfers between devices: 20.2 us -> 21.4 us  [swap(): lax.ppermute(array, 'docs', [(i, i ^ 1 << bit) for i in range(count)])]
  transfers between devices with their start and end apart: 50 -> 48, of which waited for: 13 -> 14; matrix products, arithmetic and copies ran while one was open for 1% -> 1% of each run, Pallas kernels for 29% -> 31%
where the time goes in v2:
time: 205 us
  Pallas kernels  114 us (56%)
  starting transfers between devices  54.5 us (27%)
  waiting for transfers between devices  30.5 us (15%)
  other arithmetic  2.43 us (1%)
  local copies, waits for them, and re-layouts  2.23 us (1%)
    ppermute x18, starting transfers between devices, away(): lax.ppermute(array, 'heads', [(i, i ^ distance) for i in range(count)])  27.8 us
    ppermute x30, starting transfers between devices, swap(): lax.ppermute(array, 'docs', [(i, i ^ 1 << bit) for i in range(count)])  26.7 us
    ppermute x30, waiting for transfers between devices, swap(): lax.ppermute(array, 'docs', [(i, i ^ 1 << bit) for i in range(count)])  21.4 us
    pallas_call x2, Pallas kernels, attend_forward(): pl.pallas_call(functools.partial(forward_kernel, gathered), grid_spec=plt...  20.3 us
    pallas_call x3, Pallas kernels, attend_backward(): pl.pallas_call(functools.partial(backward_kernel, bool(halves)), grid_spe...  19.9 us
    pallas_call x1, Pallas kernels, feed_up(): pl.pallas_call(up_kernel, grid_spec=pltpu.PrefetchScalarGridSpec(num_scal...  17.6 us
    pallas_call x1, Pallas kernels, feed_down(): pl.pallas_call(functools.partial(down_kernel, bool(halves)), grid_spec=pl...  16.1 us
    pallas_call x2, Pallas kernels, table_products(): pl.pallas_call(functools.partial(table_kernel, skip), grid=(steps,), in_s...  12.4 us
  transfers between devices with their start and end apart: 48, of which 14 were waited for; matrix products, arithmetic and copies ran while one was open for 1% of the time, Pallas kernels for 31%

profile of v2, /device:TPU:0, one launch (start us, length us, event | category | flops | bytes accessed | tf_op | source)
XLA Modules:
  0.0 204.7 jit_solution(8185391690256438723)
XLA Ops:
  0.7 1.6 first_piece.1
  2.3 3.0 %collective-permute-start = (bf16[80,768]{1,0:T(8,128)(2,1)S(1)}, bf16[80,768]{1,0:T(8,128)(2,1)S(1)}, u32[]{:S(2)}, u32[]{:S(2)}) collective-permute-start(bf16[80,768]{1,0:T(8,128)(2,1)S(1)} %get-tuple-element.180), channel_id=1, source_target_pairs={{0,1},{1,0},{2,3},{3,2},{4,5},{5,4},{6,7},{7,6},{8,9},{9,8},{10,11... | collective-permute-start | bytes 368648 | tf_op jit(solution)/shard_map/ppermute | solution.py:1234
  5.3 2.6 %collective-permute-start.1 = (bf16[80,768]{1,0:T(8,128)(2,1)S(1)}, bf16[80,768]{1,0:T(8,128)(2,1)S(1)}, u32[]{:S(2)}, u32[]{:S(2)}) collective-permute-start(bf16[80,768]{1,0:T(8,128)(2,1)S(1)} %get-tuple-element.180), channel_id=1, source_target_pairs={{0,2},{1,3},{2,0},{3,1},{4,6},{5,7},{6,4},{7,5},{8,10},{9,11},{10,... | collective-permute-start | bytes 368648 | tf_op jit(solution)/shard_map/ppermute | solution.py:1234
  8.6 3.6 %buckets.1 = (s32[512,512]{1,0:T(8,128)S(1)}, s32[5,128,128]{2,1,0:T(8,128)S(1)}) custom-call(s32[4]{0:T(128)S(1)} %pad_add_fusion.place_ref, s32[4]{0:T(128)S(1)} %copy-done.30, s32[2,2048]{1,0:T(2,128)} %box_ref.1), custom_call_target="tpu_custom_call" | custom-call | flops 1 | bytes 1 | tf_op jit(solution)/shard_map/buckets/pallas_call | solution.py:100
  12.2 6.0 %attend_forward.2 = (bf16[1,512,192]{2,1,0:T(8,128)(2,1)S(1)}, bf16[1,192,512]{2,1,0:T(8,128)(2,1)S(1)}, bf16[1,3,512,512]{3,2,1,0:T(8,128)(2,1)S(1)}, bf16[1,576,512]{2,1,0:T(8,128)(2,1)S(1)}, f32[1,8,512]{2,1,0:T(8,128)S(1)}) custom-call(s32[4]{0:T(128)S(1)} %pad_add_fusion.place_ref, bf16[512,768]{1,0:T(8,128)(2,1)} %x_ref.11, ...), custom_call_target="tpu_custom_call" | custom-call | flops 1 | bytes 1 | tf_op jit(solution)/shard_map/attend_forward/pallas_call | solution.py:322
  18.4 1.8 collective-permute-start.3
  20.2 1.6 collective-permute-start.5
  21.8 2.5 %collective-permute-done.3 = bf16[3,40,768]{2,1,0:T(8,128)(2,1)S(1)} collective-permute-done((bf16[3,40,768]{2,1,0:T(8,128)(2,1)S(1)}, bf16[3,40,768]{2,1,0:T(8,128)(2,1)S(1)}, u32[]{:S(2)}, u32[]{:S(2)}) %collective-permute-start.3) | collective-permute-done | bytes 184352 | tf_op jit(solution)/shard_map/ppermute | solution.py:1229
  24.4 1.6 collective-permute-start.4
  26.1 1.6 collective-permute-start.6
  27.7 5.7 %collective-permute-done.4 = bf16[2,3,40,768]{3,2,1,0:T(8,128)(2,1)S(1)} collective-permute-done((bf16[2,3,40,768]{3,2,1,0:T(8,128)(2,1)S(1)}, bf16[2,3,40,768]{3,2,1,0:T(8,128)(2,1)S(1)}, u32[]{:S(2)}, u32[]{:S(2)}) %collective-permute-start.4) | collective-permute-done | bytes 368672 | tf_op jit(solution)/shard_map/ppermute | solution.py:1229
  34.3 2.3 %collective-permute-done.8.refs_3_ = bf16[2,2,3,32,768]{4,3,2,1,0:T(8,128)(2,1)S(1)} collective-permute-done((bf16[2,2,3,32,768]{4,3,2,1,0:T(8,128)(2,1)S(1)}, bf16[2,2,3,32,768]{4,3,2,1,0:T(8,128)(2,1)S(1)}, u32[]{:S(2)}, u32[]{:S(2)}) %collective-permute-start.8) | collective-permute-done | bytes 589856 | tf_op jit(solution)/shard_map/ppermute | solution.py:1229
  36.5 14.3 %attend_forward.3 = (bf16[3,576,768]{2,1,0:T(8,128)(2,1)}, bf16[3,512,192]{2,1,0:T(8,128)(2,1)S(1)}, bf16[3,192,512]{2,1,0:T(8,128)(2,1)}, bf16[3,3,512,512]{3,2...) custom-call(s32[4]{0:T(128)S(1)} %pad_add_fusion.place_ref, bf16[512,768]{1,0:T(8,128)(2,1)S(1)} %copy-done, ...), custom_call_target="tpu_custom_call" | custom-call | flops 1 | bytes 1 | tf_op jit(solution)/shard_map/attend_forward/pallas_call | solution.py:322
  51.5 17.6 %feed_up.1 = (bf16[512,768]{1,0:T(8,128)(2,1)}, f32[512,768]{1,0:T(8,128)S(1)}, bf16[512,768]{1,0:T(8,128)(2,1)S(1)}, bf16[3072,512]{1,0:T(8,128)(2,1)S(1)}, bf1...) custom-call(s32[4]{0:T(128)S(1)} %pad_add_fusion.place_ref, ...), custom_call_target="tpu_custom_call" | custom-call | flops 1 | bytes 1 | tf_op jit(solution)/shard_map/feed_up/pallas_call | solution.py:672
  69.1 2.5 %back_weights.1 = bf16[1536,768]{1,0:T(8,128)(2,1)S(1)} custom-call(s32[4]{0:T(128)S(1)} %pad_add_fusion.place_ref, bf16[3072,512]{1,0:T(8,128)(2,1)S(1)} %get-tuple-element.191.left_ref, bf16[512,768]{1,0:T(8,128)(2,1)S(1)} %get-tuple-element.194.right_ref.branch_ref), custom_call_target="tpu_custom_call" | custom-call | flops 1 | bytes 1 | tf_op jit(solution)/shard_map/back_weights/pallas_call | solution.py:888
  71.9 4.4 %collective-permute-done.9.got_ref = bf16[4,384,768]{2,1,0:T(8,128)(2,1)S(1)} collective-permute-done((bf16[4,384,768]{2,1,0:T(8,128)(2,1)S(1)}, bf16[4,384,768]{2,1,0:T(8,128)(2,1)S(1)}, u32[]{:S(2)}, u32[]{:S(2)}) %collective-permute-start.9) | collective-permute-done | bytes 2359328 | tf_op jit(solution)/shard_map/ppermute | solution.py:1229
  76.3 2.9 %kept_weights.1 = (bf16[2,192,768]{2,1,0:T(8,128)(2,1)S(1)}, bf16[2,192,768]{2,1,0:T(8,128)(2,1)S(1)}, bf16[2,192,768]{2,1,0:T(8,128)(2,1)S(1)}, bf16[2,192,768]{2,1,0:T(8,128)(2,1)S(1)}) custom-call(s32[4]{0:T(128)S(1)} %pad_add_fusion.place_ref, bf16[3072,512]{1,0:T(8,128)(2,1)S(1)} %get-tuple-element.191.left_ref, ...), custom_call_target="tpu_custom_call" | custom-call | flops 1 | bytes 1 | tf_op jit(solution)/shard_map/kept_weights/pallas_call | solution.py:932
  80.2 1.5 collective-permute-start.11
  82.5 16.1 %feed_down.1 = (f32[8,3072]{1,0:T(8,128)S(1)}, f32[512,768]{1,0:T(8,128)S(1)}, bf16[1,192,512]{2,1,0:T(8,128)(2,1)S(1)}, bf16[3,192,512]{2,1,0:T(8,128)(2,1)S(1)...) custom-call(s32[4]{0:T(128)S(1)} %copy-done.17, ...), custom_call_target="tpu_custom_call" | custom-call | flops 1 | bytes 1 | tf_op jit(solution)/shard_map/feed_down/pallas_call | solution.py:841
  101.6 6.1 %attend_backward.3 = (f32[512,768]{1,0:T(8,128)S(1)}, bf16[1,3,512,512]{3,2,1,0:T(8,128)(2,1)S(1)}, f32[1,1,576]{2,1,0:T(1,128)S(1)}, bf16[1,4,72,768]{3,2,1,0:T(8,128)(2,1)S(1)}, bf16[1,4,72,768]{3,2,1,0:T(8,128)(2,1)S(1)}) custom-call(s32[4]{0:T(128)S(1)} %copy-done.18, bf16[512,768]{1,0:T(8,128)(2,1)S(1)} %copy-done, bf16[1,576,768]{2,1,0:T(8,128)(2,1)S(1)} %bitcast.87, ...), custom_call_target="tpu_custom_call" | custom-call | flops 1 | bytes 1 | tf_op jit(solution)/shard_map/attend_backward/pallas_call | solution.py:437
  107.7 1.7 collective-permute-done.13.a_got
  109.5 1.9 sum_chips.3
  113.5 1.4 collective-permute-start.17
  115.0 1.5 collective-permute-start.18
  116.5 4.7 %attend_backward.4 = (f32[512,768]{1,0:T(8,128)S(1)}, bf16[1,3,512,512]{3,2,1,0:T(8,128)(2,1)S(1)}, f32[1,1,576]{2,1,0:T(1,128)S(1)}, bf16[1,4,72,768]{3,2,1,0:T(8,128)(2,1)S(1)}, bf16[1,4,72,768]{3,2,1,0:T(8,128)(2,1)S(1)}) custom-call(s32[4]{0:T(128)S(1)} %copy-done.18, bf16[512,768]{1,0:T(8,128)(2,1)S(1)} %copy-done, bf16[3,576,768]{2,1,0:T(8,128)(2,1)S(1)} %copy-done.2, ...), custom_call_target="tpu_custom_call" | custom-call | flops 1 | bytes 1 | tf_op jit(solution)/shard_map/attend_backward/pallas_call | solution.py:437
  122.4 2.4 %collective-permute-start.19 = (bf16[96,768]{1,0:T(8,128)(2,1)S(1)}, bf16[96,768]{1,0:T(8,128)(2,1)S(1)}, u32[]{:S(2)}, u32[]{:S(2)}) collective-permute-start(bf16[96,768]{1,0:T(8,128)(2,1)S(1)} %slice_bitcast_fusion.1), channel_id=1, source_target_pairs={{0,2},{1,3},{2,0},{3,1},{4,6},{5,7},{6,4},{7,5},{8,10},{9,11},{10,... | collective-permute-start | bytes 442376 | tf_op jit(solution)/shard_map/ppermute | solution.py:1234
  124.8 9.1 %attend_backward.5 = (f32[512,768]{1,0:T(8,128)S(1)}, bf16[2,3,512,512]{3,2,1,0:T(8,128)(2,1)S(1)}, f32[2,1,576]{2,1,0:T(1,128)S(1)}, bf16[2,4,72,768]{3,2,1,0:T(8,128)(2,1)S(1)}, bf16[2,4,72,768]{3,2,1,0:T(8,128)(2,1)S(1)}) custom-call(s32[4]{0:T(128)S(1)} %copy-done.18, bf16[512,768]{1,0:T(8,128)(2,1)S(1)} %copy-done, bf16[3,576,768]{2,1,0:T(8,128)(2,1)S(1)} %copy-done.2, ...), custom_call_target="tpu_custom_call" | custom-call | flops 1 | bytes 1 | tf_op jit(solution)/shard_map/attend_backward/pallas_call | solution.py:437
  134.0 1.3 sum_pairs.4
  135.6 1.5 collective-permute-start.22
  138.3 2.0 collective-permute-start.24
  140.3 6.2 %table_products.2.refs_4_ = f32[96,512]{1,0:T(8,128)S(1)} custom-call(bf16[1,3,512,512]{3,2,1,0:T(8,128)(2,1)S(1)} %get-tuple-element.255.refs_0_, bf16[1,3,512,512]{3,2,1,0:T(8,128)(2,1)S(1)} %get-tuple-element.256.refs_1_, bf16[2,3,512,512]{3,2,1,0:T(8,128)(2,1)S(1)} %get-tuple-element.257.refs_2_, ...), custom_call_target="tpu_custom_call" | custom-call | flops 1 | bytes 1 | tf_op jit(solution)/shard_map/table_products/pallas_call | solution.py:496
  152.5 1.8 collective-permute-start.27
  155.1 6.2 %table_products.3.refs_0_ = f32[96,512]{1,0:T(8,128)S(1)} custom-call(bf16[1,3,512,512]{3,2,1,0:T(8,128)(2,1)S(1)} %get-tuple-element.255.refs_0_, bf16[1,3,512,512]{3,2,1,0:T(8,128)(2,1)S(1)} %get-tuple-element.256.refs_1_, bf16[2,3,512,512]{3,2,1,0:T(8,128)(2,1)S(1)} %get-tuple-element.257.refs_2_, ...), custom_call_target="tpu_custom_call" | custom-call | flops 1 | bytes 1 | tf_op jit(solution)/shard_map/table_products/pallas_call | solution.py:496
  161.3 1.6 collective-permute-start.31
  163.0 1.3 collective-permute-done.28
  164.3 1.4 sum_pairs.5
  165.7 1.5 collective-permute-start.29
  168.6 2.4 %collective-permute-start.36 = (bf16[24,1920]{1,0:T(8,128)(2,1)S(1)}, bf16[24,1920]{1,0:T(8,128)(2,1)S(1)}, u32[]{:S(2)}, u32[]{:S(2)}) collective-permute-start(bf16[24,1920]{1,0:T(8,128)(2,1)S(1)} %slice_bitcast_fusion.3), channel_id=1, source_target_pairs={{0,1},{1,0},{2,3},{3,2},{4,5},{5,4},{6,7},{7,6},{8,9},{9,8},{10,11... | collective-permute-start | bytes 276488 | tf_op jit(solution)/shard_map/ppermute | solution.py:1234
  173.4 2.5 %collective-permute-start.33 = (bf16[88,768]{1,0:T(8,128)(2,1)S(1)}, bf16[88,768]{1,0:T(8,128)(2,1)S(1)}, u32[]{:S(2)}, u32[]{:S(2)}) collective-permute-start(bf16[88,768]{1,0:T(8,128)(2,1)S(1)} %get-tuple-element.308), channel_id=1, source_target_pairs={{0,2},{1,3},{2,0},{3,1},{4,6},{5,7},{6,4},{7,5},{8,10},{9,11},{10,... | collective-permute-start | bytes 405512 | tf_op jit(solution)/shard_map/ppermute | solution.py:1234
  175.9 1.9 collective-permute-start.34
  177.8 1.6 join_quarters.2
  179.4 2.5 %collective-permute-start.40 = (bf16[24,1920]{1,0:T(8,128)(2,1)S(1)}, bf16[24,1920]{1,0:T(8,128)(2,1)S(1)}, u32[]{:S(2)}, u32[]{:S(2)}) collective-permute-start(bf16[24,1920]{1,0:T(8,128)(2,1)S(1)} %fusion.1.refs_3_), channel_id=1, source_target_pairs={{0,1},{1,0},{2,3},{3,2},{4,5},{5,4},{6,7},{7,6},{8,9},{9,8},{10,11... | collective-permute-start | bytes 276488 | tf_op jit(solution)/shard_map/ppermute | solution.py:1234
  181.9 4.8 %collective-permute-done.33 = bf16[88,768]{1,0:T(8,128)(2,1)S(1)} collective-permute-done((bf16[88,768]{1,0:T(8,128)(2,1)S(1)}, bf16[88,768]{1,0:T(8,128)(2,1)S(1)}, u32[]{:S(2)}, u32[]{:S(2)}) %collective-permute-start.33) | collective-permute-done | bytes 135200 | tf_op jit(solution)/shard_map/ppermute | solution.py:1234
  187.7 1.4 collective-permute-start.38
  189.6 2.1 %collective-permute-start.46 = (bf16[2,24,1920]{2,1,0:T(8,128)(2,1)S(1)}, bf16[2,24,1920]{2,1,0:T(8,128)(2,1)S(1)}, u32[]{:S(2)}, u32[]{:S(2)}) collective-permute-start(bf16[2,24,1920]{2,1,0:T(8,128)(2,1)S(1)} %pad_maximum_fusion.8), channel_id=1, source_target_pairs={{0,1},{1,0},{2,3},{3,2},{4,5},{5,4},{6,7},{7,6},{8,9},{9,8},{10,11... | collective-permute-start | bytes 552968 | tf_op jit(solution)/shard_map/ppermute | solution.py:1234
  195.1 2.5 %collective-permute-done.41 = bf16[2,40,768]{2,1,0:T(8,128)(2,1)S(1)} collective-permute-done((bf16[2,40,768]{2,1,0:T(8,128)(2,1)S(1)}, bf16[2,40,768]{2,1,0:T(8,128)(2,1)S(1)}, u32[]{:S(2)}, u32[]{:S(2)}) %collective-permute-start.41) | collective-permute-done | bytes 122912 | tf_op jit(solution)/shard_map/ppermute | solution.py:1229
  200.5 1.7 join_quarters.3
  202.2 1.9 join_chips.1
  (191 shorter events, 31.1 us)
Async XLA Ops:
  2.3 16.0 %collective-permute-start = (bf16[80,768]{1,0:T(8,128)(2,1)S(1)}, bf16[80,768]{1,0:T(8,128)(2,1)S(1)}, u32[]{:S(2)}, u32[]{:S(2)}) collective-permute-start(bf16[80,768]{1,0:T(8,128)(2,1)S(1)} %get-tuple-element.180), channel_id=1, source_target_pairs={{0,1},{1,0},{2,3},{3,2},{4,5},{5,4},{6,7},{7,6},{8,9},{9,8},{10,11... | collective-permute-start | bytes 368648 | tf_op jit(solution)/shard_map/ppermute | solution.py:1234
  5.3 13.0 %collective-permute-start.1 = (bf16[80,768]{1,0:T(8,128)(2,1)S(1)}, bf16[80,768]{1,0:T(8,128)(2,1)S(1)}, u32[]{:S(2)}, u32[]{:S(2)}) collective-permute-start(bf16[80,768]{1,0:T(8,128)(2,1)S(1)} %get-tuple-element.180), channel_id=1, source_target_pairs={{0,2},{1,3},{2,0},{3,1},{4,6},{5,7},{6,4},{7,5},{8,10},{9,11},{10,... | collective-permute-start | bytes 368648 | tf_op jit(solution)/shard_map/ppermute | solution.py:1234
  7.9 10.4 %collective-permute-start.2 = (bf16[80,768]{1,0:T(8,128)(2,1)S(1)}, bf16[80,768]{1,0:T(8,128)(2,1)S(1)}, u32[]{:S(2)}, u32[]{:S(2)}) collective-permute-start(bf16[80,768]{1,0:T(8,128)(2,1)S(1)} %get-tuple-element.180), channel_id=1, source_target_pairs={{0,3},{1,2},{2,1},{3,0},{4,7},{5,6},{6,5},{7,4},{8,11},{9,10},{10,... | collective-permute-start | bytes 368648 | tf_op jit(solution)/shard_map/ppermute | solution.py:1234
  18.4 5.9 %collective-permute-start.3 = (bf16[3,40,768]{2,1,0:T(8,128)(2,1)S(1)}, bf16[3,40,768]{2,1,0:T(8,128)(2,1)S(1)}, u32[]{:S(2)}, u32[]{:S(2)}) collective-permute-start(bf16[3,40,768]{2,1,0:T(8,128)(2,1)S(1)} %get-tuple-element.342), channel_id=1, source_target_pairs={{0,8},{4,12},{8,0},{12,4},{16,24},{20,28},{24,16},{28,20},{1,9},{5... | collective-permute-start | bytes 552968 | tf_op jit(solution)/shard_map/ppermute | solution.py:1229
  20.2 5.7 %collective-permute-start.5 = (bf16[3,32,768]{2,1,0:T(8,128)(2,1)S(1)}, bf16[3,32,768]{2,1,0:T(8,128)(2,1)S(1)}, u32[]{:S(2)}, u32[]{:S(2)}) collective-permute-start(bf16[3,32,768]{2,1,0:T(8,128)(2,1)S(1)} %get-tuple-element.338), channel_id=1, source_target_pairs={{0,16},{4,20},{8,24},{12,28},{16,0},{20,4},{24,8},{28,12},{1,17},{... | collective-permute-start | bytes 442376 | tf_op jit(solution)/shard_map/ppermute | solution.py:1229
  24.4 9.0 %collective-permute-start.4 = (bf16[2,3,40,768]{3,2,1,0:T(8,128)(2,1)S(1)}, bf16[2,3,40,768]{3,2,1,0:T(8,128)(2,1)S(1)}, u32[]{:S(2)}, u32[]{:S(2)}) collective-permute-start(bf16[2,3,40,768]{3,2,1,0:T(8,128)(2,1)S(1)} %get-tuple-element.340), channel_id=1, source_target_pairs={{0,16},{4,20},{8,24},{12,28},{16,0},{20,4},{24,8},{28,12},{1,17},{... | collective-permute-start | bytes 1105928 | tf_op jit(solution)/shard_map/ppermute | solution.py:1229
  26.1 7.4 %collective-permute-start.6 = (bf16[2,3,32,768]{3,2,1,0:T(8,128)(2,1)S(1)}, bf16[2,3,32,768]{3,2,1,0:T(8,128)(2,1)S(1)}, u32[]{:S(2)}, u32[]{:S(2)}) collective-permute-start(bf16[2,3,32,768]{3,2,1,0:T(8,128)(2,1)S(1)} %get-tuple-element.344), channel_id=1, source_target_pairs={{0,8},{4,12},{8,0},{12,4},{16,24},{20,28},{24,16},{28,20},{1,9},{5... | collective-permute-start | bytes 884744 | tf_op jit(solution)/shard_map/ppermute | solution.py:1229
  33.4 3.1 %collective-permute-start.7 = (bf16[2,2,3,40,768]{4,3,2,1,0:T(8,128)(2,1)S(1)}, bf16[2,2,3,40,768]{4,3,2,1,0:T(8,128)(2,1)S(1)}, u32[]{:S(2)}, u32[]{:S(2)}) collective-permute-start(bf16[2,2,3,40,768]{4,3,2,1,0:T(8,128)(2,1)S(1)} %pad_maximum_fusion.refs_0_), channel_id=1, source_target_pairs={{0,4},{4,0},{8,12},{12,8},{16,20},{20,16},{24,28},{28,24},{1,5},{5... | collective-permute-start | bytes 2211848 | tf_op jit(solution)/shard_map/ppermute | solution.py:1229
  33.6 3.0 %collective-permute-start.8 = (bf16[2,2,3,32,768]{4,3,2,1,0:T(8,128)(2,1)S(1)}, bf16[2,2,3,32,768]{4,3,2,1,0:T(8,128)(2,1)S(1)}, u32[]{:S(2)}, u32[]{:S(2)}) collective-permute-start(bf16[2,2,3,32,768]{4,3,2,1,0:T(8,128)(2,1)S(1)} %pad_maximum_fusion.1.refs_1_), channel_id=1, source_target_pairs={{0,4},{4,0},{8,12},{12,8},{16,20},{20,16},{24,28},{28,24},{1,5},{5... | collective-permute-start | bytes 1769480 | tf_op jit(solution)/shard_map/ppermute | solution.py:1229
  71.7 4.6 %collective-permute-start.9 = (bf16[4,384,768]{2,1,0:T(8,128)(2,1)S(1)}, bf16[4,384,768]{2,1,0:T(8,128)(2,1)S(1)}, u32[]{:S(2)}, u32[]{:S(2)}) collective-permute-start(bf16[4,384,768]{2,1,0:T(8,128)(2,1)S(1)} %bitcast.92), channel_id=1, source_target_pairs={{0,4},{4,0},{8,12},{12,8},{16,20},{20,16},{24,28},{28,24},{1,5},{5... | collective-permute-start | bytes 7077896 | tf_op jit(solution)/shard_map/ppermute | solution.py:1229
  79.2 19.3 %collective-permute-start.10 = (bf16[2,192,768]{2,1,0:T(8,128)(2,1)S(1)}, bf16[2,192,768]{2,1,0:T(8,128)(2,1)S(1)}, u32[]{:S(2)}, u32[]{:S(2)}) collective-permute-start(bf16[2,192,768]{2,1,0:T(8,128)(2,1)S(1)} %get-tuple-element.192), channel_id=1, source_target_pairs={{0,8},{4,12},{8,0},{12,4},{16,24},{20,28},{24,16},{28,20},{1,9},{5... | collective-permute-start | bytes 1769480 | tf_op jit(solution)/shard_map/ppermute | solution.py:1229
  80.2 18.3 %collective-permute-start.11 = (bf16[2,192,768]{2,1,0:T(8,128)(2,1)S(1)}, bf16[2,192,768]{2,1,0:T(8,128)(2,1)S(1)}, u32[]{:S(2)}, u32[]{:S(2)}) collective-permute-start(bf16[2,192,768]{2,1,0:T(8,128)(2,1)S(1)} %get-tuple-element.193), channel_id=1, source_target_pairs={{0,16},{4,20},{8,24},{12,28},{16,0},{20,4},{24,8},{28,12},{1,17},{... | collective-permute-start | bytes 1769480 | tf_op jit(solution)/shard_map/ppermute | solution.py:1229
  99.8 9.7 %collective-permute-start.12 = (bf16[4,96,3840]{2,1,0:T(8,128)(2,1)}, bf16[4,96,3840]{2,1,0:T(8,128)(2,1)S(1)}, u32[]{:S(2)}, u32[]{:S(2)}) collective-permute-start(bf16[4,96,3840]{2,1,0:T(8,128)(2,1)} %get-tuple-element.212), channel_id=1, source_target_pairs={{0,4},{4,0},{8,12},{12,8},{16,20},{20,16},{24,28},{28,24},{1,5},{5... | collective-permute-start | bytes 8847368 | tf_op jit(solution)/shard_map/ppermute | solution.py:1229
  99.9 9.4 %collective-permute-start.13 = (bf16[192,768]{1,0:T(8,128)(2,1)S(1)}, bf16[192,768]{1,0:T(8,128)(2,1)S(1)}, u32[]{:S(2)}, u32[]{:S(2)}) collective-permute-start(bf16[192,768]{1,0:T(8,128)(2,1)S(1)} %get-tuple-element.211), channel_id=1, source_target_pairs={{0,16},{4,20},{8,24},{12,28},{16,0},{20,4},{24,8},{28,12},{1,17},{... | collective-permute-start | bytes 884744 | tf_op jit(solution)/shard_map/ppermute | solution.py:1229
  100.5 9.1 %collective-permute-start.14 = (bf16[192,768]{1,0:T(8,128)(2,1)S(1)}, bf16[192,768]{1,0:T(8,128)(2,1)S(1)}, u32[]{:S(2)}, u32[]{:S(2)}) collective-permute-start(bf16[192,768]{1,0:T(8,128)(2,1)S(1)} %get-tuple-element.213), channel_id=1, source_target_pairs={{0,8},{4,12},{8,0},{12,4},{16,24},{20,28},{24,16},{28,20},{1,9},{5... | collective-permute-start | bytes 884744 | tf_op jit(solution)/shard_map/ppermute | solution.py:1229
  112.8 9.5 %collective-permute-start.15 = (bf16[1,4,72,768]{3,2,1,0:T(8,128)(2,1)S(1)}, bf16[1,4,72,768]{3,2,1,0:T(8,128)(2,1)S(1)}, u32[]{:S(2)}, u32[]{:S(2)}) collective-permute-start(bf16[1,4,72,768]{3,2,1,0:T(8,128)(2,1)S(1)} %get-tuple-element.230), channel_id=1, source_target_pairs={{0,4},{4,0},{8,12},{12,8},{16,20},{20,16},{24,28},{28,24},{1,5},{5... | collective-permute-start | bytes 1327112 | tf_op jit(solution)/shard_map/ppermute | solution.py:1229
  112.8 9.4 %collective-permute-start.16 = (bf16[2,96,768]{2,1,0:T(8,128)(2,1)S(1)}, bf16[2,96,768]{2,1,0:T(8,128)(2,1)S(1)}, u32[]{:S(2)}, u32[]{:S(2)}) collective-permute-start(bf16[2,96,768]{2,1,0:T(8,128)(2,1)S(1)} %get-tuple-element.227), channel_id=1, source_target_pairs={{0,1},{1,0},{2,3},{3,2},{4,5},{5,4},{6,7},{7,6},{8,9},{9,8},{10,11... | collective-permute-start | bytes 884744 | tf_op jit(solution)/shard_map/ppermute | solution.py:1234
  113.5 20.5 %collective-permute-start.17 = (bf16[2,48,3840]{2,1,0:T(8,128)(2,1)S(1)}, bf16[2,48,3840]{2,1,0:T(8,128)(2,1)S(1)}, u32[]{:S(2)}, u32[]{:S(2)}) collective-permute-start(bf16[2,48,3840]{2,1,0:T(8,128)(2,1)S(1)} %get-tuple-element.228), channel_id=1, source_target_pairs={{0,8},{4,12},{8,0},{12,4},{16,24},{20,28},{24,16},{28,20},{1,9},{5... | collective-permute-start | bytes 2211848 | tf_op jit(solution)/shard_map/ppermute | solution.py:1229
  115.0 19.0 %collective-permute-start.18 = (bf16[2,48,3840]{2,1,0:T(8,128)(2,1)S(1)}, bf16[2,48,3840]{2,1,0:T(8,128)(2,1)S(1)}, u32[]{:S(2)}, u32[]{:S(2)}) collective-permute-start(bf16[2,48,3840]{2,1,0:T(8,128)(2,1)S(1)} %get-tuple-element.229), channel_id=1, source_target_pairs={{0,16},{4,20},{8,24},{12,28},{16,0},{20,4},{24,8},{28,12},{1,17},{... | collective-permute-start | bytes 2211848 | tf_op jit(solution)/shard_map/ppermute | solution.py:1229
  122.3 11.7 %collective-permute-start.20 = (bf16[1,4,72,768]{3,2,1,0:T(8,128)(2,1)S(1)}, bf16[1,4,72,768]{3,2,1,0:T(8,128)(2,1)S(1)}, u32[]{:S(2)}, u32[]{:S(2)}) collective-permute-start(bf16[1,4,72,768]{3,2,1,0:T(8,128)(2,1)S(1)} %get-tuple-element.236), channel_id=1, source_target_pairs={{0,4},{4,0},{8,12},{12,8},{16,20},{20,16},{24,28},{28,24},{1,5},{5... | collective-permute-start | bytes 1327112 | tf_op jit(solution)/shard_map/ppermute | solution.py:1229
  122.4 11.5 %collective-permute-start.19 = (bf16[96,768]{1,0:T(8,128)(2,1)S(1)}, bf16[96,768]{1,0:T(8,128)(2,1)S(1)}, u32[]{:S(2)}, u32[]{:S(2)}) collective-permute-start(bf16[96,768]{1,0:T(8,128)(2,1)S(1)} %slice_bitcast_fusion.1), channel_id=1, source_target_pairs={{0,2},{1,3},{2,0},{3,1},{4,6},{5,7},{6,4},{7,5},{8,10},{9,11},{10,... | collective-permute-start | bytes 442376 | tf_op jit(solution)/shard_map/ppermute | solution.py:1234
  135.3 12.5 %collective-permute-start.21 = (bf16[2,4,72,768]{3,2,1,0:T(8,128)(2,1)S(1)}, bf16[2,4,72,768]{3,2,1,0:T(8,128)(2,1)S(1)}, u32[]{:S(2)}, u32[]{:S(2)}) collective-permute-start(bf16[2,4,72,768]{3,2,1,0:T(8,128)(2,1)S(1)} %get-tuple-element.251), channel_id=1, source_target_pairs={{0,4},{4,0},{8,12},{12,8},{16,20},{20,16},{24,28},{28,24},{1,5},{5... | collective-permute-start | bytes 2654216 | tf_op jit(solution)/shard_map/ppermute | solution.py:1229
  135.6 12.2 %collective-permute-start.22 = (bf16[48,3840]{1,0:T(8,128)(2,1)S(1)}, bf16[48,3840]{1,0:T(8,128)(2,1)S(1)}, u32[]{:S(2)}, u32[]{:S(2)}) collective-permute-start(bf16[48,3840]{1,0:T(8,128)(2,1)S(1)} %get-tuple-element.252), channel_id=1, source_target_pairs={{0,16},{4,20},{8,24},{12,28},{16,0},{20,4},{24,8},{28,12},{1,17},{... | collective-permute-start | bytes 1105928 | tf_op jit(solution)/shard_map/ppermute | solution.py:1229
  137.2 10.7 %collective-permute-start.23 = (bf16[48,3840]{1,0:T(8,128)(2,1)S(1)}, bf16[48,3840]{1,0:T(8,128)(2,1)S(1)}, u32[]{:S(2)}, u32[]{:S(2)}) collective-permute-start(bf16[48,3840]{1,0:T(8,128)(2,1)S(1)} %get-tuple-element.253), channel_id=1, source_target_pairs={{0,8},{4,12},{8,0},{12,4},{16,24},{20,28},{24,16},{28,20},{1,9},{5... | collective-permute-start | bytes 1105928 | tf_op jit(solution)/shard_map/ppermute | solution.py:1229
  138.3 9.5 %collective-permute-start.24 = (bf16[96,768]{1,0:T(8,128)(2,1)S(1)}, bf16[96,768]{1,0:T(8,128)(2,1)S(1)}, u32[]{:S(2)}, u32[]{:S(2)}) collective-permute-start(bf16[96,768]{1,0:T(8,128)(2,1)S(1)} %fusion.refs_0_), channel_id=1, source_target_pairs={{0,2},{1,3},{2,0},{3,1},{4,6},{5,7},{6,4},{7,5},{8,10},{9,11},{10,... | collective-permute-start | bytes 442376 | tf_op jit(solution)/shard_map/ppermute | solution.py:1234
  151.0 13.3 %collective-permute-start.25 = (bf16[2,144,768]{2,1,0:T(8,128)(2,1)S(1)}, bf16[2,144,768]{2,1,0:T(8,128)(2,1)S(1)}, u32[]{:S(2)}, u32[]{:S(2)}) collective-permute-start(bf16[2,144,768]{2,1,0:T(8,128)(2,1)S(1)} %get-tuple-element.276), channel_id=1, source_target_pairs={{0,8},{4,12},{8,0},{12,4},{16,24},{20,28},{24,16},{28,20},{1,9},{5... | collective-permute-start | bytes 1327112 | tf_op jit(solution)/shard_map/ppermute | solution.py:1229
  152.0 12.3 %collective-permute-start.26 = (bf16[2,144,768]{2,1,0:T(8,128)(2,1)S(1)}, bf16[2,144,768]{2,1,0:T(8,128)(2,1)S(1)}, u32[]{:S(2)}, u32[]{:S(2)}) collective-permute-start(bf16[2,144,768]{2,1,0:T(8,128)(2,1)S(1)} %get-tuple-element.277), channel_id=1, source_target_pairs={{0,16},{4,20},{8,24},{12,28},{16,0},{20,4},{24,8},{28,12},{1,17},{... | collective-permute-start | bytes 1327112 | tf_op jit(solution)/shard_map/ppermute | solution.py:1229
  152.5 10.5 %collective-permute-start.27 = (bf16[2,24,1920]{2,1,0:T(8,128)(2,1)S(1)}, bf16[2,24,1920]{2,1,0:T(8,128)(2,1)S(1)}, u32[]{:S(2)}, u32[]{:S(2)}) collective-permute-start(bf16[2,24,1920]{2,1,0:T(8,128)(2,1)S(1)} %get-tuple-element.278), channel_id=1, source_target_pairs={{0,1},{1,0},{2,3},{3,2},{4,5},{5,4},{6,7},{7,6},{8,9},{9,8},{10,11... | collective-permute-start | bytes 552968 | tf_op jit(solution)/shard_map/ppermute | solution.py:1234
  154.3 10.0 %collective-permute-start.28 = (bf16[2,24,1920]{2,1,0:T(8,128)(2,1)S(1)}, bf16[2,24,1920]{2,1,0:T(8,128)(2,1)S(1)}, u32[]{:S(2)}, u32[]{:S(2)}) collective-permute-start(bf16[2,24,1920]{2,1,0:T(8,128)(2,1)S(1)} %get-tuple-element.279), channel_id=1, source_target_pairs={{0,2},{1,3},{2,0},{3,1},{4,6},{5,7},{6,4},{7,5},{8,10},{9,11},{10,... | collective-permute-start | bytes 552968 | tf_op jit(solution)/shard_map/ppermute | solution.py:1234
  161.3 10.8 %collective-permute-start.31 = (bf16[2,96,768]{2,1,0:T(8,128)(2,1)S(1)}, bf16[2,96,768]{2,1,0:T(8,128)(2,1)S(1)}, u32[]{:S(2)}, u32[]{:S(2)}) collective-permute-start(bf16[2,96,768]{2,1,0:T(8,128)(2,1)S(1)} %pad_maximum_fusion.5), channel_id=1, source_target_pairs={{0,1},{1,0},{2,3},{3,2},{4,5},{5,4},{6,7},{7,6},{8,9},{9,8},{10,11... | collective-permute-start | bytes 884744 | tf_op jit(solution)/shard_map/ppermute | solution.py:1234
  165.7 6.4 %collective-permute-start.29 = (bf16[144,768]{1,0:T(8,128)(2,1)S(1)}, bf16[144,768]{1,0:T(8,128)(2,1)S(1)}, u32[]{:S(2)}, u32[]{:S(2)}) collective-permute-start(bf16[144,768]{1,0:T(8,128)(2,1)S(1)} %get-tuple-element.291), channel_id=1, source_target_pairs={{0,16},{4,20},{8,24},{12,28},{16,0},{20,4},{24,8},{28,12},{1,17},{... | collective-permute-start | bytes 663560 | tf_op jit(solution)/shard_map/ppermute | solution.py:1229
  167.2 5.9 %collective-permute-start.30 = (bf16[144,768]{1,0:T(8,128)(2,1)S(1)}, bf16[144,768]{1,0:T(8,128)(2,1)S(1)}, u32[]{:S(2)}, u32[]{:S(2)}) collective-permute-start(bf16[144,768]{1,0:T(8,128)(2,1)S(1)} %get-tuple-element.292), channel_id=1, source_target_pairs={{0,8},{4,12},{8,0},{12,4},{16,24},{20,28},{24,16},{28,20},{1,9},{5... | collective-permute-start | bytes 663560 | tf_op jit(solution)/shard_map/ppermute | solution.py:1229
  168.1 9.7 %collective-permute-start.35 = (bf16[24,1920]{1,0:T(8,128)(2,1)S(1)}, bf16[24,1920]{1,0:T(8,128)(2,1)S(1)}, u32[]{:S(2)}, u32[]{:S(2)}) collective-permute-start(bf16[24,1920]{1,0:T(8,128)(2,1)S(1)} %slice_bitcast_fusion.4), channel_id=1, source_target_pairs={{0,2},{1,3},{2,0},{3,1},{4,6},{5,7},{6,4},{7,5},{8,10},{9,11},{10,... | collective-permute-start | bytes 276488 | tf_op jit(solution)/shard_map/ppermute | solution.py:1234
  168.6 9.1 %collective-permute-start.36 = (bf16[24,1920]{1,0:T(8,128)(2,1)S(1)}, bf16[24,1920]{1,0:T(8,128)(2,1)S(1)}, u32[]{:S(2)}, u32[]{:S(2)}) collective-permute-start(bf16[24,1920]{1,0:T(8,128)(2,1)S(1)} %slice_bitcast_fusion.3), channel_id=1, source_target_pairs={{0,1},{1,0},{2,3},{3,2},{4,5},{5,4},{6,7},{7,6},{8,9},{9,8},{10,11... | collective-permute-start | bytes 276488 | tf_op jit(solution)/shard_map/ppermute | solution.py:1234
  173.3 8.7 %collective-permute-start.32 = (bf16[88,768]{1,0:T(8,128)(2,1)S(1)}, bf16[88,768]{1,0:T(8,128)(2,1)S(1)}, u32[]{:S(2)}, u32[]{:S(2)}) collective-permute-start(bf16[88,768]{1,0:T(8,128)(2,1)S(1)} %get-tuple-element.307), channel_id=1, source_target_pairs={{0,1},{1,0},{2,3},{3,2},{4,5},{5,4},{6,7},{7,6},{8,9},{9,8},{10,11... | collective-permute-start | bytes 405512 | tf_op jit(solution)/shard_map/ppermute | solution.py:1234
  173.4 13.4 %collective-permute-start.33 = (bf16[88,768]{1,0:T(8,128)(2,1)S(1)}, bf16[88,768]{1,0:T(8,128)(2,1)S(1)}, u32[]{:S(2)}, u32[]{:S(2)}) collective-permute-start(bf16[88,768]{1,0:T(8,128)(2,1)S(1)} %get-tuple-element.308), channel_id=1, source_target_pairs={{0,2},{1,3},{2,0},{3,1},{4,6},{5,7},{6,4},{7,5},{8,10},{9,11},{10,... | collective-permute-start | bytes 405512 | tf_op jit(solution)/shard_map/ppermute | solution.py:1234
  175.9 10.9 %collective-permute-start.34 = (bf16[88,768]{1,0:T(8,128)(2,1)S(1)}, bf16[88,768]{1,0:T(8,128)(2,1)S(1)}, u32[]{:S(2)}, u32[]{:S(2)}) collective-permute-start(bf16[88,768]{1,0:T(8,128)(2,1)S(1)} %get-tuple-element.309), channel_id=1, source_target_pairs={{0,3},{1,2},{2,1},{3,0},{4,7},{5,6},{6,5},{7,4},{8,11},{9,10},{10,... | collective-permute-start | bytes 405512 | tf_op jit(solution)/shard_map/ppermute | solution.py:1234
  179.4 10.2 %collective-permute-start.39 = (bf16[24,1920]{1,0:T(8,128)(2,1)S(1)}, bf16[24,1920]{1,0:T(8,128)(2,1)S(1)}, u32[]{:S(2)}, u32[]{:S(2)}) collective-permute-start(bf16[24,1920]{1,0:T(8,128)(2,1)S(1)} %fusion.2.refs_0_), channel_id=1, source_target_pairs={{0,2},{1,3},{2,0},{3,1},{4,6},{5,7},{6,4},{7,5},{8,10},{9,11},{10,... | collective-permute-start | bytes 276488 | tf_op jit(solution)/shard_map/ppermute | solution.py:1234
  179.4 10.2 %collective-permute-start.40 = (bf16[24,1920]{1,0:T(8,128)(2,1)S(1)}, bf16[24,1920]{1,0:T(8,128)(2,1)S(1)}, u32[]{:S(2)}, u32[]{:S(2)}) collective-permute-start(bf16[24,1920]{1,0:T(8,128)(2,1)S(1)} %fusion.1.refs_3_), channel_id=1, source_target_pairs={{0,1},{1,0},{2,3},{3,2},{4,5},{5,4},{6,7},{7,6},{8,9},{9,8},{10,11... | collective-permute-start | bytes 276488 | tf_op jit(solution)/shard_map/ppermute | solution.py:1234
  186.9 5.7 %collective-permute-start.37 = (bf16[40,768]{1,0:T(8,128)(2,1)S(1)}, bf16[40,768]{1,0:T(8,128)(2,1)S(1)}, u32[]{:S(2)}, u32[]{:S(2)}) collective-permute-start(bf16[40,768]{1,0:T(8,128)(2,1)S(1)} %get-tuple-element.350), channel_id=1, source_target_pairs={{0,8},{4,12},{8,0},{12,4},{16,24},{20,28},{24,16},{28,20},{1,9},{5... | collective-permute-start | bytes 184328 | tf_op jit(solution)/shard_map/ppermute | solution.py:1229
  187.7 4.9 %collective-permute-start.38 = (bf16[48,768]{1,0:T(8,128)(2,1)S(1)}, bf16[48,768]{1,0:T(8,128)(2,1)S(1)}, u32[]{:S(2)}, u32[]{:S(2)}) collective-permute-start(bf16[48,768]{1,0:T(8,128)(2,1)S(1)} %pad_maximum_fusion.12), channel_id=1, source_target_pairs={{0,16},{4,20},{8,24},{12,28},{16,0},{20,4},{24,8},{28,12},{1,17},{... | collective-permute-start | bytes 221192 | tf_op jit(solution)/shard_map/ppermute | solution.py:1229
  189.6 10.8 %collective-permute-start.46 = (bf16[2,24,1920]{2,1,0:T(8,128)(2,1)S(1)}, bf16[2,24,1920]{2,1,0:T(8,128)(2,1)S(1)}, u32[]{:S(2)}, u32[]{:S(2)}) collective-permute-start(bf16[2,24,1920]{2,1,0:T(8,128)(2,1)S(1)} %pad_maximum_fusion.8), channel_id=1, source_target_pairs={{0,1},{1,0},{2,3},{3,2},{4,5},{5,4},{6,7},{7,6},{8,9},{9,8},{10,11... | collective-permute-start | bytes 552968 | tf_op jit(solution)/shard_map/ppermute | solution.py:1234
  191.8 8.7 %collective-permute-start.47 = (bf16[2,24,1920]{2,1,0:T(8,128)(2,1)S(1)}, bf16[2,24,1920]{2,1,0:T(8,128)(2,1)S(1)}, u32[]{:S(2)}, u32[]{:S(2)}) collective-permute-start(bf16[2,24,1920]{2,1,0:T(8,128)(2,1)S(1)} %pad_maximum_fusion.9), channel_id=1, source_target_pairs={{0,2},{1,3},{2,0},{3,1},{4,6},{5,7},{6,4},{7,5},{8,10},{9,11},{10,... | collective-permute-start | bytes 552968 | tf_op jit(solution)/shard_map/ppermute | solution.py:1234
  192.6 4.9 %collective-permute-start.41 = (bf16[2,40,768]{2,1,0:T(8,128)(2,1)S(1)}, bf16[2,40,768]{2,1,0:T(8,128)(2,1)S(1)}, u32[]{:S(2)}, u32[]{:S(2)}) collective-permute-start(bf16[2,40,768]{2,1,0:T(8,128)(2,1)S(1)} %get-tuple-element.346), channel_id=1, source_target_pairs={{0,16},{4,20},{8,24},{12,28},{16,0},{20,4},{24,8},{28,12},{1,17},{... | collective-permute-start | bytes 368648 | tf_op jit(solution)/shard_map/ppermute | solution.py:1229
  193.9 4.9 %collective-permute-start.42 = (bf16[2,40,768]{2,1,0:T(8,128)(2,1)S(1)}, bf16[2,40,768]{2,1,0:T(8,128)(2,1)S(1)}, u32[]{:S(2)}, u32[]{:S(2)}) collective-permute-start(bf16[2,40,768]{2,1,0:T(8,128)(2,1)S(1)} %pad_maximum_fusion.11), channel_id=1, source_target_pairs={{0,8},{4,12},{8,0},{12,4},{16,24},{20,28},{24,16},{28,20},{1,9},{5... | collective-permute-start | bytes 368648 | tf_op jit(solution)/shard_map/ppermute | solution.py:1229
  197.6 4.6 %collective-permute-start.43 = (bf16[2,2,40,768]{3,2,1,0:T(8,128)(2,1)S(1)}, bf16[2,2,40,768]{3,2,1,0:T(8,128)(2,1)S(1)}, u32[]{:S(2)}, u32[]{:S(2)}) collective-permute-start(bf16[2,2,40,768]{3,2,1,0:T(8,128)(2,1)S(1)} %pad_maximum_fusion.6.mine_a), channel_id=1, source_target_pairs={{0,4},{4,0},{8,12},{12,8},{16,20},{20,16},{24,28},{28,24},{1,5},{5... | collective-permute-start | bytes 737288 | tf_op jit(solution)/shard_map/ppermute | solution.py:1229
  198.9 3.4 %collective-permute-start.44 = (bf16[2,2,32,768]{3,2,1,0:T(8,128)(2,1)S(1)}, bf16[2,2,32,768]{3,2,1,0:T(8,128)(2,1)S(1)}, u32[]{:S(2)}, u32[]{:S(2)}) collective-permute-start(bf16[2,2,32,768]{3,2,1,0:T(8,128)(2,1)S(1)} %pad_maximum_fusion.7.mine_b), channel_id=1, source_target_pairs={{0,4},{4,0},{8,12},{12,8},{16,20},{20,16},{24,28},{28,24},{1,5},{5... | collective-permute-start | bytes 589832 | tf_op jit(solution)/shard_map/ppermute | solution.py:1229
  199.0 3.3 %collective-permute-start.45 = (bf16[16,768]{1,0:T(8,128)(2,1)S(1)}, bf16[16,768]{1,0:T(8,128)(2,1)S(1)}, u32[]{:S(2)}, u32[]{:S(2)}) collective-permute-start(bf16[16,768]{1,0:T(8,128)(2,1)S(1)} %fusion.3.ends_ref), channel_id=1, source_target_pairs={{0,4},{4,0},{8,12},{12,8},{16,20},{20,16},{24,28},{28,24},{1,5},{5... | collective-permute-start | bytes 73736 | tf_op jit(solution)/shard_map/ppermute | solution.py:1229
  (37 other events, 377.2 us)

commit v3 on v2

--- a/solution.py
+++ b/solution.py
@@ -453,7 +453,7 @@
         ),
         out_shape=out_shape,
         name="attend_backward",
-        compiler_params=limit(26),
+        compiler_params=limit(30),
         cost_estimate=HINT,
     )(place, x, w, qkv, raised, inverse, grad, start)
 
@@ -1456,7 +1456,8 @@
         dense = [total_of(item[0], got) for item, got in zip(dense, dense_got)]
         dense_one = [away(dense[0], 2), away(dense[1], 1)]
         (out_back,) = join_quarters(place, [(back, back_one, back_two)], ((2, 1, 3),), (width,))
-        last_got = tie(last_got, dense, out_back)
+        grad_input = dx.astype(BF)
+        last_got = tie(last_got, dense, out_back, grad_input)
         quarter = total_of(last[0][:small], *[item[:small] for item in last_got])
         ends = tree([item[small:].astype(F32) for item in [last[0]] + last_got]).astype(BF)
         first, second = quarter[:cut], quarter[cut:]
@@ -1520,6 +1521,7 @@
         full = spread_docs(sum_heads([blocks[s] for s in range(groups)]))
         full = full.reshape(columns, width).astype(F32)
 
+        grad_input = dx.astype(BF)
         mine = lambda vector: lax.dynamic_slice_in_dim(
             vector, docs * (vector.shape[0] // count), vector.shape[0] // count
         )
@@ -1529,7 +1531,7 @@
         grad_inner = mine(total[6:begin].reshape(-1))
     return (
         layer_output,
-        dx.astype(BF),
+        grad_input,
         full.reshape(3, own, width).transpose(2, 0, 1),
         grad_bias,
         grad_tables,

time: 205 us -> 203 us (level)
  transfers between devices with their start and end apart: 48 -> 48, of which waited for: 14 -> 15; matrix products, arithmetic and copies ran while one was open for 1% -> 1% of each run, Pallas kernels for 31% -> 31%
where the time goes in v3:
time: 203 us
  Pallas kernels  113 us (56%)
  starting transfers between devices  54.4 us (27%)
  waiting for transfers between devices  30.3 us (15%)
  other arithmetic  2.43 us (1%)
    ppermute x18, starting transfers between devices, away(): lax.ppermute(array, 'heads', [(i, i ^ distance) for i in range(count)])  27.6 us
    ppermute x30, starting transfers between devices, swap(): lax.ppermute(array, 'docs', [(i, i ^ 1 << bit) for i in range(count)])  26.8 us
    ppermute x30, waiting for transfers between devices, swap(): lax.ppermute(array, 'docs', [(i, i ^ 1 << bit) for i in range(count)])  20.4 us
    pallas_call x2, Pallas kernels, attend_forward(): pl.pallas_call(functools.partial(forward_kernel, gathered), grid_spec=plt...  20.4 us
    pallas_call x3, Pallas kernels, attend_backward(): pl.pallas_call(functools.partial(backward_kernel, bool(halves)), grid_spe...  20 us
    pallas_call x1, Pallas kernels, feed_up(): pl.pallas_call(up_kernel, grid_spec=pltpu.PrefetchScalarGridSpec(num_scal...  17.6 us
    pallas_call x1, Pallas kernels, feed_down(): pl.pallas_call(functools.partial(down_kernel, bool(halves)), grid_spec=pl...  15.5 us
    pallas_call x2, Pallas kernels, table_products(): pl.pallas_call(functools.partial(table_kernel, skip), grid=(steps,), in_s...  12.4 us
  transfers between devices with their start and end apart: 48, of which 15 were waited for; matrix products, arithmetic and copies ran while one was open for 1% of the time, Pallas kernels for 31%

profile of v3, /device:TPU:0, one launch (start us, length us, event | category | flops | bytes accessed | tf_op | source)
XLA Modules:
  0.0 202.6 jit_solution(7568595243512545451)
XLA Ops:
  0.7 1.6 first_piece.1
  2.3 3.0 %collective-permute-start = (bf16[80,768]{1,0:T(8,128)(2,1)S(1)}, bf16[80,768]{1,0:T(8,128)(2,1)S(1)}, u32[]{:S(2)}, u32[]{:S(2)}) collective-permute-start(bf16[80,768]{1,0:T(8,128)(2,1)S(1)} %get-tuple-element.180), channel_id=1, source_target_pairs={{0,1},{1,0},{2,3},{3,2},{4,5},{5,4},{6,7},{7,6},{8,9},{9,8},{10,11... | collective-permute-start | bytes 368648 | tf_op jit(solution)/shard_map/ppermute | solution.py:1234
  5.3 2.6 %collective-permute-start.1 = (bf16[80,768]{1,0:T(8,128)(2,1)S(1)}, bf16[80,768]{1,0:T(8,128)(2,1)S(1)}, u32[]{:S(2)}, u32[]{:S(2)}) collective-permute-start(bf16[80,768]{1,0:T(8,128)(2,1)S(1)} %get-tuple-element.180), channel_id=1, source_target_pairs={{0,2},{1,3},{2,0},{3,1},{4,6},{5,7},{6,4},{7,5},{8,10},{9,11},{10,... | collective-permute-start | bytes 368648 | tf_op jit(solution)/shard_map/ppermute | solution.py:1234
  8.6 3.6 %buckets.1 = (s32[512,512]{1,0:T(8,128)S(1)}, s32[5,128,128]{2,1,0:T(8,128)S(1)}) custom-call(s32[4]{0:T(128)S(1)} %pad_add_fusion.place_ref, s32[4]{0:T(128)S(1)} %copy-done.19, s32[2,2048]{1,0:T(2,128)} %box_ref.1), custom_call_target="tpu_custom_call" | custom-call | flops 1 | bytes 1 | tf_op jit(solution)/shard_map/buckets/pallas_call | solution.py:100
  12.2 6.0 %attend_forward.2 = (bf16[1,512,192]{2,1,0:T(8,128)(2,1)S(1)}, bf16[1,192,512]{2,1,0:T(8,128)(2,1)S(1)}, bf16[1,3,512,512]{3,2,1,0:T(8,128)(2,1)S(1)}, bf16[1,576,512]{2,1,0:T(8,128)(2,1)S(1)}, f32[1,8,512]{2,1,0:T(8,128)S(1)}) custom-call(s32[4]{0:T(128)S(1)} %pad_add_fusion.place_ref, bf16[512,768]{1,0:T(8,128)(2,1)} %x_ref.11, ...), custom_call_target="tpu_custom_call" | custom-call | flops 1 | bytes 1 | tf_op jit(solution)/shard_map/attend_forward/pallas_call | solution.py:322
  18.4 1.8 collective-permute-start.3
  20.2 1.6 collective-permute-start.5
  21.8 2.5 %collective-permute-done.3 = bf16[3,40,768]{2,1,0:T(8,128)(2,1)S(1)} collective-permute-done((bf16[3,40,768]{2,1,0:T(8,128)(2,1)S(1)}, bf16[3,40,768]{2,1,0:T(8,128)(2,1)S(1)}, u32[]{:S(2)}, u32[]{:S(2)}) %collective-permute-start.3) | collective-permute-done | bytes 184352 | tf_op jit(solution)/shard_map/ppermute | solution.py:1229
  24.3 1.6 collective-permute-start.4
  26.1 1.6 collective-permute-start.6
  27.6 5.7 %collective-permute-done.4 = bf16[2,3,40,768]{3,2,1,0:T(8,128)(2,1)S(1)} collective-permute-done((bf16[2,3,40,768]{3,2,1,0:T(8,128)(2,1)S(1)}, bf16[2,3,40,768]{3,2,1,0:T(8,128)(2,1)S(1)}, u32[]{:S(2)}, u32[]{:S(2)}) %collective-permute-start.4) | collective-permute-done | bytes 368672 | tf_op jit(solution)/shard_map/ppermute | solution.py:1229
  34.2 2.3 %collective-permute-done.8.refs_3_ = bf16[2,2,3,32,768]{4,3,2,1,0:T(8,128)(2,1)S(1)} collective-permute-done((bf16[2,2,3,32,768]{4,3,2,1,0:T(8,128)(2,1)S(1)}, bf16[2,2,3,32,768]{4,3,2,1,0:T(8,128)(2,1)S(1)}, u32[]{:S(2)}, u32[]{:S(2)}) %collective-permute-start.8) | collective-permute-done | bytes 589856 | tf_op jit(solution)/shard_map/ppermute | solution.py:1229
  36.5 14.3 %attend_forward.3 = (bf16[3,576,768]{2,1,0:T(8,128)(2,1)}, bf16[3,512,192]{2,1,0:T(8,128)(2,1)S(1)}, bf16[3,192,512]{2,1,0:T(8,128)(2,1)}, bf16[3,3,512,512]{3,2...) custom-call(s32[4]{0:T(128)S(1)} %pad_add_fusion.place_ref, bf16[512,768]{1,0:T(8,128)(2,1)S(1)} %copy-done, ...), custom_call_target="tpu_custom_call" | custom-call | flops 1 | bytes 1 | tf_op jit(solution)/shard_map/attend_forward/pallas_call | solution.py:322
  50.9 17.6 %feed_up.1 = (bf16[512,768]{1,0:T(8,128)(2,1)}, f32[512,768]{1,0:T(8,128)S(1)}, bf16[512,768]{1,0:T(8,128)(2,1)S(1)}, bf16[3072,512]{1,0:T(8,128)(2,1)S(1)}, bf1...) custom-call(s32[4]{0:T(128)S(1)} %pad_add_fusion.place_ref, ...), custom_call_target="tpu_custom_call" | custom-call | flops 1 | bytes 1 | tf_op jit(solution)/shard_map/feed_up/pallas_call | solution.py:672
  68.5 2.5 %back_weights.1 = bf16[1536,768]{1,0:T(8,128)(2,1)S(1)} custom-call(s32[4]{0:T(128)S(1)} %pad_add_fusion.place_ref, bf16[3072,512]{1,0:T(8,128)(2,1)S(1)} %get-tuple-element.191.left_ref, bf16[512,768]{1,0:T(8,128)(2,1)S(1)} %get-tuple-element.194.right_ref.branch_ref), custom_call_target="tpu_custom_call" | custom-call | flops 1 | bytes 1 | tf_op jit(solution)/shard_map/back_weights/pallas_call | solution.py:888
  71.2 4.4 %collective-permute-done.9.got_ref = bf16[4,384,768]{2,1,0:T(8,128)(2,1)S(1)} collective-permute-done((bf16[4,384,768]{2,1,0:T(8,128)(2,1)S(1)}, bf16[4,384,768]{2,1,0:T(8,128)(2,1)S(1)}, u32[]{:S(2)}, u32[]{:S(2)}) %collective-permute-start.9) | collective-permute-done | bytes 2359328 | tf_op jit(solution)/shard_map/ppermute | solution.py:1229
  75.6 2.9 %kept_weights.1 = (bf16[2,192,768]{2,1,0:T(8,128)(2,1)S(1)}, bf16[2,192,768]{2,1,0:T(8,128)(2,1)S(1)}, bf16[2,192,768]{2,1,0:T(8,128)(2,1)S(1)}, bf16[2,192,768]{2,1,0:T(8,128)(2,1)S(1)}) custom-call(s32[4]{0:T(128)S(1)} %pad_add_fusion.place_ref, bf16[3072,512]{1,0:T(8,128)(2,1)S(1)} %get-tuple-element.191.left_ref, ...), custom_call_target="tpu_custom_call" | custom-call | flops 1 | bytes 1 | tf_op jit(solution)/shard_map/kept_weights/pallas_call | solution.py:932
  79.5 1.5 collective-permute-start.11
  81.1 15.5 %feed_down.1 = (f32[8,3072]{1,0:T(8,128)S(1)}, f32[512,768]{1,0:T(8,128)S(1)}, bf16[1,192,512]{2,1,0:T(8,128)(2,1)S(1)}, bf16[3,192,512]{2,1,0:T(8,128)(2,1)S(1)...) custom-call(s32[4]{0:T(128)S(1)} %pad_add_fusion.place_ref, ...), custom_call_target="tpu_custom_call" | custom-call | flops 1 | bytes 1 | tf_op jit(solution)/shard_map/feed_down/pallas_call | solution.py:841
  99.6 6.1 %attend_backward.3 = (f32[512,768]{1,0:T(8,128)S(1)}, bf16[1,3,512,512]{3,2,1,0:T(8,128)(2,1)S(1)}, f32[1,1,576]{2,1,0:T(1,128)S(1)}, bf16[1,4,72,768]{3,2,1,0:T(8,128)(2,1)S(1)}, bf16[1,4,72,768]{3,2,1,0:T(8,128)(2,1)S(1)}) custom-call(s32[4]{0:T(128)S(1)} %pad_add_fusion.place_ref, bf16[512,768]{1,0:T(8,128)(2,1)S(1)} %copy-done, ...), custom_call_target="tpu_custom_call" | custom-call | flops 1 | bytes 1 | tf_op jit(solution)/shard_map/attend_backward/pallas_call | solution.py:437
  105.8 1.6 collective-permute-done.13.a_got
  107.6 1.9 sum_chips.3
  111.6 1.5 collective-permute-start.17
  113.1 1.5 collective-permute-start.18
  114.6 4.7 %attend_backward.4 = (f32[512,768]{1,0:T(8,128)S(1)}, bf16[1,3,512,512]{3,2,1,0:T(8,128)(2,1)S(1)}, f32[1,1,576]{2,1,0:T(1,128)S(1)}, bf16[1,4,72,768]{3,2,1,0:T(8,128)(2,1)S(1)}, bf16[1,4,72,768]{3,2,1,0:T(8,128)(2,1)S(1)}) custom-call(s32[4]{0:T(128)S(1)} %pad_add_fusion.place_ref, bf16[512,768]{1,0:T(8,128)(2,1)S(1)} %copy-done, ...), custom_call_target="tpu_custom_call" | custom-call | flops 1 | bytes 1 | tf_op jit(solution)/shard_map/attend_backward/pallas_call | solution.py:437
  120.5 2.4 %collective-permute-start.19 = (bf16[96,768]{1,0:T(8,128)(2,1)S(1)}, bf16[96,768]{1,0:T(8,128)(2,1)S(1)}, u32[]{:S(2)}, u32[]{:S(2)}) collective-permute-start(bf16[96,768]{1,0:T(8,128)(2,1)S(1)} %slice_bitcast_fusion.1), channel_id=1, source_target_pairs={{0,2},{1,3},{2,0},{3,1},{4,6},{5,7},{6,4},{7,5},{8,10},{9,11},{10,... | collective-permute-start | bytes 442376 | tf_op jit(solution)/shard_map/ppermute | solution.py:1234
  122.9 9.1 %attend_backward.5 = (f32[512,768]{1,0:T(8,128)S(1)}, bf16[2,3,512,512]{3,2,1,0:T(8,128)(2,1)S(1)}, f32[2,1,576]{2,1,0:T(1,128)S(1)}, bf16[2,4,72,768]{3,2,1,0:T(8,128)(2,1)S(1)}, bf16[2,4,72,768]{3,2,1,0:T(8,128)(2,1)S(1)}) custom-call(s32[4]{0:T(128)S(1)} %pad_add_fusion.place_ref, bf16[512,768]{1,0:T(8,128)(2,1)S(1)} %copy-done, ...), custom_call_target="tpu_custom_call" | custom-call | flops 1 | bytes 1 | tf_op jit(solution)/shard_map/attend_backward/pallas_call | solution.py:437
  132.2 1.3 sum_pairs.4
  133.7 1.5 collective-permute-start.22
  136.4 2.0 collective-permute-start.24
  138.4 6.2 %table_products.2.refs_4_ = f32[96,512]{1,0:T(8,128)S(1)} custom-call(bf16[1,3,512,512]{3,2,1,0:T(8,128)(2,1)S(1)} %get-tuple-element.255.refs_0_, bf16[1,3,512,512]{3,2,1,0:T(8,128)(2,1)S(1)} %get-tuple-element.256.refs_1_, bf16[2,3,512,512]{3,2,1,0:T(8,128)(2,1)S(1)} %get-tuple-element.257.refs_2_, ...), custom_call_target="tpu_custom_call" | custom-call | flops 1 | bytes 1 | tf_op jit(solution)/shard_map/table_products/pallas_call | solution.py:496
  144.6 1.3 collective-permute-done.24.refs_1_
  150.6 1.8 collective-permute-start.27
  153.2 6.2 %table_products.3.refs_0_ = f32[96,512]{1,0:T(8,128)S(1)} custom-call(bf16[1,3,512,512]{3,2,1,0:T(8,128)(2,1)S(1)} %get-tuple-element.255.refs_0_, bf16[1,3,512,512]{3,2,1,0:T(8,128)(2,1)S(1)} %get-tuple-element.256.refs_1_, bf16[2,3,512,512]{3,2,1,0:T(8,128)(2,1)S(1)} %get-tuple-element.257.refs_2_, ...), custom_call_target="tpu_custom_call" | custom-call | flops 1 | bytes 1 | tf_op jit(solution)/shard_map/table_products/pallas_call | solution.py:496
  159.4 1.6 collective-permute-start.31
  162.3 1.4 sum_pairs.5
  163.8 1.5 collective-permute-start.29
  166.7 2.4 %collective-permute-start.36 = (bf16[24,1920]{1,0:T(8,128)(2,1)S(1)}, bf16[24,1920]{1,0:T(8,128)(2,1)S(1)}, u32[]{:S(2)}, u32[]{:S(2)}) collective-permute-start(bf16[24,1920]{1,0:T(8,128)(2,1)S(1)} %slice_bitcast_fusion.3), channel_id=1, source_target_pairs={{0,1},{1,0},{2,3},{3,2},{4,5},{5,4},{6,7},{7,6},{8,9},{9,8},{10,11... | collective-permute-start | bytes 276488 | tf_op jit(solution)/shard_map/ppermute | solution.py:1234
  171.4 2.5 %collective-permute-start.33 = (bf16[88,768]{1,0:T(8,128)(2,1)S(1)}, bf16[88,768]{1,0:T(8,128)(2,1)S(1)}, u32[]{:S(2)}, u32[]{:S(2)}) collective-permute-start(bf16[88,768]{1,0:T(8,128)(2,1)S(1)} %get-tuple-element.308), channel_id=1, source_target_pairs={{0,2},{1,3},{2,0},{3,1},{4,6},{5,7},{6,4},{7,5},{8,10},{9,11},{10,... | collective-permute-start | bytes 405512 | tf_op jit(solution)/shard_map/ppermute | solution.py:1234
  173.9 1.9 collective-permute-start.34
  175.9 1.6 join_quarters.2
  177.5 2.5 %collective-permute-start.40 = (bf16[24,1920]{1,0:T(8,128)(2,1)S(1)}, bf16[24,1920]{1,0:T(8,128)(2,1)S(1)}, u32[]{:S(2)}, u32[]{:S(2)}) collective-permute-start(bf16[24,1920]{1,0:T(8,128)(2,1)S(1)} %fusion.1.refs_3_), channel_id=1, source_target_pairs={{0,1},{1,0},{2,3},{3,2},{4,5},{5,4},{6,7},{7,6},{8,9},{9,8},{10,11... | collective-permute-start | bytes 276488 | tf_op jit(solution)/shard_map/ppermute | solution.py:1234
  180.0 4.8 %collective-permute-done.33 = bf16[88,768]{1,0:T(8,128)(2,1)S(1)} collective-permute-done((bf16[88,768]{1,0:T(8,128)(2,1)S(1)}, bf16[88,768]{1,0:T(8,128)(2,1)S(1)}, u32[]{:S(2)}, u32[]{:S(2)}) %collective-permute-start.33) | collective-permute-done | bytes 135200 | tf_op jit(solution)/shard_map/ppermute | solution.py:1234
  185.8 1.3 collective-permute-start.38
  187.8 2.1 %collective-permute-start.46 = (bf16[2,24,1920]{2,1,0:T(8,128)(2,1)S(1)}, bf16[2,24,1920]{2,1,0:T(8,128)(2,1)S(1)}, u32[]{:S(2)}, u32[]{:S(2)}) collective-permute-start(bf16[2,24,1920]{2,1,0:T(8,128)(2,1)S(1)} %pad_maximum_fusion.8), channel_id=1, source_target_pairs={{0,1},{1,0},{2,3},{3,2},{4,5},{5,4},{6,7},{7,6},{8,9},{9,8},{10,11... | collective-permute-start | bytes 552968 | tf_op jit(solution)/shard_map/ppermute | solution.py:1234
  193.2 2.4 %collective-permute-done.41 = bf16[2,40,768]{2,1,0:T(8,128)(2,1)S(1)} collective-permute-done((bf16[2,40,768]{2,1,0:T(8,128)(2,1)S(1)}, bf16[2,40,768]{2,1,0:T(8,128)(2,1)S(1)}, u32[]{:S(2)}, u32[]{:S(2)}) %collective-permute-start.41) | collective-permute-done | bytes 122912 | tf_op jit(solution)/shard_map/ppermute | solution.py:1229
  198.4 1.7 join_quarters.3
  200.1 1.9 join_chips.1
  (169 shorter events, 29.7 us)
Async XLA Ops:
  2.3 16.0 %collective-permute-start = (bf16[80,768]{1,0:T(8,128)(2,1)S(1)}, bf16[80,768]{1,0:T(8,128)(2,1)S(1)}, u32[]{:S(2)}, u32[]{:S(2)}) collective-permute-start(bf16[80,768]{1,0:T(8,128)(2,1)S(1)} %get-tuple-element.180), channel_id=1, source_target_pairs={{0,1},{1,0},{2,3},{3,2},{4,5},{5,4},{6,7},{7,6},{8,9},{9,8},{10,11... | collective-permute-start | bytes 368648 | tf_op jit(solution)/shard_map/ppermute | solution.py:1234
  5.3 13.0 %collective-permute-start.1 = (bf16[80,768]{1,0:T(8,128)(2,1)S(1)}, bf16[80,768]{1,0:T(8,128)(2,1)S(1)}, u32[]{:S(2)}, u32[]{:S(2)}) collective-permute-start(bf16[80,768]{1,0:T(8,128)(2,1)S(1)} %get-tuple-element.180), channel_id=1, source_target_pairs={{0,2},{1,3},{2,0},{3,1},{4,6},{5,7},{6,4},{7,5},{8,10},{9,11},{10,... | collective-permute-start | bytes 368648 | tf_op jit(solution)/shard_map/ppermute | solution.py:1234
  7.9 10.4 %collective-permute-start.2 = (bf16[80,768]{1,0:T(8,128)(2,1)S(1)}, bf16[80,768]{1,0:T(8,128)(2,1)S(1)}, u32[]{:S(2)}, u32[]{:S(2)}) collective-permute-start(bf16[80,768]{1,0:T(8,128)(2,1)S(1)} %get-tuple-element.180), channel_id=1, source_target_pairs={{0,3},{1,2},{2,1},{3,0},{4,7},{5,6},{6,5},{7,4},{8,11},{9,10},{10,... | collective-permute-start | bytes 368648 | tf_op jit(solution)/shard_map/ppermute | solution.py:1234
  18.4 5.9 %collective-permute-start.3 = (bf16[3,40,768]{2,1,0:T(8,128)(2,1)S(1)}, bf16[3,40,768]{2,1,0:T(8,128)(2,1)S(1)}, u32[]{:S(2)}, u32[]{:S(2)}) collective-permute-start(bf16[3,40,768]{2,1,0:T(8,128)(2,1)S(1)} %get-tuple-element.342), channel_id=1, source_target_pairs={{0,8},{4,12},{8,0},{12,4},{16,24},{20,28},{24,16},{28,20},{1,9},{5... | collective-permute-start | bytes 552968 | tf_op jit(solution)/shard_map/ppermute | solution.py:1229
  20.2 5.7 %collective-permute-start.5 = (bf16[3,32,768]{2,1,0:T(8,128)(2,1)S(1)}, bf16[3,32,768]{2,1,0:T(8,128)(2,1)S(1)}, u32[]{:S(2)}, u32[]{:S(2)}) collective-permute-start(bf16[3,32,768]{2,1,0:T(8,128)(2,1)S(1)} %get-tuple-element.338), channel_id=1, source_target_pairs={{0,16},{4,20},{8,24},{12,28},{16,0},{20,4},{24,8},{28,12},{1,17},{... | collective-permute-start | bytes 442376 | tf_op jit(solution)/shard_map/ppermute | solution.py:1229
  24.3 9.0 %collective-permute-start.4 = (bf16[2,3,40,768]{3,2,1,0:T(8,128)(2,1)S(1)}, bf16[2,3,40,768]{3,2,1,0:T(8,128)(2,1)S(1)}, u32[]{:S(2)}, u32[]{:S(2)}) collective-permute-start(bf16[2,3,40,768]{3,2,1,0:T(8,128)(2,1)S(1)} %get-tuple-element.340), channel_id=1, source_target_pairs={{0,16},{4,20},{8,24},{12,28},{16,0},{20,4},{24,8},{28,12},{1,17},{... | collective-permute-start | bytes 1105928 | tf_op jit(solution)/shard_map/ppermute | solution.py:1229
  26.1 7.4 %collective-permute-start.6 = (bf16[2,3,32,768]{3,2,1,0:T(8,128)(2,1)S(1)}, bf16[2,3,32,768]{3,2,1,0:T(8,128)(2,1)S(1)}, u32[]{:S(2)}, u32[]{:S(2)}) collective-permute-start(bf16[2,3,32,768]{3,2,1,0:T(8,128)(2,1)S(1)} %get-tuple-element.344), channel_id=1, source_target_pairs={{0,8},{4,12},{8,0},{12,4},{16,24},{20,28},{24,16},{28,20},{1,9},{5... | collective-permute-start | bytes 884744 | tf_op jit(solution)/shard_map/ppermute | solution.py:1229
  33.4 3.1 %collective-permute-start.7 = (bf16[2,2,3,40,768]{4,3,2,1,0:T(8,128)(2,1)S(1)}, bf16[2,2,3,40,768]{4,3,2,1,0:T(8,128)(2,1)S(1)}, u32[]{:S(2)}, u32[]{:S(2)}) collective-permute-start(bf16[2,2,3,40,768]{4,3,2,1,0:T(8,128)(2,1)S(1)} %pad_maximum_fusion.refs_0_), channel_id=1, source_target_pairs={{0,4},{4,0},{8,12},{12,8},{16,20},{20,16},{24,28},{28,24},{1,5},{5... | collective-permute-start | bytes 2211848 | tf_op jit(solution)/shard_map/ppermute | solution.py:1229
  33.6 3.0 %collective-permute-start.8 = (bf16[2,2,3,32,768]{4,3,2,1,0:T(8,128)(2,1)S(1)}, bf16[2,2,3,32,768]{4,3,2,1,0:T(8,128)(2,1)S(1)}, u32[]{:S(2)}, u32[]{:S(2)}) collective-permute-start(bf16[2,2,3,32,768]{4,3,2,1,0:T(8,128)(2,1)S(1)} %pad_maximum_fusion.1.refs_1_), channel_id=1, source_target_pairs={{0,4},{4,0},{8,12},{12,8},{16,20},{20,16},{24,28},{28,24},{1,5},{5... | collective-permute-start | bytes 1769480 | tf_op jit(solution)/shard_map/ppermute | solution.py:1229
  71.0 4.6 %collective-permute-start.9 = (bf16[4,384,768]{2,1,0:T(8,128)(2,1)S(1)}, bf16[4,384,768]{2,1,0:T(8,128)(2,1)S(1)}, u32[]{:S(2)}, u32[]{:S(2)}) collective-permute-start(bf16[4,384,768]{2,1,0:T(8,128)(2,1)S(1)} %bitcast.92), channel_id=1, source_target_pairs={{0,4},{4,0},{8,12},{12,8},{16,20},{20,16},{24,28},{28,24},{1,5},{5... | collective-permute-start | bytes 7077896 | tf_op jit(solution)/shard_map/ppermute | solution.py:1229
  78.5 18.1 %collective-permute-start.10 = (bf16[2,192,768]{2,1,0:T(8,128)(2,1)S(1)}, bf16[2,192,768]{2,1,0:T(8,128)(2,1)S(1)}, u32[]{:S(2)}, u32[]{:S(2)}) collective-permute-start(bf16[2,192,768]{2,1,0:T(8,128)(2,1)S(1)} %get-tuple-element.192), channel_id=1, source_target_pairs={{0,8},{4,12},{8,0},{12,4},{16,24},{20,28},{24,16},{28,20},{1,9},{5... | collective-permute-start | bytes 1769480 | tf_op jit(solution)/shard_map/ppermute | solution.py:1229
  79.5 17.1 %collective-permute-start.11 = (bf16[2,192,768]{2,1,0:T(8,128)(2,1)S(1)}, bf16[2,192,768]{2,1,0:T(8,128)(2,1)S(1)}, u32[]{:S(2)}, u32[]{:S(2)}) collective-permute-start(bf16[2,192,768]{2,1,0:T(8,128)(2,1)S(1)} %get-tuple-element.193), channel_id=1, source_target_pairs={{0,16},{4,20},{8,24},{12,28},{16,0},{20,4},{24,8},{28,12},{1,17},{... | collective-permute-start | bytes 1769480 | tf_op jit(solution)/shard_map/ppermute | solution.py:1229
  97.9 9.7 %collective-permute-start.12 = (bf16[4,96,3840]{2,1,0:T(8,128)(2,1)S(1)}, bf16[4,96,3840]{2,1,0:T(8,128)(2,1)S(1)}, u32[]{:S(2)}, u32[]{:S(2)}) collective-permute-start(bf16[4,96,3840]{2,1,0:T(8,128)(2,1)S(1)} %get-tuple-element.212), channel_id=1, source_target_pairs={{0,4},{4,0},{8,12},{12,8},{16,20},{20,16},{24,28},{28,24},{1,5},{5... | collective-permute-start | bytes 8847368 | tf_op jit(solution)/shard_map/ppermute | solution.py:1229
  98.0 9.4 %collective-permute-start.13 = (bf16[192,768]{1,0:T(8,128)(2,1)S(1)}, bf16[192,768]{1,0:T(8,128)(2,1)S(1)}, u32[]{:S(2)}, u32[]{:S(2)}) collective-permute-start(bf16[192,768]{1,0:T(8,128)(2,1)S(1)} %get-tuple-element.211), channel_id=1, source_target_pairs={{0,16},{4,20},{8,24},{12,28},{16,0},{20,4},{24,8},{28,12},{1,17},{... | collective-permute-start | bytes 884744 | tf_op jit(solution)/shard_map/ppermute | solution.py:1229
  98.5 9.1 %collective-permute-start.14 = (bf16[192,768]{1,0:T(8,128)(2,1)S(1)}, bf16[192,768]{1,0:T(8,128)(2,1)S(1)}, u32[]{:S(2)}, u32[]{:S(2)}) collective-permute-start(bf16[192,768]{1,0:T(8,128)(2,1)S(1)} %get-tuple-element.213), channel_id=1, source_target_pairs={{0,8},{4,12},{8,0},{12,4},{16,24},{20,28},{24,16},{28,20},{1,9},{5... | collective-permute-start | bytes 884744 | tf_op jit(solution)/shard_map/ppermute | solution.py:1229
  110.8 9.5 %collective-permute-start.15 = (bf16[1,4,72,768]{3,2,1,0:T(8,128)(2,1)S(1)}, bf16[1,4,72,768]{3,2,1,0:T(8,128)(2,1)S(1)}, u32[]{:S(2)}, u32[]{:S(2)}) collective-permute-start(bf16[1,4,72,768]{3,2,1,0:T(8,128)(2,1)S(1)} %get-tuple-element.230), channel_id=1, source_target_pairs={{0,4},{4,0},{8,12},{12,8},{16,20},{20,16},{24,28},{28,24},{1,5},{5... | collective-permute-start | bytes 1327112 | tf_op jit(solution)/shard_map/ppermute | solution.py:1229
  110.9 9.4 %collective-permute-start.16 = (bf16[2,96,768]{2,1,0:T(8,128)(2,1)S(1)}, bf16[2,96,768]{2,1,0:T(8,128)(2,1)S(1)}, u32[]{:S(2)}, u32[]{:S(2)}) collective-permute-start(bf16[2,96,768]{2,1,0:T(8,128)(2,1)S(1)} %get-tuple-element.227), channel_id=1, source_target_pairs={{0,1},{1,0},{2,3},{3,2},{4,5},{5,4},{6,7},{7,6},{8,9},{9,8},{10,11... | collective-permute-start | bytes 884744 | tf_op jit(solution)/shard_map/ppermute | solution.py:1234
  111.6 20.5 %collective-permute-start.17 = (bf16[2,48,3840]{2,1,0:T(8,128)(2,1)S(1)}, bf16[2,48,3840]{2,1,0:T(8,128)(2,1)S(1)}, u32[]{:S(2)}, u32[]{:S(2)}) collective-permute-start(bf16[2,48,3840]{2,1,0:T(8,128)(2,1)S(1)} %get-tuple-element.228), channel_id=1, source_target_pairs={{0,8},{4,12},{8,0},{12,4},{16,24},{20,28},{24,16},{28,20},{1,9},{5... | collective-permute-start | bytes 2211848 | tf_op jit(solution)/shard_map/ppermute | solution.py:1229
  113.1 19.0 %collective-permute-start.18 = (bf16[2,48,3840]{2,1,0:T(8,128)(2,1)S(1)}, bf16[2,48,3840]{2,1,0:T(8,128)(2,1)S(1)}, u32[]{:S(2)}, u32[]{:S(2)}) collective-permute-start(bf16[2,48,3840]{2,1,0:T(8,128)(2,1)S(1)} %get-tuple-element.229), channel_id=1, source_target_pairs={{0,16},{4,20},{8,24},{12,28},{16,0},{20,4},{24,8},{28,12},{1,17},{... | collective-permute-start | bytes 2211848 | tf_op jit(solution)/shard_map/ppermute | solution.py:1229
  120.4 11.7 %collective-permute-start.20 = (bf16[1,4,72,768]{3,2,1,0:T(8,128)(2,1)S(1)}, bf16[1,4,72,768]{3,2,1,0:T(8,128)(2,1)S(1)}, u32[]{:S(2)}, u32[]{:S(2)}) collective-permute-start(bf16[1,4,72,768]{3,2,1,0:T(8,128)(2,1)S(1)} %get-tuple-element.236), channel_id=1, source_target_pairs={{0,4},{4,0},{8,12},{12,8},{16,20},{20,16},{24,28},{28,24},{1,5},{5... | collective-permute-start | bytes 1327112 | tf_op jit(solution)/shard_map/ppermute | solution.py:1229
  120.5 11.6 %collective-permute-start.19 = (bf16[96,768]{1,0:T(8,128)(2,1)S(1)}, bf16[96,768]{1,0:T(8,128)(2,1)S(1)}, u32[]{:S(2)}, u32[]{:S(2)}) collective-permute-start(bf16[96,768]{1,0:T(8,128)(2,1)S(1)} %slice_bitcast_fusion.1), channel_id=1, source_target_pairs={{0,2},{1,3},{2,0},{3,1},{4,6},{5,7},{6,4},{7,5},{8,10},{9,11},{10,... | collective-permute-start | bytes 442376 | tf_op jit(solution)/shard_map/ppermute | solution.py:1234
  133.5 12.5 %collective-permute-start.21 = (bf16[2,4,72,768]{3,2,1,0:T(8,128)(2,1)S(1)}, bf16[2,4,72,768]{3,2,1,0:T(8,128)(2,1)S(1)}, u32[]{:S(2)}, u32[]{:S(2)}) collective-permute-start(bf16[2,4,72,768]{3,2,1,0:T(8,128)(2,1)S(1)} %get-tuple-element.251), channel_id=1, source_target_pairs={{0,4},{4,0},{8,12},{12,8},{16,20},{20,16},{24,28},{28,24},{1,5},{5... | collective-permute-start | bytes 2654216 | tf_op jit(solution)/shard_map/ppermute | solution.py:1229
  133.7 12.3 %collective-permute-start.22 = (bf16[48,3840]{1,0:T(8,128)(2,1)S(1)}, bf16[48,3840]{1,0:T(8,128)(2,1)S(1)}, u32[]{:S(2)}, u32[]{:S(2)}) collective-permute-start(bf16[48,3840]{1,0:T(8,128)(2,1)S(1)} %get-tuple-element.252), channel_id=1, source_target_pairs={{0,16},{4,20},{8,24},{12,28},{16,0},{20,4},{24,8},{28,12},{1,17},{... | collective-permute-start | bytes 1105928 | tf_op jit(solution)/shard_map/ppermute | solution.py:1229
  135.2 10.7 %collective-permute-start.23 = (bf16[48,3840]{1,0:T(8,128)(2,1)S(1)}, bf16[48,3840]{1,0:T(8,128)(2,1)S(1)}, u32[]{:S(2)}, u32[]{:S(2)}) collective-permute-start(bf16[48,3840]{1,0:T(8,128)(2,1)S(1)} %get-tuple-element.253), channel_id=1, source_target_pairs={{0,8},{4,12},{8,0},{12,4},{16,24},{20,28},{24,16},{28,20},{1,9},{5... | collective-permute-start | bytes 1105928 | tf_op jit(solution)/shard_map/ppermute | solution.py:1229
  136.4 9.6 %collective-permute-start.24 = (bf16[96,768]{1,0:T(8,128)(2,1)S(1)}, bf16[96,768]{1,0:T(8,128)(2,1)S(1)}, u32[]{:S(2)}, u32[]{:S(2)}) collective-permute-start(bf16[96,768]{1,0:T(8,128)(2,1)S(1)} %fusion.refs_0_), channel_id=1, source_target_pairs={{0,2},{1,3},{2,0},{3,1},{4,6},{5,7},{6,4},{7,5},{8,10},{9,11},{10,... | collective-permute-start | bytes 442376 | tf_op jit(solution)/shard_map/ppermute | solution.py:1234
  149.1 13.3 %collective-permute-start.25 = (bf16[2,144,768]{2,1,0:T(8,128)(2,1)S(1)}, bf16[2,144,768]{2,1,0:T(8,128)(2,1)S(1)}, u32[]{:S(2)}, u32[]{:S(2)}) collective-permute-start(bf16[2,144,768]{2,1,0:T(8,128)(2,1)S(1)} %get-tuple-element.276), channel_id=1, source_target_pairs={{0,8},{4,12},{8,0},{12,4},{16,24},{20,28},{24,16},{28,20},{1,9},{5... | collective-permute-start | bytes 1327112 | tf_op jit(solution)/shard_map/ppermute | solution.py:1229
  150.1 12.2 %collective-permute-start.26 = (bf16[2,144,768]{2,1,0:T(8,128)(2,1)S(1)}, bf16[2,144,768]{2,1,0:T(8,128)(2,1)S(1)}, u32[]{:S(2)}, u32[]{:S(2)}) collective-permute-start(bf16[2,144,768]{2,1,0:T(8,128)(2,1)S(1)} %get-tuple-element.277), channel_id=1, source_target_pairs={{0,16},{4,20},{8,24},{12,28},{16,0},{20,4},{24,8},{28,12},{1,17},{... | collective-permute-start | bytes 1327112 | tf_op jit(solution)/shard_map/ppermute | solution.py:1229
  150.6 10.4 %collective-permute-start.27 = (bf16[2,24,1920]{2,1,0:T(8,128)(2,1)S(1)}, bf16[2,24,1920]{2,1,0:T(8,128)(2,1)S(1)}, u32[]{:S(2)}, u32[]{:S(2)}) collective-permute-start(bf16[2,24,1920]{2,1,0:T(8,128)(2,1)S(1)} %get-tuple-element.278), channel_id=1, source_target_pairs={{0,1},{1,0},{2,3},{3,2},{4,5},{5,4},{6,7},{7,6},{8,9},{9,8},{10,11... | collective-permute-start | bytes 552968 | tf_op jit(solution)/shard_map/ppermute | solution.py:1234
  152.4 10.0 %collective-permute-start.28 = (bf16[2,24,1920]{2,1,0:T(8,128)(2,1)S(1)}, bf16[2,24,1920]{2,1,0:T(8,128)(2,1)S(1)}, u32[]{:S(2)}, u32[]{:S(2)}) collective-permute-start(bf16[2,24,1920]{2,1,0:T(8,128)(2,1)S(1)} %get-tuple-element.279), channel_id=1, source_target_pairs={{0,2},{1,3},{2,0},{3,1},{4,6},{5,7},{6,4},{7,5},{8,10},{9,11},{10,... | collective-permute-start | bytes 552968 | tf_op jit(solution)/shard_map/ppermute | solution.py:1234
  159.4 11.7 %collective-permute-start.31 = (bf16[2,96,768]{2,1,0:T(8,128)(2,1)S(1)}, bf16[2,96,768]{2,1,0:T(8,128)(2,1)S(1)}, u32[]{:S(2)}, u32[]{:S(2)}) collective-permute-start(bf16[2,96,768]{2,1,0:T(8,128)(2,1)S(1)} %pad_maximum_fusion.5), channel_id=1, source_target_pairs={{0,1},{1,0},{2,3},{3,2},{4,5},{5,4},{6,7},{7,6},{8,9},{9,8},{10,11... | collective-permute-start | bytes 884744 | tf_op jit(solution)/shard_map/ppermute | solution.py:1234
  163.8 7.3 %collective-permute-start.29 = (bf16[144,768]{1,0:T(8,128)(2,1)S(1)}, bf16[144,768]{1,0:T(8,128)(2,1)S(1)}, u32[]{:S(2)}, u32[]{:S(2)}) collective-permute-start(bf16[144,768]{1,0:T(8,128)(2,1)S(1)} %get-tuple-element.291), channel_id=1, source_target_pairs={{0,16},{4,20},{8,24},{12,28},{16,0},{20,4},{24,8},{28,12},{1,17},{... | collective-permute-start | bytes 663560 | tf_op jit(solution)/shard_map/ppermute | solution.py:1229
  165.3 5.9 %collective-permute-start.30 = (bf16[144,768]{1,0:T(8,128)(2,1)S(1)}, bf16[144,768]{1,0:T(8,128)(2,1)S(1)}, u32[]{:S(2)}, u32[]{:S(2)}) collective-permute-start(bf16[144,768]{1,0:T(8,128)(2,1)S(1)} %get-tuple-element.292), channel_id=1, source_target_pairs={{0,8},{4,12},{8,0},{12,4},{16,24},{20,28},{24,16},{28,20},{1,9},{5... | collective-permute-start | bytes 663560 | tf_op jit(solution)/shard_map/ppermute | solution.py:1229
  166.1 9.7 %collective-permute-start.35 = (bf16[24,1920]{1,0:T(8,128)(2,1)S(1)}, bf16[24,1920]{1,0:T(8,128)(2,1)S(1)}, u32[]{:S(2)}, u32[]{:S(2)}) collective-permute-start(bf16[24,1920]{1,0:T(8,128)(2,1)S(1)} %slice_bitcast_fusion.4), channel_id=1, source_target_pairs={{0,2},{1,3},{2,0},{3,1},{4,6},{5,7},{6,4},{7,5},{8,10},{9,11},{10,... | collective-permute-start | bytes 276488 | tf_op jit(solution)/shard_map/ppermute | solution.py:1234
  166.7 9.1 %collective-permute-start.36 = (bf16[24,1920]{1,0:T(8,128)(2,1)S(1)}, bf16[24,1920]{1,0:T(8,128)(2,1)S(1)}, u32[]{:S(2)}, u32[]{:S(2)}) collective-permute-start(bf16[24,1920]{1,0:T(8,128)(2,1)S(1)} %slice_bitcast_fusion.3), channel_id=1, source_target_pairs={{0,1},{1,0},{2,3},{3,2},{4,5},{5,4},{6,7},{7,6},{8,9},{9,8},{10,11... | collective-permute-start | bytes 276488 | tf_op jit(solution)/shard_map/ppermute | solution.py:1234
  171.4 8.7 %collective-permute-start.32 = (bf16[88,768]{1,0:T(8,128)(2,1)S(1)}, bf16[88,768]{1,0:T(8,128)(2,1)S(1)}, u32[]{:S(2)}, u32[]{:S(2)}) collective-permute-start(bf16[88,768]{1,0:T(8,128)(2,1)S(1)} %get-tuple-element.307), channel_id=1, source_target_pairs={{0,1},{1,0},{2,3},{3,2},{4,5},{5,4},{6,7},{7,6},{8,9},{9,8},{10,11... | collective-permute-start | bytes 405512 | tf_op jit(solution)/shard_map/ppermute | solution.py:1234
  171.4 13.4 %collective-permute-start.33 = (bf16[88,768]{1,0:T(8,128)(2,1)S(1)}, bf16[88,768]{1,0:T(8,128)(2,1)S(1)}, u32[]{:S(2)}, u32[]{:S(2)}) collective-permute-start(bf16[88,768]{1,0:T(8,128)(2,1)S(1)} %get-tuple-element.308), channel_id=1, source_target_pairs={{0,2},{1,3},{2,0},{3,1},{4,6},{5,7},{6,4},{7,5},{8,10},{9,11},{10,... | collective-permute-start | bytes 405512 | tf_op jit(solution)/shard_map/ppermute | solution.py:1234
  173.9 10.9 %collective-permute-start.34 = (bf16[88,768]{1,0:T(8,128)(2,1)S(1)}, bf16[88,768]{1,0:T(8,128)(2,1)S(1)}, u32[]{:S(2)}, u32[]{:S(2)}) collective-permute-start(bf16[88,768]{1,0:T(8,128)(2,1)S(1)} %get-tuple-element.309), channel_id=1, source_target_pairs={{0,3},{1,2},{2,1},{3,0},{4,7},{5,6},{6,5},{7,4},{8,11},{9,10},{10,... | collective-permute-start | bytes 405512 | tf_op jit(solution)/shard_map/ppermute | solution.py:1234
  177.5 10.2 %collective-permute-start.39 = (bf16[24,1920]{1,0:T(8,128)(2,1)S(1)}, bf16[24,1920]{1,0:T(8,128)(2,1)S(1)}, u32[]{:S(2)}, u32[]{:S(2)}) collective-permute-start(bf16[24,1920]{1,0:T(8,128)(2,1)S(1)} %fusion.2.refs_0_), channel_id=1, source_target_pairs={{0,2},{1,3},{2,0},{3,1},{4,6},{5,7},{6,4},{7,5},{8,10},{9,11},{10,... | collective-permute-start | bytes 276488 | tf_op jit(solution)/shard_map/ppermute | solution.py:1234
  177.5 10.2 %collective-permute-start.40 = (bf16[24,1920]{1,0:T(8,128)(2,1)S(1)}, bf16[24,1920]{1,0:T(8,128)(2,1)S(1)}, u32[]{:S(2)}, u32[]{:S(2)}) collective-permute-start(bf16[24,1920]{1,0:T(8,128)(2,1)S(1)} %fusion.1.refs_3_), channel_id=1, source_target_pairs={{0,1},{1,0},{2,3},{3,2},{4,5},{5,4},{6,7},{7,6},{8,9},{9,8},{10,11... | collective-permute-start | bytes 276488 | tf_op jit(solution)/shard_map/ppermute | solution.py:1234
  185.0 5.6 %collective-permute-start.37 = (bf16[40,768]{1,0:T(8,128)(2,1)S(1)}, bf16[40,768]{1,0:T(8,128)(2,1)S(1)}, u32[]{:S(2)}, u32[]{:S(2)}) collective-permute-start(bf16[40,768]{1,0:T(8,128)(2,1)S(1)} %get-tuple-element.350), channel_id=1, source_target_pairs={{0,8},{4,12},{8,0},{12,4},{16,24},{20,28},{24,16},{28,20},{1,9},{5... | collective-permute-start | bytes 184328 | tf_op jit(solution)/shard_map/ppermute | solution.py:1229
  185.8 4.8 %collective-permute-start.38 = (bf16[48,768]{1,0:T(8,128)(2,1)S(1)}, bf16[48,768]{1,0:T(8,128)(2,1)S(1)}, u32[]{:S(2)}, u32[]{:S(2)}) collective-permute-start(bf16[48,768]{1,0:T(8,128)(2,1)S(1)} %pad_maximum_fusion.12), channel_id=1, source_target_pairs={{0,16},{4,20},{8,24},{12,28},{16,0},{20,4},{24,8},{28,12},{1,17},{... | collective-permute-start | bytes 221192 | tf_op jit(solution)/shard_map/ppermute | solution.py:1229
  187.8 9.8 %collective-permute-start.46 = (bf16[2,24,1920]{2,1,0:T(8,128)(2,1)S(1)}, bf16[2,24,1920]{2,1,0:T(8,128)(2,1)S(1)}, u32[]{:S(2)}, u32[]{:S(2)}) collective-permute-start(bf16[2,24,1920]{2,1,0:T(8,128)(2,1)S(1)} %pad_maximum_fusion.8), channel_id=1, source_target_pairs={{0,1},{1,0},{2,3},{3,2},{4,5},{5,4},{6,7},{7,6},{8,9},{9,8},{10,11... | collective-permute-start | bytes 552968 | tf_op jit(solution)/shard_map/ppermute | solution.py:1234
  189.9 8.5 %collective-permute-start.47 = (bf16[2,24,1920]{2,1,0:T(8,128)(2,1)S(1)}, bf16[2,24,1920]{2,1,0:T(8,128)(2,1)S(1)}, u32[]{:S(2)}, u32[]{:S(2)}) collective-permute-start(bf16[2,24,1920]{2,1,0:T(8,128)(2,1)S(1)} %pad_maximum_fusion.9), channel_id=1, source_target_pairs={{0,2},{1,3},{2,0},{3,1},{4,6},{5,7},{6,4},{7,5},{8,10},{9,11},{10,... | collective-permute-start | bytes 552968 | tf_op jit(solution)/shard_map/ppermute | solution.py:1234
  190.6 4.9 %collective-permute-start.41 = (bf16[2,40,768]{2,1,0:T(8,128)(2,1)S(1)}, bf16[2,40,768]{2,1,0:T(8,128)(2,1)S(1)}, u32[]{:S(2)}, u32[]{:S(2)}) collective-permute-start(bf16[2,40,768]{2,1,0:T(8,128)(2,1)S(1)} %get-tuple-element.346), channel_id=1, source_target_pairs={{0,16},{4,20},{8,24},{12,28},{16,0},{20,4},{24,8},{28,12},{1,17},{... | collective-permute-start | bytes 368648 | tf_op jit(solution)/shard_map/ppermute | solution.py:1229
  191.9 4.9 %collective-permute-start.42 = (bf16[2,40,768]{2,1,0:T(8,128)(2,1)S(1)}, bf16[2,40,768]{2,1,0:T(8,128)(2,1)S(1)}, u32[]{:S(2)}, u32[]{:S(2)}) collective-permute-start(bf16[2,40,768]{2,1,0:T(8,128)(2,1)S(1)} %pad_maximum_fusion.11), channel_id=1, source_target_pairs={{0,8},{4,12},{8,0},{12,4},{16,24},{20,28},{24,16},{28,20},{1,9},{5... | collective-permute-start | bytes 368648 | tf_op jit(solution)/shard_map/ppermute | solution.py:1229
  195.6 4.5 %collective-permute-start.43 = (bf16[2,2,40,768]{3,2,1,0:T(8,128)(2,1)S(1)}, bf16[2,2,40,768]{3,2,1,0:T(8,128)(2,1)S(1)}, u32[]{:S(2)}, u32[]{:S(2)}) collective-permute-start(bf16[2,2,40,768]{3,2,1,0:T(8,128)(2,1)S(1)} %pad_maximum_fusion.6.mine_a), channel_id=1, source_target_pairs={{0,4},{4,0},{8,12},{12,8},{16,20},{20,16},{24,28},{28,24},{1,5},{5... | collective-permute-start | bytes 737288 | tf_op jit(solution)/shard_map/ppermute | solution.py:1229
  196.9 3.2 %collective-permute-start.44 = (bf16[2,2,32,768]{3,2,1,0:T(8,128)(2,1)S(1)}, bf16[2,2,32,768]{3,2,1,0:T(8,128)(2,1)S(1)}, u32[]{:S(2)}, u32[]{:S(2)}) collective-permute-start(bf16[2,2,32,768]{3,2,1,0:T(8,128)(2,1)S(1)} %pad_maximum_fusion.7.mine_b), channel_id=1, source_target_pairs={{0,4},{4,0},{8,12},{12,8},{16,20},{20,16},{24,28},{28,24},{1,5},{5... | collective-permute-start | bytes 589832 | tf_op jit(solution)/shard_map/ppermute | solution.py:1229
  197.0 3.1 %collective-permute-start.45 = (bf16[16,768]{1,0:T(8,128)(2,1)S(1)}, bf16[16,768]{1,0:T(8,128)(2,1)S(1)}, u32[]{:S(2)}, u32[]{:S(2)}) collective-permute-start(bf16[16,768]{1,0:T(8,128)(2,1)S(1)} %fusion.3.ends_ref), channel_id=1, source_target_pairs={{0,4},{4,0},{8,12},{12,8},{16,20},{20,16},{24,28},{28,24},{1,5},{5... | collective-permute-start | bytes 73736 | tf_op jit(solution)/shard_map/ppermute | solution.py:1229
  (26 other events, 231.8 us)
